TPU v7x, 32 devices: a whole 2x2x4 slice. The times are simulated.
32 devices in a mesh: dp: 4 (over x, core), seq: 8 (over z, y).
Axes of the slice: x: 2, y: 2, z: 4, core: 2. Of those that a mesh axis runs over, the one named last changes fastest.
Arguments:
- tokens: bfloat16 [1, 4, 1024, 2048], P(None, 'dp', 'seq'), may hold values from -6 to 6
- segment_ids: int32 [1, 4, 1024], P(None, 'dp', 'seq'), may hold values from 0 to 1, as said below
- out_grad: bfloat16 [1, 4, 1024, 2048], P(None, 'dp', 'seq'), may hold values from -6 to 6
- gain_attn: float32 [2048], replicated, may hold values from 0.5 to 1.5
- gain_mlp: float32 [2048], replicated, may hold values from 0.5 to 1.5
- w_query: bfloat16 [2048, 2048], P(None, 'dp'), may hold values from -0.125 to 0.125
- w_key: bfloat16 [2048, 256], replicated, may hold values from -0.125 to 0.125
- w_value: bfloat16 [2048, 256], replicated, may hold values from -0.125 to 0.125
- w_out: bfloat16 [2048, 2048], P('dp'), may hold values from -0.5 to 0.5
- w_gate: bfloat16 [2048, 16384], P(None, 'dp'), may hold values from -0.125 to 0.125
- w_up: bfloat16 [2048, 16384], P(None, 'dp'), may hold values from -0.125 to 0.125
- w_down: bfloat16 [16384, 2048], P('dp'), may hold values from -0.046875 to 0.046875
- query_adapt: bfloat16 [2048, 256], replicated, may hold values from -0.125 to 0.125
- query_expand: bfloat16 [256, 2048], P(None, 'dp'), may hold values from -0.375 to 0.375
- key_adapt: bfloat16 [2048, 256], replicated, may hold values from -0.125 to 0.125
- key_expand: bfloat16 [256, 256], replicated, may hold values from -0.375 to 0.375
- value_adapt: bfloat16 [2048, 256], replicated, may hold values from -0.125 to 0.125
- value_expand: bfloat16 [256, 256], replicated, may hold values from -0.375 to 0.375
- out_adapt: bfloat16 [2048, 256], P('dp'), may hold values from -0.5 to 0.5
- out_expand: bfloat16 [256, 2048], replicated, may hold values from -0.375 to 0.375
- gate_adapt: bfloat16 [2048, 256], replicated, may hold values from -0.125 to 0.125
- gate_expand: bfloat16 [256, 16384], P(None, 'dp'), may hold values from -0.375 to 0.375
- up_adapt: bfloat16 [2048, 256], replicated, may hold values from -0.125 to 0.125
- up_expand: bfloat16 [256, 16384], P(None, 'dp'), may hold values from -0.375 to 0.375
- down_adapt: bfloat16 [16384, 256], P('dp'), may hold values from -0.046875 to 0.046875
- down_expand: bfloat16 [256, 2048], replicated, may hold values from -0.375 to 0.375
Outputs:
- layer_out: bfloat16 [1, 4, 1024, 2048], P(None, 'dp', 'seq')
- tokens_grad: bfloat16 [1, 4, 1024, 2048], P(None, 'dp', 'seq')
- grad_gain_attn: float32 [2048], P(('dp', 'seq'))
- grad_gain_mlp: float32 [2048], P(('dp', 'seq'))
- grad_w_query: float32 [2048, 2048], P('seq', 'dp')
- grad_w_key: float32 [2048, 256], P(('dp', 'seq'))
- grad_w_value: float32 [2048, 256], P(('dp', 'seq'))
- grad_w_out: float32 [2048, 2048], P('dp', 'seq')
- grad_w_gate: float32 [2048, 16384], P('seq', 'dp')
- grad_w_up: float32 [2048, 16384], P('seq', 'dp')
- grad_w_down: float32 [16384, 2048], P('dp', 'seq')
- grad_query_adapt: float32 [2048, 256], P(('dp', 'seq'))
- grad_query_expand: float32 [256, 2048], P('seq', 'dp')
- grad_key_adapt: float32 [2048, 256], P(('dp', 'seq'))
- grad_key_expand: float32 [256, 256], P(('dp', 'seq'))
- grad_value_adapt: float32 [2048, 256], P(('dp', 'seq'))
- grad_value_expand: float32 [256, 256], P(('dp', 'seq'))
- grad_out_adapt: float32 [2048, 256], P('dp', 'seq')
- grad_out_expand: float32 [256, 2048], P(('dp', 'seq'))
- grad_gate_adapt: float32 [2048, 256], P(('dp', 'seq'))
- grad_gate_expand: float32 [256, 16384], P('seq', 'dp')
- grad_up_adapt: float32 [2048, 256], P(('dp', 'seq'))
- grad_up_expand: float32 [256, 16384], P('seq', 'dp')
- grad_down_adapt: float32 [16384, 256], P('dp', 'seq')
- grad_down_expand: float32 [256, 2048], P(('dp', 'seq'))
Inputs may be any that keep to these rules, and one draw needn't show every extreme that they name: `segment_ids`: every sequence holds two documents: document 0 ends within the first 128 tokens, at a place drawn from the seed, and document 1 runs from there to the sequence's end.
All inputs are finite; a program needn't handle non-finite values.
Results may differ from a plain program's by a relative error of at most 0.028.
Values may be sent and summed in bfloat16 or wider, within the bound.
A program may use at most 384 MiB of HBM per device.

v0:
```python
import jax
import jax.numpy as jnp
from jax import lax
from jax.sharding import PartitionSpec as P

HD = 256


EPSILON = 1e-06
ROTARY_BASE = 10000.0
MASKED = -1e30


def matmul(left, right):
    return jnp.dot(left, right, preferred_element_type=jnp.float32)


def contract(form, left, right):
    return jnp.einsum(form, left, right, preferred_element_type=jnp.float32)


def rotary(positions, size):
    half_size = size // 2
    frequency = ROTARY_BASE ** (-(jnp.arange(half_size, dtype=jnp.float32) * 2.0) / size)
    angles = positions.astype(jnp.float32)[:, None] * frequency[None, :]
    return (jnp.cos(angles), jnp.sin(angles))


def rotate(values, cosine_table, sine_table):
    half_size = values.shape[-1] // 2
    first_half = values[..., :half_size]
    second_half = values[..., half_size:]
    return jnp.concatenate(
        [
            first_half * cosine_table - second_half * sine_table,
            second_half * cosine_table + first_half * sine_table,
        ],
        axis=-1,
    )


def normalize(values, gain_vector):
    inverse_rms = lax.rsqrt(jnp.mean(values * values, axis=-1, keepdims=True) + EPSILON)
    unit_rows = values * inverse_rms
    return (unit_rows * gain_vector, unit_rows, inverse_rms)


def norm_backward(grad_normed, unit_rows, inverse_rms, gain_vector):
    gain_term = jnp.sum(grad_normed * unit_rows, axis=0)
    grad_unit = grad_normed * gain_vector
    inner = jnp.mean(grad_unit * unit_rows, axis=-1, keepdims=True)
    return (gain_term, inverse_rms * (grad_unit - unit_rows * inner))


def gelu_tanh(values):
    return jax.nn.gelu(values, approximate=True)


def reduce_shard(terms):
    return (
        lax.psum_scatter(
            terms[0].astype(jnp.bfloat16), "seq", scatter_dimension=0, tiled=True
        ).astype(jnp.float32),
        lax.psum_scatter(
            terms[1].astype(jnp.bfloat16), "seq", scatter_dimension=1, tiled=True
        ).astype(jnp.float32),
        lax.psum_scatter(
            terms[2].astype(jnp.bfloat16), "seq", scatter_dimension=0, tiled=True
        ).astype(jnp.float32),
        lax.psum_scatter(
            terms[3].astype(jnp.bfloat16), "seq", scatter_dimension=0, tiled=True
        ).astype(jnp.float32),
        lax.psum_scatter(
            terms[4].astype(jnp.bfloat16), "seq", scatter_dimension=1, tiled=True
        ).astype(jnp.float32),
        lax.psum_scatter(
            terms[5].astype(jnp.bfloat16), "seq", scatter_dimension=0, tiled=True
        ).astype(jnp.float32),
        lax.psum_scatter(
            terms[6].astype(jnp.bfloat16), "seq", scatter_dimension=1, tiled=True
        ).astype(jnp.float32),
        lax.psum_scatter(
            terms[7].astype(jnp.bfloat16), "seq", scatter_dimension=0, tiled=True
        ).astype(jnp.float32),
        lax.psum_scatter(
            terms[8].astype(jnp.bfloat16), "seq", scatter_dimension=0, tiled=True
        ).astype(jnp.float32),
        lax.psum_scatter(
            terms[9].astype(jnp.bfloat16), "seq", scatter_dimension=1, tiled=True
        ).astype(jnp.float32),
    )


def reduce_shared(terms):
    return (
        lax.psum_scatter(terms[0], ("dp", "seq"), scatter_dimension=0, tiled=True),
        lax.psum_scatter(terms[1], ("dp", "seq"), scatter_dimension=0, tiled=True),
        lax.psum_scatter(terms[2], ("dp", "seq"), scatter_dimension=0, tiled=True),
        lax.psum_scatter(terms[3], ("dp", "seq"), scatter_dimension=0, tiled=True),
        lax.psum_scatter(terms[4], ("dp", "seq"), scatter_dimension=0, tiled=True),
        lax.psum_scatter(terms[5], ("dp", "seq"), scatter_dimension=0, tiled=True),
        lax.psum_scatter(terms[6], ("dp", "seq"), scatter_dimension=0, tiled=True),
        lax.psum_scatter(terms[7], ("dp", "seq"), scatter_dimension=0, tiled=True),
        lax.psum_scatter(terms[8], ("dp", "seq"), scatter_dimension=0, tiled=True),
        lax.psum_scatter(terms[9], ("dp", "seq"), scatter_dimension=0, tiled=True),
        lax.psum_scatter(terms[10], ("dp", "seq"), scatter_dimension=0, tiled=True),
        lax.psum_scatter(terms[11], ("dp", "seq"), scatter_dimension=0, tiled=True),
        lax.psum_scatter(terms[12], ("dp", "seq"), scatter_dimension=0, tiled=True),
    )


def local(
    tokens,
    segment_ids,
    out_grad,
    gain_attn,
    gain_mlp,
    w_query,
    w_key,
    w_value,
    w_out,
    w_gate,
    w_up,
    w_down,
    query_adapt,
    query_expand,
    key_adapt,
    key_expand,
    value_adapt,
    value_expand,
    out_adapt,
    out_expand,
    gate_adapt,
    gate_expand,
    up_adapt,
    up_expand,
    down_adapt,
    down_expand,
):
    batches = tokens.shape[0]
    rows = tokens.shape[2]
    groups = lax.axis_size("dp")
    length = rows * lax.axis_size("seq")
    heads_dev = w_query.shape[1] // HD
    scale_qk = HD ** (-0.5)
    segments_all = lax.all_gather(segment_ids, ("dp", "seq"), axis=2, tiled=True).reshape(
        batches, groups, length
    )
    seq_start = lax.axis_index("seq") * rows
    positions = seq_start + jnp.arange(rows, dtype=jnp.int32)
    key_positions = jnp.arange(length, dtype=jnp.int32)
    cosine_table, sine_table = rotary(positions, HD)
    cosine_heads = cosine_table[:, None, :]
    sine_heads = sine_table[:, None, :]
    segments = segments_all[0]
    own_segments = lax.dynamic_slice_in_dim(segments, seq_start, rows, 1)
    causal = (key_positions[None, :] <= positions[:, None])[None, :, :]
    allowed = (causal & (own_segments[:, :, None] == segments[:, None, :]))[:, None, :, :]
    token_rows = tokens[0, 0].astype(jnp.float32)
    normed, unit_attn, rms_attn = normalize(token_rows, gain_attn)
    normed_attn = normed.astype(jnp.bfloat16)
    query_low = matmul(normed_attn, query_adapt).astype(jnp.bfloat16)
    key_low = matmul(normed_attn, key_adapt).astype(jnp.bfloat16)
    value_low = matmul(normed_attn, value_adapt).astype(jnp.bfloat16)
    key_pre = matmul(normed_attn, w_key) + matmul(key_low, key_expand)
    value_pre = matmul(normed_attn, w_value) + matmul(value_low, value_expand)
    key_rot = rotate(key_pre, cosine_table, sine_table).astype(jnp.bfloat16)
    value_rows = value_pre.astype(jnp.bfloat16)
    normed_all = lax.all_gather(normed_attn[None], "dp", axis=0, tiled=True)
    query_low_all = lax.all_gather(query_low[None], "dp", axis=0, tiled=True)
    key_group = lax.all_gather(key_rot[None], "dp", axis=0, tiled=True)
    value_group = lax.all_gather(value_rows[None], "dp", axis=0, tiled=True)
    keys_all = lax.all_gather(key_group, "seq", axis=1, tiled=True)
    values_all = lax.all_gather(value_group, "seq", axis=1, tiled=True)
    queries = matmul(normed_all, w_query) + matmul(query_low_all, query_expand)
    query_rot = rotate(
        queries.reshape(groups, rows, heads_dev, HD), cosine_heads, sine_heads
    ).astype(jnp.bfloat16)
    scores = jnp.where(allowed, contract("sthd,sjd->shtj", query_rot, keys_all) * scale_qk, MASKED)
    row_top = jnp.max(scores, axis=-1, keepdims=True)
    log_total = row_top + jnp.log(jnp.sum(jnp.exp(scores - row_top), axis=-1, keepdims=True))
    forward_probs = jnp.exp(scores - log_total)
    prob_low = forward_probs.astype(jnp.bfloat16)
    heads_out = (
        contract("shtj,sjd->sthd", prob_low, values_all)
        .reshape(groups, rows, heads_dev * HD)
        .astype(jnp.bfloat16)
    )
    out_sum = lax.psum_scatter(
        matmul(heads_out, w_out).astype(jnp.bfloat16), "dp", scatter_dimension=0, tiled=True
    ).astype(jnp.float32)
    out_low_sum = lax.psum_scatter(
        matmul(heads_out, out_adapt).astype(jnp.bfloat16), "dp", scatter_dimension=0, tiled=True
    ).astype(jnp.float32)
    out_low = out_low_sum[0].astype(jnp.bfloat16)
    middle = token_rows + (out_sum[0] + matmul(out_low, out_expand))
    normed, unit_mlp, rms_mlp = normalize(middle, gain_mlp)
    normed_mlp = normed.astype(jnp.bfloat16)
    gate_low = matmul(normed_mlp, gate_adapt).astype(jnp.bfloat16)
    up_low = matmul(normed_mlp, up_adapt).astype(jnp.bfloat16)
    normed_mlp_all = lax.all_gather(normed_mlp[None], "dp", axis=0, tiled=True)
    gate_low_all = lax.all_gather(gate_low[None], "dp", axis=0, tiled=True)
    up_low_all = lax.all_gather(up_low[None], "dp", axis=0, tiled=True)
    gating = matmul(normed_mlp_all, w_gate) + matmul(gate_low_all, gate_expand)
    lifting = matmul(normed_mlp_all, w_up) + matmul(up_low_all, up_expand)
    activated, gelu_back = jax.vjp(gelu_tanh, gating)
    mixture = (activated * lifting).astype(jnp.bfloat16)
    down_sum = lax.psum_scatter(
        matmul(mixture, w_down).astype(jnp.bfloat16), "dp", scatter_dimension=0, tiled=True
    ).astype(jnp.float32)
    down_low_sum = lax.psum_scatter(
        matmul(mixture, down_adapt).astype(jnp.bfloat16), "dp", scatter_dimension=0, tiled=True
    ).astype(jnp.float32)
    down_low = down_low_sum[0].astype(jnp.bfloat16)
    result_rows = (middle + (down_sum[0] + matmul(down_low, down_expand))).astype(jnp.bfloat16)
    grad_middle = out_grad[0, 0].astype(jnp.float32)
    grad_branch = grad_middle.astype(jnp.bfloat16)
    grad_down_low = contract("td,rd->tr", grad_branch, down_expand).astype(jnp.bfloat16)
    grad_branch_all = lax.all_gather(grad_branch[None], "dp", axis=0, tiled=True)
    grad_down_low_all = lax.all_gather(grad_down_low[None], "dp", axis=0, tiled=True)
    grad_mixture = contract("std,fd->stf", grad_branch_all, w_down) + contract(
        "str,fr->stf", grad_down_low_all, down_adapt
    )
    grad_mixture_wide = grad_mixture.astype(jnp.bfloat16).astype(jnp.float32)
    grad_gate = gelu_back(grad_mixture_wide * lifting)[0].astype(jnp.bfloat16)
    grad_up = (grad_mixture_wide * activated).astype(jnp.bfloat16)
    grad_normed_part = contract("stf,df->std", grad_gate, w_gate) + contract(
        "stf,df->std", grad_up, w_up
    )
    grad_gate_low_part = contract("stf,rf->str", grad_gate, gate_expand)
    grad_up_low_part = contract("stf,rf->str", grad_up, up_expand)
    grad_normed_sum = lax.psum_scatter(
        grad_normed_part.astype(jnp.bfloat16), "dp", scatter_dimension=0, tiled=True
    ).astype(jnp.float32)
    grad_gate_low_sum = lax.psum_scatter(
        grad_gate_low_part.astype(jnp.bfloat16), "dp", scatter_dimension=0, tiled=True
    ).astype(jnp.float32)
    grad_up_low_sum = lax.psum_scatter(
        grad_up_low_part.astype(jnp.bfloat16), "dp", scatter_dimension=0, tiled=True
    ).astype(jnp.float32)
    grad_gate_low = grad_gate_low_sum[0].astype(jnp.bfloat16)
    grad_up_low = grad_up_low_sum[0].astype(jnp.bfloat16)
    grad_normed_mlp = (
        grad_normed_sum[0]
        + contract("tr,dr->td", grad_gate_low, gate_adapt)
        + contract("tr,dr->td", grad_up_low, up_adapt)
    )
    gain_mlp_term, grad_from_mlp = norm_backward(grad_normed_mlp, unit_mlp, rms_mlp, gain_mlp)
    grad_middle = grad_middle + grad_from_mlp
    grad_branch_attn = grad_middle.astype(jnp.bfloat16)
    grad_out_low = contract("td,rd->tr", grad_branch_attn, out_expand).astype(jnp.bfloat16)
    grad_attn_all = lax.all_gather(grad_branch_attn[None], "dp", axis=0, tiled=True)
    grad_out_low_all = lax.all_gather(grad_out_low[None], "dp", axis=0, tiled=True)
    grad_heads = (
        contract("std,nd->stn", grad_attn_all, w_out)
        + contract("str,nr->stn", grad_out_low_all, out_adapt)
    ).astype(jnp.bfloat16)
    grad_heads_split = grad_heads.reshape(groups, rows, heads_dev, HD)
    scores_again = jnp.where(
        allowed, contract("sthd,sjd->shtj", query_rot, keys_all) * scale_qk, MASKED
    )
    probabilities = jnp.exp(scores_again - log_total)
    grad_values_part = contract(
        "shtj,sthd->sjd", probabilities.astype(jnp.bfloat16), grad_heads_split
    )
    grad_probs = contract("sthd,sjd->shtj", grad_heads_split, values_all)
    delta_rows = jnp.sum(probabilities * grad_probs, axis=-1, keepdims=True)
    grad_scores = (probabilities * (grad_probs - delta_rows)).astype(jnp.bfloat16)
    grad_query_rot = contract("shtj,sjd->sthd", grad_scores, keys_all) * scale_qk
    grad_keys_part = contract("shtj,sthd->sjd", grad_scores, query_rot) * scale_qk
    grad_keys_seq = lax.psum_scatter(
        grad_keys_part.astype(jnp.bfloat16), "seq", scatter_dimension=1, tiled=True
    )
    grad_values_seq = lax.psum_scatter(
        grad_values_part.astype(jnp.bfloat16), "seq", scatter_dimension=1, tiled=True
    )
    grad_query = (
        rotate(grad_query_rot, cosine_heads, -sine_heads)
        .reshape(groups, rows, heads_dev * HD)
        .astype(jnp.bfloat16)
    )
    grad_normed_part = contract("stn,dn->std", grad_query, w_query)
    grad_query_low_part = contract("stn,rn->str", grad_query, query_expand)
    grad_normed_sum = lax.psum_scatter(
        grad_normed_part.astype(jnp.bfloat16), "dp", scatter_dimension=0, tiled=True
    ).astype(jnp.float32)
    grad_query_low_sum = lax.psum_scatter(
        grad_query_low_part.astype(jnp.bfloat16), "dp", scatter_dimension=0, tiled=True
    ).astype(jnp.float32)
    grad_key_sum = lax.psum_scatter(grad_keys_seq, "dp", scatter_dimension=0, tiled=True).astype(
        jnp.float32
    )
    grad_value_sum = lax.psum_scatter(
        grad_values_seq, "dp", scatter_dimension=0, tiled=True
    ).astype(jnp.float32)
    grad_key = rotate(grad_key_sum[0], cosine_table, -sine_table).astype(jnp.bfloat16)
    grad_value = grad_value_sum[0].astype(jnp.bfloat16)
    grad_query_low = grad_query_low_sum[0].astype(jnp.bfloat16)
    grad_key_low = contract("te,re->tr", grad_key, key_expand).astype(jnp.bfloat16)
    grad_value_low = contract("te,re->tr", grad_value, value_expand).astype(jnp.bfloat16)
    grad_normed_attn = (
        grad_normed_sum[0]
        + contract("te,de->td", grad_key, w_key)
        + contract("te,de->td", grad_value, w_value)
        + contract("tr,dr->td", grad_query_low, query_adapt)
        + contract("tr,dr->td", grad_key_low, key_adapt)
        + contract("tr,dr->td", grad_value_low, value_adapt)
    )
    gain_attn_term, grad_from_attn = norm_backward(grad_normed_attn, unit_attn, rms_attn, gain_attn)
    grad_rows = (grad_middle + grad_from_attn).astype(jnp.bfloat16)
    shard_terms = (
        contract("std,stn->dn", normed_all, grad_query),
        contract("stn,std->nd", heads_out, grad_attn_all),
        contract("std,stf->df", normed_mlp_all, grad_gate),
        contract("std,stf->df", normed_mlp_all, grad_up),
        contract("stf,std->fd", mixture, grad_branch_all),
        contract("str,stn->rn", query_low_all, grad_query),
        contract("stn,str->nr", heads_out, grad_out_low_all),
        contract("str,stf->rf", gate_low_all, grad_gate),
        contract("str,stf->rf", up_low_all, grad_up),
        contract("stf,str->fr", mixture, grad_down_low_all),
    )
    shared_terms = (
        gain_attn_term,
        gain_mlp_term,
        contract("td,te->de", normed_attn, grad_key),
        contract("td,te->de", normed_attn, grad_value),
        contract("td,tr->dr", normed_attn, grad_query_low),
        contract("td,tr->dr", normed_attn, grad_key_low),
        contract("tr,te->re", key_low, grad_key),
        contract("td,tr->dr", normed_attn, grad_value_low),
        contract("tr,te->re", value_low, grad_value),
        contract("tr,td->rd", out_low, grad_branch_attn),
        contract("td,tr->dr", normed_mlp, grad_gate_low),
        contract("td,tr->dr", normed_mlp, grad_up_low),
        contract("tr,td->rd", down_low, grad_branch),
    )
    result_rows, grad_rows, shard_terms, shared_terms = (
        result_rows,
        grad_rows,
        shard_terms,
        shared_terms,
    )
    results = [result_rows]
    input_grads = [grad_rows]
    shard_done = reduce_shard(shard_terms)
    shared_done = reduce_shared(shared_terms)
    layer_out = jnp.stack(results)[:, None]
    tokens_grad = jnp.stack(input_grads)[:, None]
    return (
        layer_out,
        tokens_grad,
        shared_done[0],
        shared_done[1],
        shard_done[0],
        shared_done[2],
        shared_done[3],
        shard_done[1],
        shard_done[2],
        shard_done[3],
        shard_done[4],
        shared_done[4],
        shard_done[5],
        shared_done[5],
        shared_done[6],
        shared_done[7],
        shared_done[8],
        shard_done[6],
        shared_done[9],
        shared_done[10],
        shard_done[7],
        shared_done[11],
        shard_done[8],
        shard_done[9],
        shared_done[12],
    )


def solution(mesh):
    in_specs = (
        P(None, "dp", "seq", None),
        P(None, "dp", "seq"),
        P(None, "dp", "seq", None),
        P(),
        P(),
        P(None, "dp"),
        P(),
        P(),
        P("dp", None),
        P(None, "dp"),
        P(None, "dp"),
        P("dp", None),
        P(),
        P(None, "dp"),
        P(),
        P(),
        P(),
        P(),
        P("dp", None),
        P(),
        P(),
        P(None, "dp"),
        P(),
        P(None, "dp"),
        P("dp", None),
        P(),
    )
    out_specs = (
        P(None, "dp", "seq", None),
        P(None, "dp", "seq", None),
        P(("dp", "seq")),
        P(("dp", "seq")),
        P("seq", "dp"),
        P(("dp", "seq"), None),
        P(("dp", "seq"), None),
        P("dp", "seq"),
        P("seq", "dp"),
        P("seq", "dp"),
        P("dp", "seq"),
        P(("dp", "seq"), None),
        P("seq", "dp"),
        P(("dp", "seq"), None),
        P(("dp", "seq"), None),
        P(("dp", "seq"), None),
        P(("dp", "seq"), None),
        P("dp", "seq"),
        P(("dp", "seq"), None),
        P(("dp", "seq"), None),
        P("seq", "dp"),
        P(("dp", "seq"), None),
        P("seq", "dp"),
        P("dp", "seq"),
        P(("dp", "seq"), None),
    )
    return jax.shard_map(local, mesh=mesh, in_specs=in_specs, out_specs=out_specs, check_vma=False)
```

profile of v0, /device:TPU:0, one launch (start us, length us, event | category | flops | bytes accessed | tf_op | source)
XLA Modules:
  0.0 3579.5 jit_solution(2377326924781920073)
XLA Ops:
  15.0 7.6 all_gather.45
  26.1 7.7 all-gather
  34.7 68.8 %all_gather.44 = s32[1,1,4096]{2,1,0:T(1,128)S(1)} all-gather(s32[1,1,128]{2,1,0:T(1,128)S(1)} %copy-done.66), channel_id=1, replica_groups=mesh['dp'=4,'seq'=8] {'dp','seq'}, dimensions={2}, use_global_device_ids=true | all-gather | bytes 16896 | tf_op jit(solution)/shard_map/all_gather | solution.py:146
  106.4 5.8 all-gather.1
  128.6 12.8 all-gather.16.cloned.1.call-done
  147.4 4.4 convolution_convert_fusion.1
  154.2 5.8 all-gather.6
  159.9 5.8 reduce-scatter.37.cloned.1.call-done
  165.7 34.6 reduce-scatter.35.cloned.1.call-done
  204.3 20.0 all-gather.24.cloned.1.call-done
  224.3 12.4 fusion
  236.8 5.2 add_convert_fusion
  242.3 7.4 all-gather.4
  250.1 5.9 all-gather.3
  256.0 12.4 fusion.6
  268.4 14.5 fusion.10
  285.1 13.1 fusion.19
  298.2 15.6 fusion.4
  315.9 15.3 add_convert_fusion.1
  331.3 5.0 fusion.84
  336.4 33.8 reduce-scatter.43.cloned.1.call-done
  372.7 20.4 reduce-scatter.47.cloned.1.call-done
  399.0 6.4 all-gather.8
  405.4 14.4 all-gather.26.cloned.1.call-done
  431.3 4.6 bitcast_convert_fusion.5
  436.0 63.6 %reduce-scatter.51.cloned.1.call-done = bf16[4,128,256]{2,1,0:T(8,128)(2,1)} async-done(((bf16[4,1024,256]{2,1,0:T(8,128)(2,1)}), bf16[4,128,256]{2,1,0:T(8,128)(2,1)}) %reduce-scatter.51.cloned.1.call-update) | async-done | bytes 262160 | tf_op jit(solution)/shard_map/reduce_scatter | solution.py:271
  499.7 4.8 fusion.87
  507.8 63.2 %reduce-scatter.55.cloned.1.call-done = bf16[4,128,256]{2,1,0:T(8,128)(2,1)} async-done(((bf16[4,1024,256]{2,1,0:T(8,128)(2,1)}), bf16[4,128,256]{2,1,0:T(8,128)(2,1)}) %reduce-scatter.55.cloned.1.call-update) | async-done | bytes 262160 | tf_op jit(solution)/shard_map/reduce_scatter | solution.py:274
  571.1 21.5 reduce-scatter.53.cloned.1.call-done
  596.1 4.8 fusion.20
  601.0 4.9 fusion.21
  606.2 4.8 fusion.22
  611.1 14.6 fusion.30
  627.0 4.2 bitcast_convert_fusion.3
  632.4 4.3 convolution_convert_fusion
  636.8 4.3 bitcast_convert_fusion.4
  641.5 15.0 bitcast_convert_fusion.2
  656.6 14.9 bitcast_convert_fusion.1
  671.8 15.0 bitcast_convert_fusion
  710.5 22.1 reduce-scatter.93.cloned.1.call-done
  734.4 69.0 %reduce-scatter.97.cloned.1.call-done = bf16[32,4096]{1,0:T(8,128)(2,1)} async-done(((bf16[256,4096]{1,0:T(8,128)(2,1)}), bf16[32,4096]{1,0:T(8,128)(2,1)}) %reduce-scatter.97.cloned.1.call-update) | async-done | bytes 262160 | tf_op jit(solution)/shard_map/reduce_scatter | solution.py:85
  805.1 68.5 %reduce-scatter.99.cloned.1.call-done = bf16[4096,32]{0,1:T(8,128)(2,1)} async-done(((bf16[4096,256]{0,1:T(8,128)(2,1)}), bf16[4096,32]{0,1:T(8,128)(2,1)}) %reduce-scatter.99.cloned.1.call-update) | async-done | bytes 262160 | tf_op jit(solution)/shard_map/reduce_scatter | solution.py:88
  875.4 32.0 reduce-scatter.39.cloned.1.call-done
  909.9 62.1 %reduce-scatter.87.cloned.1.call-done = bf16[512,32]{0,1:T(8,128)(2,1)} async-done(((bf16[512,256]{0,1:T(8,128)(2,1)}), bf16[512,32]{0,1:T(8,128)(2,1)}) %reduce-scatter.87.cloned.1.call-update) | async-done | bytes 32784 | tf_op jit(solution)/shard_map/reduce_scatter | solution.py:79
  973.5 69.7 %reduce-scatter.67.cloned.1.call-done = bf16[512,256]{1,0:T(8,128)(2,1)} async-done(((bf16[512,2048]{1,0:T(8,128)(2,1)}), bf16[512,256]{1,0:T(8,128)(2,1)}) %reduce-scatter.67.cloned.1.call-update) | async-done | bytes 262160 | tf_op jit(solution)/shard_map/reduce_scatter | solution.py:64
  1044.9 62.2 %reduce-scatter.77.cloned.1.call-done = bf16[32,512]{1,0:T(8,128)(2,1)} async-done(((bf16[256,512]{1,0:T(8,128)(2,1)}), bf16[32,512]{1,0:T(8,128)(2,1)}) %reduce-scatter.77.cloned.1.call-update) | async-done | bytes 32784 | tf_op jit(solution)/shard_map/reduce_scatter | solution.py:76
  1108.5 31.6 reduce-scatter.49.cloned.1.call-done
  1147.6 40.4 %all-reduce.2 = (f32[2048]{0:T(1024)S(1)}, f32[2048]{0:T(1024)S(1)}) all-reduce(f32[2048]{0:T(1024)S(1)} %get-tuple-element.27, f32[2048]{0:T(1024)S(1)} %copy-done.60), channel_id=24, replica_groups=mesh['dp'=4,'seq'=8] {'dp','seq'}, use_global_device_ids=true, to_apply=%region_21.22.clone | all-reduce | flops 4096 | bytes 32768
  1189.2 23.0 reduce-scatter.61.cloned.1.call-done
  1216.9 281.1 %reduce-scatter.69.cloned.1.call-done = bf16[256,4096]{1,0:T(8,128)(2,1)} async-done(((bf16[2048,4096]{1,0:T(8,128)(2,1)}), bf16[256,4096]{1,0:T(8,128)(2,1)}) %reduce-scatter.69.cloned.1.call-update) | async-done | bytes 2097168 | tf_op jit(solution)/shard_map/reduce_scatter | solution.py:67
  1502.1 281.3 %reduce-scatter.71.cloned.1.call-done = bf16[256,4096]{1,0:T(8,128)(2,1)} async-done(((bf16[2048,4096]{1,0:T(8,128)(2,1)}), bf16[256,4096]{1,0:T(8,128)(2,1)}) %reduce-scatter.71.cloned.1.call-update) | async-done | bytes 2097168 | tf_op jit(solution)/shard_map/reduce_scatter | solution.py:70
  1783.5 4.2 convert_element_type.333
  1787.7 281.7 %reduce-scatter.73.cloned.1.call-done = bf16[4096,256]{1,0:T(8,128)(2,1)} async-done(((bf16[4096,2048]{1,0:T(8,128)(2,1)}), bf16[4096,256]{1,0:T(8,128)(2,1)}) %reduce-scatter.73.cloned.1.call-update) | async-done | bytes 2097168 | tf_op jit(solution)/shard_map/reduce_scatter | solution.py:73
  2073.3 135.2 %reduce-scatter.91.cloned.1.call-done = f32[64,256]{1,0:T(8,128)} async-done(((f32[2048,256]{1,0:T(8,128)}), f32[64,256]{1,0:T(8,128)}) %reduce-scatter.91.cloned.1.call-update) | async-done | bytes 65552 | tf_op jit(solution)/shard_map/reduce_scatter | solution.py:106
  2208.5 137.1 %reduce-scatter.95.cloned.1.call-done = f32[64,256]{1,0:T(8,128)} async-done(((f32[2048,256]{1,0:T(8,128)}), f32[64,256]{1,0:T(8,128)}) %reduce-scatter.95.cloned.1.call-update) | async-done | bytes 65552 | tf_op jit(solution)/shard_map/reduce_scatter | solution.py:107
  2345.7 137.7 %reduce-scatter.101.cloned.1.call-done = f32[8,2048]{1,0:T(8,128)} async-done(((f32[256,2048]{1,0:T(8,128)}), f32[8,2048]{1,0:T(8,128)}) %reduce-scatter.101.cloned.1.call-update) | async-done | bytes 65552 | tf_op jit(solution)/shard_map/reduce_scatter | solution.py:108
  2483.4 137.1 %reduce-scatter.89.cloned.1.call-done = f32[8,2048]{1,0:T(8,128)} async-done(((f32[256,2048]{1,0:T(8,128)}), f32[8,2048]{1,0:T(8,128)}) %reduce-scatter.89.cloned.1.call-update) | async-done | bytes 65552 | tf_op jit(solution)/shard_map/reduce_scatter | solution.py:105
  2620.5 133.2 %reduce-scatter.81.cloned.1.call-done = f32[8,256]{1,0:T(8,128)} async-done(((f32[256,256]{1,0:T(8,128)}), f32[8,256]{1,0:T(8,128)}) %reduce-scatter.81.cloned.1.call-update) | async-done | bytes 8208 | tf_op jit(solution)/shard_map/reduce_scatter | solution.py:102
  2753.7 133.1 %reduce-scatter.85.cloned.1.call-done = f32[8,256]{1,0:T(8,128)} async-done(((f32[256,256]{1,0:T(8,128)}), f32[8,256]{1,0:T(8,128)}) %reduce-scatter.85.cloned.1.call-update) | async-done | bytes 8208 | tf_op jit(solution)/shard_map/reduce_scatter | solution.py:104
  2886.8 137.1 %reduce-scatter.63.cloned.1.call-done = f32[64,256]{1,0:T(8,128)} async-done(((f32[2048,256]{1,0:T(8,128)}), f32[64,256]{1,0:T(8,128)}) %reduce-scatter.63.cloned.1.call-update) | async-done | bytes 65552 | tf_op jit(solution)/shard_map/reduce_scatter | solution.py:98
  3023.9 137.0 %reduce-scatter.65.cloned.1.call-done = f32[64,256]{1,0:T(8,128)} async-done(((f32[2048,256]{1,0:T(8,128)}), f32[64,256]{1,0:T(8,128)}) %reduce-scatter.65.cloned.1.call-update) | async-done | bytes 65552 | tf_op jit(solution)/shard_map/reduce_scatter | solution.py:99
  3160.9 136.8 %reduce-scatter.79.cloned.1.call-done = f32[64,256]{1,0:T(8,128)} async-done(((f32[2048,256]{1,0:T(8,128)}), f32[64,256]{1,0:T(8,128)}) %reduce-scatter.79.cloned.1.call-update) | async-done | bytes 65552 | tf_op jit(solution)/shard_map/reduce_scatter | solution.py:101
  3297.7 137.4 %reduce-scatter.83.cloned.1.call-done = f32[64,256]{1,0:T(8,128)} async-done(((f32[2048,256]{1,0:T(8,128)}), f32[64,256]{1,0:T(8,128)}) %reduce-scatter.83.cloned.1.call-update) | async-done | bytes 65552 | tf_op jit(solution)/shard_map/reduce_scatter | solution.py:103
  3435.1 137.3 %reduce-scatter.75.cloned.1.call-done = f32[64,256]{1,0:T(8,128)} async-done(((f32[2048,256]{1,0:T(8,128)}), f32[64,256]{1,0:T(8,128)}) %reduce-scatter.75.cloned.1.call-update) | async-done | bytes 65552 | tf_op jit(solution)/shard_map/reduce_scatter | solution.py:100
  (314 shorter events, 135.6 us)
Async XLA Ops:
  7.2 277.0 %copy-start = (bf16[256,4096]{1,0:T(8,128)(2,1)S(1)}, bf16[256,4096]{1,0:T(8,128)(2,1)}, u32[]{:S(2)}) copy-start(bf16[256,4096]{1,0:T(8,128)(2,1)} %param.47) | copy-start | bytes 6291460
  7.2 15.5 copy-start.2
  7.2 15.5 copy-start.39
  7.2 105.9 %all-gather.20.cloned.1.call-start = ((), (), s32[]{:S(2)}) async-start(), calls=%async_computation.36 | async-start | bytes 2621440 | tf_op jit(solution)/shard_map/all_gather | solution.py:169
  8.7 96.1 %copy-start.58 = (f32[128]{0:T(128)}, f32[128]{0:T(128)S(1)}, u32[]{:S(2)}) copy-start(f32[128]{0:T(128)S(1)} %add_rsqrt_fusion.1) | copy-start | bytes 1540
  10.7 112.4 %all-gather.18.cloned.1.call-start = ((), (), s32[]{:S(2)}) async-start(), calls=%async_computation.35 | async-start | bytes 2359296 | tf_op jit(solution)/shard_map/all_gather | solution.py:173
  10.8 15.1 copy-start.63
  10.8 15.1 copy-start.65
  12.7 22.0 copy-start.47
  12.7 22.1 copy-start.66
  22.7 118.7 %all-gather.16.cloned.1.call-start = ((), (), s32[]{:S(2)}) async-start(), calls=%async_computation.34 | async-start | bytes 2359296 | tf_op jit(solution)/shard_map/all_gather | solution.py:174
  24.3 87.9 %copy-start.52 = (bf16[128,256]{1,0:T(8,128)(2,1)}, bf16[128,256]{1,0:T(8,128)(2,1)S(1)}, u32[]{:S(2)}) copy-start(bf16[128,256]{1,0:T(8,128)(2,1)S(1)} %convolution_convert_fusion.10) | copy-start | bytes 196612
  34.7 131.0 %reduce-scatter.37.cloned.1.call-start = ((), (), s32[]{:S(2)}) async-start(), calls=%async_computation.38 | async-start | bytes 327680 | tf_op jit(solution)/shard_map/reduce_scatter | solution.py:192
  113.1 28.3 copy-start.12
  147.3 53.0 %reduce-scatter.35.cloned.1.call-start = ((), (), s32[]{:S(2)}) async-start(), calls=%async_computation.37 | async-start | bytes 2621440 | tf_op jit(solution)/shard_map/reduce_scatter | solution.py:189
  151.8 51.4 %copy-start.57 = (f32[2048]{0:T(1024)S(1)}, f32[2048]{0:T(1024)}, u32[]{:S(2)}) copy-start(f32[2048]{0:T(1024)} %param.30) | copy-start | bytes 24580
  151.8 72.6 %all-gather.24.cloned.1.call-start = ((), (), s32[]{:S(2)}) async-start(), calls=%async_computation.72 | async-start | bytes 2621440 | tf_op jit(solution)/shard_map/all_gather | solution.py:219
  152.4 103.6 %all-gather.22.cloned.1.call-start = ((), (), s32[]{:S(2)}) async-start(), calls=%async_computation.71 | async-start | bytes 2621440 | tf_op jit(solution)/shard_map/all_gather | solution.py:201
  159.9 76.8 %copy-start.29 = (bf16[512,256]{1,0:T(8,128)(2,1)}, bf16[512,256]{1,0:T(8,128)(2,1)S(1)}, u32[]{:S(2)}) copy-start(bf16[512,256]{1,0:T(8,128)(2,1)S(1)} %all-gather.6) | copy-start | bytes 786436
  204.1 132.3 %reduce-scatter.45.cloned.1.call-start = ((), (), s32[]{:S(2)}) async-start(), calls=%async_computation.42 | async-start | bytes 327680 | tf_op jit(solution)/shard_map/reduce_scatter | solution.py:235
  256.0 28.2 copy-start.32
  298.2 15.6 copy-start.20
  315.8 54.4 %reduce-scatter.43.cloned.1.call-start = ((), (), s32[]{:S(2)}) async-start(), calls=%async_computation.41 | async-start | bytes 2621440 | tf_op jit(solution)/shard_map/reduce_scatter | solution.py:232
  331.2 39.0 %copy-start.22 = (bf16[2048,256]{1,0:T(8,128)(2,1)S(1)}, bf16[2048,256]{1,0:T(8,128)(2,1)}, u32[]{:S(2)}) copy-start(bf16[2048,256]{1,0:T(8,128)(2,1)} %param.46) | copy-start | bytes 3145732
  331.2 61.9 %copy-start.5 = (f32[128,2048]{1,0:T(8,128)S(1)}, f32[128,2048]{1,0:T(8,128)}, u32[]{:S(2)}) copy-start(f32[128,2048]{1,0:T(8,128)} %copy-done.4) | copy-start | bytes 3145732
  331.2 61.9 %reduce-scatter.47.cloned.1.call-start = ((), (), s32[]{:S(2)}) async-start(), calls=%async_computation.43 | async-start | bytes 327680 | tf_op jit(solution)/shard_map/reduce_scatter | solution.py:238
  336.3 83.5 %all-gather.26.cloned.1.call-start = ((), (), s32[]{:S(2)}) async-start(), calls=%async_computation.73 | async-start | bytes 2621440 | tf_op jit(solution)/shard_map/all_gather | solution.py:252
  395.9 27.6 copy-start.11
  397.1 102.6 %reduce-scatter.51.cloned.1.call-start = ((), (), s32[]{:S(2)}) async-start(), calls=%async_computation.45 | async-start | bytes 2359296 | tf_op jit(solution)/shard_map/reduce_scatter | solution.py:271
  431.3 139.7 %reduce-scatter.55.cloned.1.call-start = ((), (), s32[]{:S(2)}) async-start(), calls=%async_computation.47 | async-start | bytes 2359296 | tf_op jit(solution)/shard_map/reduce_scatter | solution.py:274
  436.0 156.6 %reduce-scatter.53.cloned.1.call-start = ((), (), s32[]{:S(2)}) async-start(), calls=%async_computation.46 | async-start | bytes 327680 | tf_op jit(solution)/shard_map/reduce_scatter | solution.py:290
  499.7 192.0 %reduce-scatter.41.cloned.1.call-start = ((), (), s32[]{:S(2)}) async-start(), calls=%async_computation.40 | async-start | bytes 327680 | tf_op jit(solution)/shard_map/reduce_scatter | solution.py:211
  504.5 88.9 %copy-start.64 = (f32[128]{0:T(128)S(1)}, f32[128]{0:T(128)}, u32[]{:S(2)}) copy-start(f32[128]{0:T(128)} %copy-done.63) | copy-start | bytes 1540
  504.6 90.4 %copy-start.35 = (bf16[256,512]{1,0:T(8,128)(2,1)S(1)}, bf16[256,512]{1,0:T(8,128)(2,1)}, u32[]{:S(2)}) copy-start(bf16[256,512]{1,0:T(8,128)(2,1)} %param.39) | copy-start | bytes 786436
  504.6 192.8 %reduce-scatter.57.cloned.1.call-start = ((), (), s32[]{:S(2)}) async-start(), calls=%async_computation.48 | async-start | bytes 327680 | tf_op jit(solution)/shard_map/reduce_scatter | solution.py:293
  507.7 88.3 %copy-start.33 = (bf16[512,256]{1,0:T(8,128)(2,1)S(1)}, bf16[512,256]{1,0:T(8,128)(2,1)}, u32[]{:S(2)}) copy-start(bf16[512,256]{1,0:T(8,128)(2,1)} %copy-done.32) | copy-start | bytes 786436
  571.0 136.7 %reduce-scatter.59.cloned.1.call-start = ((), (), s32[]{:S(2)}) async-start(), calls=%async_computation.49 | async-start | bytes 327680 | tf_op jit(solution)/shard_map/reduce_scatter | solution.py:287
  596.0 136.6 %reduce-scatter.93.cloned.1.call-start = ((), (), s32[]{:S(2)}) async-start(), calls=%async_computation.66 | async-start | bytes 2359296 | tf_op jit(solution)/shard_map/reduce_scatter | solution.py:82
  600.9 202.4 %reduce-scatter.97.cloned.1.call-start = ((), (), s32[]{:S(2)}) async-start(), calls=%async_computation.68 | async-start | bytes 2359296 | tf_op jit(solution)/shard_map/reduce_scatter | solution.py:85
  605.9 267.8 %reduce-scatter.99.cloned.1.call-start = ((), (), s32[]{:S(2)}) async-start(), calls=%async_computation.69 | async-start | bytes 2359296 | tf_op jit(solution)/shard_map/reduce_scatter | solution.py:88
  611.0 296.4 %reduce-scatter.39.cloned.1.call-start = ((), (), s32[]{:S(2)}) async-start(), calls=%async_computation.39 | async-start | bytes 2621440 | tf_op jit(solution)/shard_map/reduce_scatter | solution.py:208
  625.7 346.3 %reduce-scatter.87.cloned.1.call-start = ((), (), s32[]{:S(2)}) async-start(), calls=%async_computation.63 | async-start | bytes 294912 | tf_op jit(solution)/shard_map/reduce_scatter | solution.py:79
  626.9 416.2 %reduce-scatter.67.cloned.1.call-start = ((), (), s32[]{:S(2)}) async-start(), calls=%async_computation.53 | async-start | bytes 2359296 | tf_op jit(solution)/shard_map/reduce_scatter | solution.py:64
  631.2 475.9 %reduce-scatter.77.cloned.1.call-start = ((), (), s32[]{:S(2)}) async-start(), calls=%async_computation.58 | async-start | bytes 294912 | tf_op jit(solution)/shard_map/reduce_scatter | solution.py:76
  632.4 507.8 %reduce-scatter.49.cloned.1.call-start = ((), (), s32[]{:S(2)}) async-start(), calls=%async_computation.44 | async-start | bytes 2621440 | tf_op jit(solution)/shard_map/reduce_scatter | solution.py:284
  636.8 575.5 %reduce-scatter.61.cloned.1.call-start = ((), (), s32[]{:S(2)}) async-start(), calls=%async_computation.50 | async-start | bytes 2359296 | tf_op jit(solution)/shard_map/reduce_scatter | solution.py:61
  641.1 856.9 %reduce-scatter.69.cloned.1.call-start = ((), (), s32[]{:S(2)}) async-start(), calls=%async_computation.54 | async-start | bytes 18874368 | tf_op jit(solution)/shard_map/reduce_scatter | solution.py:67
  656.5 1126.9 %reduce-scatter.71.cloned.1.call-start = ((), (), s32[]{:S(2)}) async-start(), calls=%async_computation.55 | async-start | bytes 18874368 | tf_op jit(solution)/shard_map/reduce_scatter | solution.py:70
  671.5 1397.8 %reduce-scatter.73.cloned.1.call-start = ((), (), s32[]{:S(2)}) async-start(), calls=%async_computation.56 | async-start | bytes 18874368 | tf_op jit(solution)/shard_map/reduce_scatter | solution.py:73
  686.8 1521.7 %reduce-scatter.91.cloned.1.call-start = ((), (), s32[]{:S(2)}) async-start(), calls=%async_computation.65 | async-start | bytes 2162688 | tf_op jit(solution)/shard_map/reduce_scatter | solution.py:106
  689.7 1656.0 %reduce-scatter.95.cloned.1.call-start = ((), (), s32[]{:S(2)}) async-start(), calls=%async_computation.67 | async-start | bytes 2162688 | tf_op jit(solution)/shard_map/reduce_scatter | solution.py:107
  691.6 1791.8 %reduce-scatter.101.cloned.1.call-start = ((), (), s32[]{:S(2)}) async-start(), calls=%async_computation.70 | async-start | bytes 2162688 | tf_op jit(solution)/shard_map/reduce_scatter | solution.py:108
  694.4 1926.1 %reduce-scatter.89.cloned.1.call-start = ((), (), s32[]{:S(2)}) async-start(), calls=%async_computation.64 | async-start | bytes 2162688 | tf_op jit(solution)/shard_map/reduce_scatter | solution.py:105
  696.2 2057.5 %reduce-scatter.81.cloned.1.call-start = ((), (), s32[]{:S(2)}) async-start(), calls=%async_computation.60 | async-start | bytes 270336 | tf_op jit(solution)/shard_map/reduce_scatter | solution.py:102
  697.3 2189.5 %reduce-scatter.85.cloned.1.call-start = ((), (), s32[]{:S(2)}) async-start(), calls=%async_computation.62 | async-start | bytes 270336 | tf_op jit(solution)/shard_map/reduce_scatter | solution.py:104
  699.2 2324.7 %reduce-scatter.63.cloned.1.call-start = ((), (), s32[]{:S(2)}) async-start(), calls=%async_computation.51 | async-start | bytes 2162688 | tf_op jit(solution)/shard_map/reduce_scatter | solution.py:98
  701.3 2459.5 %reduce-scatter.65.cloned.1.call-start = ((), (), s32[]{:S(2)}) async-start(), calls=%async_computation.52 | async-start | bytes 2162688 | tf_op jit(solution)/shard_map/reduce_scatter | solution.py:99
  703.3 2594.4 %reduce-scatter.79.cloned.1.call-start = ((), (), s32[]{:S(2)}) async-start(), calls=%async_computation.59 | async-start | bytes 2162688 | tf_op jit(solution)/shard_map/reduce_scatter | solution.py:101
  705.5 2729.6 %reduce-scatter.83.cloned.1.call-start = ((), (), s32[]{:S(2)}) async-start(), calls=%async_computation.61 | async-start | bytes 2162688 | tf_op jit(solution)/shard_map/reduce_scatter | solution.py:103
  707.7 199.8 %copy-start.55 = (bf16[1,128,256]{2,1,0:T(8,128)(2,1)S(1)}, bf16[1,128,256]{2,1,0:T(8,128)(2,1)}, u32[]{:S(2)}) copy-start(bf16[1,128,256]{2,1,0:T(8,128)(2,1)} %reduce-scatter.41.cloned.1.call-done) | copy-start | bytes 196612
  707.7 2864.7 %reduce-scatter.75.cloned.1.call-start = ((), (), s32[]{:S(2)}) async-start(), calls=%async_computation.57 | async-start | bytes 2162688 | tf_op jit(solution)/shard_map/reduce_scatter | solution.py:100
  909.9 234.0 %copy-start.45 = (bf16[1,128,256]{2,1,0:T(8,128)(2,1)S(1)}, bf16[1,128,256]{2,1,0:T(8,128)(2,1)}, u32[]{:S(2)}) copy-start(bf16[1,128,256]{2,1,0:T(8,128)(2,1)} %reduce-scatter.59.cloned.1.call-done) | copy-start | bytes 196612
  1145.6 68.4 %copy-start.62 = (f32[128]{0:T(128)S(1)}, f32[128]{0:T(128)}, u32[]{:S(2)}) copy-start(f32[128]{0:T(128)} %copy-done.61) | copy-start | bytes 1540
  1783.5 1788.9 %copy-start.1 = (bf16[256,4096]{1,0:T(8,128)(2,1)S(1)}, bf16[256,4096]{1,0:T(8,128)(2,1)}, u32[]{:S(2)}) copy-start(bf16[256,4096]{1,0:T(8,128)(2,1)} %param.47) | copy-start | bytes 6291460
  (44 other events, 226.3 us)
Sparse Core Ops, SparseCore 0:
  10.9 26.6 all-gather.19
  39.8 49.3 all-gather.17
  91.8 49.5 all-gather.15
  147.5 18.2 reduce-scatter.36
  168.8 31.4 reduce-scatter.34
  201.7 22.5 all-gather.23
  226.5 23.9 all-gather.21
  316.0 20.0 reduce-scatter.44
  338.7 31.4 reduce-scatter.42
  373.1 20.0 reduce-scatter.46
  397.2 22.5 all-gather.25
  431.4 68.1 reduce-scatter.50
  503.6 67.3 reduce-scatter.54
  573.4 19.1 reduce-scatter.52
  595.5 20.0 reduce-scatter.40
  618.0 20.0 reduce-scatter.56
  640.9 20.0 reduce-scatter.58
  664.8 67.7 reduce-scatter.92
  736.6 66.7 reduce-scatter.96
  807.1 66.4 reduce-scatter.98
  876.9 30.4 reduce-scatter.38
  910.8 61.2 reduce-scatter.86
  975.6 67.4 reduce-scatter.66
  1046.9 60.2 reduce-scatter.76
  1109.7 30.4 reduce-scatter.48
  1143.9 68.2 reduce-scatter.60
  1216.3 281.6 reduce-scatter.68
  1501.8 281.6 reduce-scatter.70
  1787.7 281.6 reduce-scatter.72
  2072.1 136.4 reduce-scatter.90
  2211.5 134.1 reduce-scatter.94
  2348.5 134.8 reduce-scatter.100
  2486.2 134.2 reduce-scatter.88
  2623.3 130.3 reduce-scatter.80
  2756.6 130.1 reduce-scatter.84
  2889.5 134.4 reduce-scatter.62
  3026.7 134.1 reduce-scatter.64
  3163.7 133.9 reduce-scatter.78
  3300.5 134.5 reduce-scatter.82
  3438.0 134.3 reduce-scatter.74
where the time goes:
time: 3590 us; the launch traced here: 3580 us
  waiting for transfers between devices  3070 us (86%)
  matrix products  276 us (8%)
  blocking collectives  156 us (4%)
  other arithmetic  39.5 us (1%)
    reduce_scatter x1, waiting for transfers between devices, reduce_shard(): lax.psum_scatter(terms[4].astype(jnp.bfloat16), 'seq', scatter_dimension=...  282 us
    reduce_scatter x1, waiting for transfers between devices, reduce_shard(): lax.psum_scatter(terms[3].astype(jnp.bfloat16), 'seq', scatter_dimension=...  281 us
    reduce_scatter x1, waiting for transfers between devices, reduce_shard(): lax.psum_scatter(terms[2].astype(jnp.bfloat16), 'seq', scatter_dimension=...  281 us
    dot_general x48, matrix products, contract(): return jnp.einsum(form, left, right, preferred_element_type=jnp.float32)  192 us
    reduce_scatter x1, waiting for transfers between devices, reduce_shared(): lax.psum_scatter(terms[12], ('dp', 'seq'), scatter_dimension=0, tiled=True)  138 us
    reduce_scatter x1, waiting for transfers between devices, reduce_shared(): lax.psum_scatter(terms[7], ('dp', 'seq'), scatter_dimension=0, tiled=True)  137 us
    reduce_scatter x1, waiting for transfers between devices, reduce_shared(): lax.psum_scatter(terms[4], ('dp', 'seq'), scatter_dimension=0, tiled=True)  137 us
    reduce_scatter x1, waiting for transfers between devices, reduce_shared(): lax.psum_scatter(terms[11], ('dp', 'seq'), scatter_dimension=0, tiled=True)  137 us
  transfers between devices with their start and end apart: 40, of which 33 were waited for; matrix products, arithmetic and copies ran while one was open for 7% of the time, Pallas kernels for 0%

commit v1 on v0

v1 whole, which is shorter than its diff:
```python
import itertools
import math

import jax
import jax.numpy as jnp
from jax import lax
from jax.experimental import pallas as pl
from jax.experimental.pallas import tpu as pltpu
from jax.sharding import PartitionSpec as P

HD = 256
EPSILON = 1e-06
ROTARY_BASE = 10000.0
MASKED = -1e30

MESH = pl.DeviceIdType.MESH
BF16 = jnp.bfloat16
F32 = jnp.float32


class Topo:
    def __init__(self, n_dp, n_seq):
        self.n_dp, self.n_seq = n_dp, n_seq
        self.size = {"c": 2, "x": n_dp // 2, "b": n_seq // 4, "l": 2, "h": 2}

    def here(self):
        dp, seq = lax.axis_index("dp"), lax.axis_index("seq")
        nb = self.size["b"]
        outer = lax.div(seq, nb)
        return {
            "c": lax.rem(dp, 2),
            "x": lax.div(dp, 2),
            "b": lax.rem(seq, nb),
            "l": lax.rem(outer, 2),
            "h": lax.div(outer, 2),
        }

    def moved(self, at, dims, offsets, sign=1):
        new = dict(at)
        for dim, offset in zip(dims, offsets):
            n = self.size[dim]
            if offset:
                new[dim] = lax.rem(at[dim] + (offset if sign > 0 else n - offset), n)
        return new

    def seq_of(self, at):
        return (at["h"] * 2 + at["l"]) * self.size["b"] + at["b"]

    def device(self, at):
        return (at["x"] * 2 + at["c"], self.seq_of(at))

    def index(self, at, group):
        dp, seq = self.device(at)
        if group == "all":
            return dp * self.n_seq + seq
        if group == "half":
            nb = self.size["b"]
            return dp * (2 * nb) + at["l"] * nb + at["b"]
        if group == "dp":
            return dp
        if group == "seq":
            return seq
        if group == "quad":
            return at["l"] * self.size["b"] + at["b"]
        raise ValueError(group)

    def group_size(self, group):
        nb = self.size["b"]
        return {
            "all": self.n_dp * self.n_seq,
            "half": self.n_dp * 2 * nb,
            "dp": self.n_dp,
            "seq": self.n_seq,
            "quad": 2 * nb,
        }[group]


GROUP_DIMS = {"all": "cxblh", "half": "cxbl", "dp": "cx", "seq": "blh", "quad": "bl"}


def remote(src, dst, send_sem, recv_sem, device):
    return pltpu.make_async_remote_copy(
        src_ref=src,
        dst_ref=dst,
        send_sem=send_sem,
        recv_sem=recv_sem,
        device_id=device,
        device_id_type=MESH,
    )


class Gather:
    def __init__(self, topo, group, x, parts):
        self.topo, self.group, self.parts = topo, group, parts
        self.inputs = [x]
        rows, cols = x.shape
        self.outputs = [jax.ShapeDtypeStruct((topo.group_size(group), rows, cols), x.dtype)]
        self.out_specs = [pl.BlockSpec(memory_space=pl.ANY)]
        self.in_specs = [pl.BlockSpec(memory_space=pl.ANY)]
        n = topo.group_size(group)
        self.scratch = [
            pltpu.SemaphoreType.DMA((len(parts), n)),
            pltpu.SemaphoreType.DMA((len(parts), n)),
            pltpu.SemaphoreType.DMA(()),
        ]

    def peers(self):
        return {
            ((dim, d),) for dim in GROUP_DIMS[self.group] for d in range(1, self.topo.size[dim])
        }

    def run(self, ins, outs, scratch):
        topo = self.topo
        (x_ref,), (out_ref,) = ins, outs
        send_sem, recv_sem, own_sem = scratch
        at = topo.here()
        own = pltpu.make_async_copy(x_ref, out_ref.at[topo.index(at, self.group)], own_sem)
        own.start()
        started = []

        def key_index(order, key):
            k = 0
            for dim, o in zip(order, key):
                k = k * topo.size[dim] + o
            return k

        def copy(part, order, row, rows, key, stage, d):
            origin = topo.moved(at, order, key, -1)
            slot = topo.index(origin, self.group)
            new_key = tuple(d if i == stage else o for i, o in enumerate(key))
            src = (
                x_ref.at[pl.ds(row, rows)]
                if not any(key)
                else out_ref.at[slot, pl.ds(row, rows)]
            )
            k = key_index(order, new_key)
            target = topo.device(topo.moved(at, [order[stage]], [d]))
            return remote(
                src,
                out_ref.at[slot, pl.ds(row, rows)],
                send_sem.at[part, k],
                recv_sem.at[part, k],
                target,
            )

        work = []
        for part, (row, rows, order) in enumerate(self.parts):
            sizes = [topo.size[dim] for dim in order]
            keys = list(itertools.product(*[range(s) for s in sizes]))
            last = {k: max([i for i, o in enumerate(k) if o], default=-1) for k in keys}
            hops = {k: sum(1 for o in k if o) for k in keys}
            for k in keys:
                work.append((hops[k], last[k], part, row, rows, order, k))
        work.sort(key=lambda w: (w[0], w[1], w[2]))
        for hops, last, part, row, rows, order, key in work:
            if hops:
                slot = topo.index(topo.moved(at, order, key, -1), self.group)
                k = key_index(order, key)
                dst = out_ref.at[slot, pl.ds(row, rows)]
                remote(dst, dst, send_sem.at[part, k], recv_sem.at[part, k], topo.device(at)).wait_recv()
            for stage in range(last + 1, len(order)):
                for d in range(1, topo.size[order[stage]]):
                    cp = copy(part, order, row, rows, key, stage, d)
                    cp.start()
                    started.append(cp)
            yield
        for cp in started:
            cp.wait_send()
        own.wait()


class Scatter:
    def __init__(self, topo, group, x, parts, out_dtype=None):
        self.topo, self.group, self.parts = topo, group, parts
        self.inputs = [x]
        n, rows, cols = x.shape
        assert n == topo.group_size(group), (n, group)
        self.outputs = [jax.ShapeDtypeStruct((rows, cols), out_dtype or F32)]
        self.in_specs = [pl.BlockSpec(memory_space=pl.ANY)]
        self.out_specs = [pl.BlockSpec(memory_space=pltpu.VMEM)]
        self.scratch = []
        for row, nrows, order in parts:
            sizes = [topo.size[dim] for dim in order]
            keep = math.prod(sizes[1:])
            self.scratch.append(pltpu.VMEM((keep, nrows, cols), x.dtype))
            self.scratch.append(pltpu.SemaphoreType.DMA((keep,)))
            for k, s in enumerate(sizes):
                rest = math.prod(sizes[k + 1 :])
                self.scratch.append(pltpu.VMEM((max(s - 1, 1), rest, nrows, cols), x.dtype))
                self.scratch.append(pltpu.SemaphoreType.DMA((max(s - 1, 1), rest)))
                self.scratch.append(pltpu.SemaphoreType.DMA((max(s - 1, 1), rest)))

    def peers(self):
        return {
            ((dim, d),) for dim in GROUP_DIMS[self.group] for d in range(1, self.topo.size[dim])
        }

    def run(self, ins, outs, scratch):
        topo = self.topo
        (x_ref,), (out_ref,) = ins, outs
        at = topo.here()
        scratch = list(scratch)
        started, jobs = [], []
        for part, (row, nrows, order) in enumerate(self.parts):
            sizes = [topo.size[dim] for dim in order]
            acc, own_sem = scratch.pop(0), scratch.pop(0)
            bufs = [(scratch.pop(0), scratch.pop(0), scratch.pop(0)) for _ in sizes]

            def flat(key, start, sizes=sizes):
                k = 0
                for o, s in zip(key[start:], sizes[start:]):
                    k = k * s + o
                return k

            keys = list(itertools.product(*[range(s) for s in sizes]))
            first = {k: min([i for i, o in enumerate(k) if o], default=len(sizes)) for k in keys}
            keys.sort(key=lambda k: (first[k], [0 if o else 1 for o in k]))
            for key in keys:
                jobs.append((first[key], part, row, nrows, order, sizes, acc, own_sem, bufs, flat, key))
        jobs.sort(key=lambda j: j[0])

        def out_copy(job, src, key, stage):
            _, part, row, nrows, order, sizes, acc, own_sem, bufs, flat, _ = job
            buf, send_sem, recv_sem = bufs[stage]
            d = key[stage]
            k = flat(key, stage + 1)
            target = topo.device(topo.moved(at, [order[stage]], [d]))
            return remote(src, buf.at[d - 1, k], send_sem.at[d - 1, k], recv_sem.at[d - 1, k], target)

        for job in jobs:
            first, part, row, nrows, order, sizes, acc, own_sem, bufs, flat, key = job
            block = topo.index(topo.moved(at, order, key), self.group)
            if first == 0:
                cp = out_copy(job, x_ref.at[block, pl.ds(row, nrows)], key, 0)
                cp.start()
                started.append(cp)
        yield
        for job in jobs:
            first, part, row, nrows, order, sizes, acc, own_sem, bufs, flat, key = job
            if first > 0:
                block = topo.index(topo.moved(at, order, key), self.group)
                k = flat(key, 1)
                pltpu.make_async_copy(
                    x_ref.at[block, pl.ds(row, nrows)], acc.at[k], own_sem.at[k]
                ).start()
        yield
        for job in jobs:
            first, part, row, nrows, order, sizes, acc, own_sem, bufs, flat, key = job
            if first == 0:
                continue
            kk = flat(key, 1)
            block = topo.index(topo.moved(at, order, key), self.group)
            pltpu.make_async_copy(
                x_ref.at[block, pl.ds(row, nrows)], acc.at[kk], own_sem.at[kk]
            ).wait()
            terms = []
            for stage in range(first):
                buf, send_sem, recv_sem = bufs[stage]
                k = flat(key, stage + 1)
                for d in range(1, sizes[stage]):
                    ref = buf.at[d - 1, k]
                    remote(ref, ref, send_sem.at[d - 1, k], recv_sem.at[d - 1, k], topo.device(at)).wait_recv()
                    terms.append((buf, d - 1, k))
            step = 16 if nrows % 16 == 0 else 8
            final = first == len(sizes)

            def add(r, _, terms=terms, acc=acc, kk=kk, final=final, row=row, step=step):
                r0 = pl.multiple_of(r * step, step)
                total = acc[kk, pl.ds(r0, step), :].astype(F32)
                for buf, d, k in terms:
                    total = total + buf[d, k, pl.ds(r0, step), :].astype(F32)
                if final:
                    out_ref[pl.ds(row + r0, step), :] = total.astype(out_ref.dtype)
                else:
                    acc[kk, pl.ds(r0, step), :] = total.astype(acc.dtype)
                return 0

            lax.fori_loop(0, nrows // step, add, 0)
            if not final:
                cp = out_copy(job, acc.at[kk], key, first)
                cp.start()
                started.append(cp)
            yield
        for cp in started:
            cp.wait_send()


class Exchange:
    def __init__(self, topo, group, x):
        self.topo, self.group = topo, group
        self.inputs = [x]
        n = x.shape[0]
        assert n == topo.group_size(group)
        self.outputs = [jax.ShapeDtypeStruct(x.shape, x.dtype)]
        self.in_specs = [pl.BlockSpec(memory_space=pl.ANY)]
        self.out_specs = [pl.BlockSpec(memory_space=pl.ANY)]
        self.scratch = [
            pltpu.SemaphoreType.DMA((n,)),
            pltpu.SemaphoreType.DMA((n,)),
            pltpu.SemaphoreType.DMA(()),
        ]

    def offsets(self):
        dims = GROUP_DIMS[self.group]
        return dims, [
            o for o in itertools.product(*[range(self.topo.size[d]) for d in dims]) if any(o)
        ]

    def peers(self):
        dims, offsets = self.offsets()
        return {tuple((dim, o) for dim, o in zip(dims, off) if o) for off in offsets}

    def run(self, ins, outs, scratch):
        topo = self.topo
        (x_ref,), (out_ref,) = ins, outs
        send_sem, recv_sem, own_sem = scratch
        at = topo.here()
        me = topo.index(at, self.group)
        own = pltpu.make_async_copy(x_ref.at[me], out_ref.at[me], own_sem)
        own.start()
        dims, offsets = self.offsets()
        started = []
        for i, off in enumerate(offsets):
            there = topo.moved(at, dims, off)
            cp = remote(
                x_ref.at[topo.index(there, self.group)],
                out_ref.at[me],
                send_sem.at[i],
                recv_sem.at[i],
                topo.device(there),
            )
            cp.start()
            started.append(cp)
        yield
        for i, off in enumerate(offsets):
            ref = out_ref.at[topo.index(topo.moved(at, dims, off, -1), self.group)]
            remote(ref, ref, send_sem.at[i], recv_sem.at[i], topo.device(at)).wait_recv()
            yield
        for cp in started:
            cp.wait_send()
        own.wait()


class Finish:
    def __init__(self, topo, x, y):
        self.topo = topo
        self.inputs = [x, y]
        self.outputs = [
            jax.ShapeDtypeStruct(x.shape, x.dtype),
            jax.ShapeDtypeStruct(y.shape, y.dtype),
        ]
        self.in_specs = [pl.BlockSpec(memory_space=pl.ANY)] * 2
        self.out_specs = [pl.BlockSpec(memory_space=pl.ANY)] * 2
        self.inner = Exchange(topo, "seq", y)
        self.scratch = self.inner.scratch + [
            pltpu.SemaphoreType.DMA(()),
            pltpu.SemaphoreType.DMA(()),
            pltpu.SemaphoreType.DMA(()),
        ]

    def peers(self):
        return self.inner.peers()

    def route(self):
        topo = self.topo
        dp, seq = lax.axis_index("dp"), lax.axis_index("seq")
        n = seq * topo.n_dp + dp
        target = (lax.div(n, topo.n_seq), lax.rem(n, topo.n_seq))
        m = dp * topo.n_seq + seq
        source = (lax.rem(m, topo.n_dp), lax.div(m, topo.n_dp))
        stays = (target[0] == dp) & (target[1] == seq)
        return target, source, stays

    def greet(self, barrier):
        target, source, stays = self.route()

        @pl.when(jnp.logical_not(stays))
        def _():
            pl.semaphore_signal(barrier, inc=1, device_id=source, device_id_type=MESH)

        return jnp.where(stays, 0, 1)

    def run(self, ins, outs, scratch):
        (x_ref, y_ref), (x_out, y_out) = ins, outs
        send_sem, recv_sem, own_sem = scratch[3:]
        target, source, stays = self.route()
        cp = remote(x_ref, x_out, send_sem, recv_sem, target)
        own = pltpu.make_async_copy(x_ref, x_out, own_sem)

        @pl.when(stays)
        def _():
            own.start()

        @pl.when(jnp.logical_not(stays))
        def _():
            cp.start()

        yield from self.inner.run([y_ref], [y_out], scratch[:3])

        @pl.when(stays)
        def _():
            own.wait()

        @pl.when(jnp.logical_not(stays))
        def _():
            cp.wait()


def communicate(topo, name, collective_id, *ops):
    n_in = [len(op.inputs) for op in ops]
    n_out = [len(op.outputs) for op in ops]
    n_scratch = [len(op.scratch) for op in ops]

    def kernel(*refs):
        refs = list(refs)
        take = lambda counts: [[refs.pop(0) for _ in range(k)] for k in counts]
        ins, outs, scratch = take(n_in), take(n_out), take(n_scratch)
        at = topo.here()
        peers = sorted(set().union(*[op.peers() for op in ops]))
        barrier = pltpu.get_barrier_semaphore()
        for peer in peers:
            there = topo.device(topo.moved(at, [p[0] for p in peer], [p[1] for p in peer]))
            pl.semaphore_signal(barrier, inc=1, device_id=there, device_id_type=MESH)
        greeted = len(peers)
        for op in ops:
            if hasattr(op, "greet"):
                greeted = greeted + op.greet(barrier)
        pl.semaphore_wait(barrier, greeted)
        running = [op.run(i, o, s) for op, i, o, s in zip(ops, ins, outs, scratch)]
        while running:
            for step in list(running):
                try:
                    next(step)
                except StopIteration:
                    running.remove(step)

    results = pl.pallas_call(
        kernel,
        name=name,
        out_shape=[s for op in ops for s in op.outputs],
        in_specs=[s for op in ops for s in op.in_specs],
        out_specs=[s for op in ops for s in op.out_specs],
        scratch_shapes=[s for op in ops for s in op.scratch],
        compiler_params=pltpu.CompilerParams(
            collective_id=collective_id, has_side_effects=True, vmem_limit_bytes=58 << 20
        ),
    )(*[x for op in ops for x in op.inputs])
    results = list(results)
    return [[results.pop(0) for _ in range(k)] for k in n_out]


def row_parts(rows, orders, weights, step=16):
    parts, row, total = [], 0, sum(weights)
    for i, (order, weight) in enumerate(zip(orders, weights)):
        n = rows - row if i == len(orders) - 1 else min(rows - row, int(round(rows * weight / total / step)) * step)
        if n:
            parts.append((row, n, order))
            row += n
    return parts


def matmul(left, right):
    return jnp.dot(left, right, preferred_element_type=jnp.float32)


def contract(form, left, right):
    return jnp.einsum(form, left, right, preferred_element_type=jnp.float32)


def rotary(positions, size):
    half_size = size // 2
    frequency = ROTARY_BASE ** (-(jnp.arange(half_size, dtype=jnp.float32) * 2.0) / size)
    angles = positions.astype(jnp.float32)[:, None] * frequency[None, :]
    return (jnp.cos(angles), jnp.sin(angles))


def rotate(values, cosine_table, sine_table):
    half_size = values.shape[-1] // 2
    first_half = values[..., :half_size]
    second_half = values[..., half_size:]
    return jnp.concatenate(
        [
            first_half * cosine_table - second_half * sine_table,
            second_half * cosine_table + first_half * sine_table,
        ],
        axis=-1,
    )


def normalize(values, gain_vector):
    inverse_rms = lax.rsqrt(jnp.mean(values * values, axis=-1, keepdims=True) + EPSILON)
    unit_rows = values * inverse_rms
    return (unit_rows * gain_vector, unit_rows, inverse_rms)


def norm_backward(grad_normed, unit_rows, inverse_rms, gain_vector):
    gain_term = jnp.sum(grad_normed * unit_rows, axis=0)
    grad_unit = grad_normed * gain_vector
    inner = jnp.mean(grad_unit * unit_rows, axis=-1, keepdims=True)
    return (gain_term, inverse_rms * (grad_unit - unit_rows * inner))


def dot_t(left, right):
    return lax.dot_general(left, right, (((1,), (1,)), ((), ())), preferred_element_type=F32)


def t_dot(left, right):
    return lax.dot_general(left, right, (((0,), (0,)), ((), ())), preferred_element_type=F32)


GELU_C = math.sqrt(2.0 / math.pi)


def gelu_parts(v):
    square = v * v
    t = jnp.tanh(GELU_C * (v + 0.044715 * v * square))
    half_up = 0.5 * (1.0 + t)
    slope = half_up + 0.5 * v * (1.0 - t * t) * (GELU_C * (1.0 + 3.0 * 0.044715 * square))
    return v * half_up, slope


def feed_forward(topo, normed_all, grad_all, w_gate, w_up, w_down, low_gu, low_d, high):
    tokens, width = normed_all.shape
    units = w_gate.shape[1]
    ranks = low_d.shape[0]
    quad = topo.group_size("quad")
    half_width = width // 2
    d_rows, r_rows = half_width // quad, ranks // quad
    tile = 512
    run = (topo.n_seq // 2) * 128 // tile
    own = tokens // tile // 2
    block = 256

    def chunk(t, high_ref):
        mine = t < own
        k = jnp.where(mine, t, t - own)
        side = jnp.where(mine, high_ref[0], 1 - high_ref[0])
        return lax.div(k, run) * 2 * run + side * run + lax.rem(k, run)

    def kernel(
        high_ref, n_ref, g_ref, wg_ref, wu_ref, wd_ref, lgu_ref, ld_ref,
        down_ref, gn_ref, dg_ref, du_ref, dd_ref,
        acc_g, acc_u, acc_d, mix_s, gg_s, gu_s,
    ):
        t = pl.program_id(0)

        @pl.when(t == 0)
        def _():
            acc_g[...] = jnp.zeros_like(acc_g)
            acc_u[...] = jnp.zeros_like(acc_u)
            acc_d[...] = jnp.zeros_like(acc_d)

        low = matmul(n_ref[...], lgu_ref[...])
        low_g = low[:, :ranks].astype(BF16)
        low_u = low[:, ranks:].astype(BF16)
        low_b = dot_t(g_ref[...], ld_ref[...]).astype(BF16)

        def one(i, _):
            cols = pl.ds(pl.multiple_of(i * block, block), block)
            gate = matmul(n_ref[...], wg_ref[:, cols])
            up = matmul(n_ref[...], wu_ref[:, cols])
            act, slope = gelu_parts(gate)
            gm = dot_t(g_ref[...], wd_ref[cols, :])
            mix_s[:, cols] = (act * up).astype(BF16)
            gg_s[:, cols] = (gm * up * slope).astype(BF16)
            gu_s[:, cols] = (gm * act).astype(BF16)
            return 0

        lax.fori_loop(0, units // block, one, 0)

        @pl.when(t < own)
        def _():
            def two(i, _):
                cols = pl.ds(pl.multiple_of(i * block, block), block)
                down_ref[:, cols] = matmul(mix_s[...], wd_ref[:, cols]).astype(BF16)
                gn_ref[:, cols] = (
                    dot_t(gg_s[...], wg_ref[cols, :]) + dot_t(gu_s[...], wu_ref[cols, :])
                ).astype(BF16)
                return 0

            lax.fori_loop(0, width // block, two, 0)

        for acc, low_rows, grads in ((acc_g, low_g, gg_s), (acc_u, low_u, gu_s), (acc_d, low_b, mix_s)):
            acc[half_width:, :] += t_dot(low_rows, grads[...])

        def three(i, _):
            rows = pl.ds(pl.multiple_of(i * block, block), block)
            cols = pl.ds(pl.multiple_of(high_ref[0] * half_width + i * block, block), block)
            acc_g[rows, :] += t_dot(n_ref[:, cols], gg_s[...])
            acc_u[rows, :] += t_dot(n_ref[:, cols], gu_s[...])
            acc_d[rows, :] += t_dot(g_ref[:, cols], mix_s[...])
            return 0

        lax.fori_loop(0, half_width // block, three, 0)

        @pl.when(t == pl.num_programs(0) - 1)
        def _():
            for acc, out in ((acc_g, dg_ref), (acc_u, du_ref), (acc_d, dd_ref)):
                for q in range(quad):
                    out[q, :d_rows, :] = acc[q * d_rows : (q + 1) * d_rows, :].astype(BF16)
                    out[q, d_rows:, :] = acc[
                        half_width + q * r_rows : half_width + (q + 1) * r_rows, :
                    ].astype(BF16)

    whole = lambda t, h: (0, 0)
    once = pl.Buffered(1)
    grads = jax.ShapeDtypeStruct((quad, d_rows + r_rows, units), BF16)
    grad_spec = pl.BlockSpec((quad, d_rows + r_rows, units), lambda t, h: (0, 0, 0), pipeline_mode=once)
    part = jax.ShapeDtypeStruct((tokens // 2, width), BF16)
    part_spec = pl.BlockSpec((tile, width), lambda t, h: (jnp.minimum(t, own - 1), 0))
    row_spec = pl.BlockSpec((tile, width), lambda t, h: (chunk(t, h), 0))
    flops = 2 * tokens * units * width * 9
    return pl.pallas_call(
        kernel,
        name="feed_forward",
        grid_spec=pltpu.PrefetchScalarGridSpec(
            num_scalar_prefetch=1,
            grid=(2 * own,),
            in_specs=[
                row_spec,
                row_spec,
                pl.BlockSpec((width, units), whole, pipeline_mode=once),
                pl.BlockSpec((width, units), whole, pipeline_mode=once),
                pl.BlockSpec((units, width), whole, pipeline_mode=once),
                pl.BlockSpec((width, 2 * ranks), whole, pipeline_mode=once),
                pl.BlockSpec((ranks, width), whole, pipeline_mode=once),
            ],
            out_specs=[part_spec, part_spec, grad_spec, grad_spec, grad_spec],
            scratch_shapes=[
                pltpu.VMEM((half_width + ranks, units), F32),
                pltpu.VMEM((half_width + ranks, units), F32),
                pltpu.VMEM((half_width + ranks, units), F32),
                pltpu.VMEM((tile, units), BF16),
                pltpu.VMEM((tile, units), BF16),
                pltpu.VMEM((tile, units), BF16),
            ],
        ),
        out_shape=[part, part, grads, grads, grads],
        compiler_params=pltpu.CompilerParams(vmem_limit_bytes=60 << 20),
        cost_estimate=pl.CostEstimate(flops=flops, bytes_accessed=4 * tokens * width, transcendentals=0),
    )(high, normed_all, grad_all, w_gate, w_up, w_down, low_gu, low_d)


def local(
    topo,
    tokens, segment_ids, out_grad, gain_attn, gain_mlp, w_query, w_key, w_value, w_out, w_gate, w_up, w_down,
    query_adapt, query_expand, key_adapt, key_expand, value_adapt, value_expand, out_adapt, out_expand,
    gate_adapt, gate_expand, up_adapt, up_expand, down_adapt, down_expand,
):
    rows, width = tokens.shape[2], tokens.shape[3]
    groups, n_seq = topo.n_dp, topo.n_seq
    length = rows * n_seq
    heads_dev = w_query.shape[1] // HD
    head_cols = heads_dev * HD
    rank = query_adapt.shape[1]
    scale_qk = HD ** (-0.5)
    quad = topo.group_size("quad")
    units = w_gate.shape[1] // quad
    seq = lax.axis_index("seq")
    dp = lax.axis_index("dp")
    high = lax.div(seq, quad)
    member = lax.rem(seq, quad)

    def merged(weight, adapt, expand):
        return (weight.astype(F32) + matmul(adapt, expand)).astype(BF16)

    def unit_cols(a):
        return lax.dynamic_slice_in_dim(a, member * units, units, 1)

    def unit_rows(a):
        return lax.dynamic_slice_in_dim(a, member * units, units, 0)

    wq = merged(w_query, query_adapt, query_expand)
    wk = merged(w_key, key_adapt, key_expand)
    wv = merged(w_value, value_adapt, value_expand)
    wo = merged(w_out, out_adapt, out_expand)
    wg = merged(unit_cols(w_gate), gate_adapt, unit_cols(gate_expand))
    wu = merged(unit_cols(w_up), up_adapt, unit_cols(up_expand))
    wd = merged(unit_rows(w_down), unit_rows(down_adapt), down_expand)
    half_rank = rank // 2
    my_ranks = lambda a, axis: lax.dynamic_slice_in_dim(a, high * half_rank, half_rank, axis)
    low_gu = jnp.concatenate([my_ranks(gate_adapt, 1), my_ranks(up_adapt, 1)], axis=1)
    low_d = my_ranks(down_expand, 0)

    token_rows = tokens[0, 0].astype(F32)
    grad_rows_in = out_grad[0, 0]
    normed, unit_attn, rms_attn = normalize(token_rows, gain_attn)
    normed_attn = normed.astype(BF16)
    positions = seq * rows + jnp.arange(rows, dtype=jnp.int32)
    cosine_table, sine_table = rotary(positions, HD)
    cosine_heads, sine_heads = cosine_table[:, None, :], sine_table[:, None, :]
    key_rot = rotate(matmul(normed_attn, wk), cosine_table, sine_table).astype(BF16)
    value_rows = matmul(normed_attn, wv).astype(BF16)
    key_value = jnp.concatenate([key_rot, value_rows], axis=1)
    seg_rows = jnp.zeros((16, rows), F32).at[0].set(segment_ids[0, 0].astype(F32))

    zyx, xzy = "lhbxc", "xlhbc"
    (normed_all,), (kv_all,), (seg_all,), (grad_all,) = communicate(
        topo, "gather_attention", 0,
        Gather(topo, "dp", normed_attn, [(0, rows, "xc")]),
        Gather(topo, "all", key_value, row_parts(rows, (zyx, xzy), (7, 4))),
        Gather(topo, "all", seg_rows, [(0, 16, zyx)]),
        Gather(topo, "all", grad_rows_in, row_parts(rows, (zyx, xzy), (7, 4))),
    )
    kv_all = kv_all.reshape(groups, length, 2 * HD)
    keys_all, values_all = kv_all[..., :HD], kv_all[..., HD:]
    segments = seg_all[:, 0, :].reshape(groups, length)
    own_segments = lax.dynamic_slice_in_dim(segments, seq * rows, rows, 1)
    key_positions = jnp.arange(length, dtype=jnp.int32)
    causal = (key_positions[None, :] <= positions[:, None])[None, :, :]
    allowed = (causal & (own_segments[:, :, None] == segments[:, None, :]))[:, None, :, :]

    queries = matmul(normed_all.reshape(groups * rows, width), wq)
    query_rot = rotate(queries.reshape(groups, rows, heads_dev, HD), cosine_heads, sine_heads).astype(BF16)
    scores = jnp.where(allowed, contract("sthd,sjd->shtj", query_rot, keys_all) * scale_qk, MASKED)
    row_top = jnp.max(scores, axis=-1, keepdims=True)
    log_total = row_top + jnp.log(jnp.sum(jnp.exp(scores - row_top), axis=-1, keepdims=True))
    prob_low = jnp.exp(scores - log_total).astype(BF16)
    heads_out = (
        contract("shtj,sjd->sthd", prob_low, values_all).reshape(groups * rows, head_cols).astype(BF16)
    )
    out_part = matmul(heads_out, wo).astype(BF16).reshape(groups, rows, width)
    (out_sum,), = communicate(
        topo, "sum_attention", 1, Scatter(topo, "dp", out_part, [(0, rows, "cx")])
    )
    middle = token_rows + out_sum
    normed, unit_mlp, rms_mlp = normalize(middle, gain_mlp)
    normed_mlp = normed.astype(BF16)
    (mlp_all,), = communicate(
        topo, "gather_mlp", 2, Gather(topo, "all", normed_mlp, row_parts(rows, (zyx, xzy), (7, 4)))
    )
    flat = lambda a: a.reshape(-1, width)
    down_part, gn_part, dg, du, dd = feed_forward(
        topo, flat(mlp_all), flat(grad_all), wg, wu, wd, low_gu, low_d, high.reshape(1)
    )
    half = topo.group_size("half")
    blocks = lambda a: a.reshape(half, rows, width)
    thirds = row_parts(rows, ("cxbl", "cblx", "clxb"), (1, 1, 1))
    down_op = Scatter(topo, "half", blocks(down_part), thirds)
    gn_op = Scatter(topo, "half", blocks(gn_part), thirds)
    if half > 16:
        (gn_sum,), = communicate(topo, "sum_mlp", 3, gn_op)
        (down_sum,), = communicate(topo, "sum_down", 10, down_op)
    else:
        (down_sum,), (gn_sum,) = communicate(topo, "sum_mlp", 3, down_op, gn_op)
    result_rows = (middle + down_sum).astype(BF16)
    gain_mlp_term, grad_from_mlp = norm_backward(gn_sum, unit_mlp, rms_mlp, gain_mlp)
    grad_middle = grad_rows_in.astype(F32) + grad_from_mlp
    grad_branch_attn = grad_middle.astype(BF16)
    (grad_attn_all,), (dg,), (du,), (dd,) = communicate(
        topo, "gather_back", 4,
        Gather(topo, "dp", grad_branch_attn, [(0, rows, "xc")]),
        Exchange(topo, "quad", dg),
        Exchange(topo, "quad", du),
        Exchange(topo, "quad", dd),
    )
    grad_attn_all = grad_attn_all.reshape(groups * rows, width)
    grad_heads = dot_t(grad_attn_all, wo).astype(BF16)
    grad_heads_split = grad_heads.reshape(groups, rows, heads_dev, HD)
    scores_again = jnp.where(allowed, contract("sthd,sjd->shtj", query_rot, keys_all) * scale_qk, MASKED)
    probabilities = jnp.exp(scores_again - log_total)
    grad_values_part = contract("shtj,sthd->sjd", probabilities.astype(BF16), grad_heads_split)
    grad_probs = contract("sthd,sjd->shtj", grad_heads_split, values_all)
    delta_rows = jnp.sum(probabilities * grad_probs, axis=-1, keepdims=True)
    grad_scores = (probabilities * (grad_probs - delta_rows)).astype(BF16)
    grad_query_rot = contract("shtj,sjd->sthd", grad_scores, keys_all) * scale_qk
    grad_keys_part = contract("shtj,sthd->sjd", grad_scores, query_rot) * scale_qk
    grad_query = (
        rotate(grad_query_rot, cosine_heads, -sine_heads).reshape(groups * rows, head_cols).astype(BF16)
    )
    gn_attn_part = dot_t(grad_query, wq).astype(BF16).reshape(groups, rows, width)
    grad_kv_part = jnp.concatenate([grad_keys_part, grad_values_part], axis=-1).astype(BF16)
    (gn_attn_sum,), (grad_kv_sum,) = communicate(
        topo, "sum_back", 5,
        Scatter(topo, "dp", gn_attn_part, [(0, rows, "cx")]),
        Scatter(
            topo, "all", grad_kv_part.reshape(groups * n_seq, rows, 2 * HD),
            row_parts(rows, ("cxblh", "cblhx"), (1, 1)),
        ),
    )
    grad_key = rotate(grad_kv_sum[:, :HD], cosine_table, -sine_table).astype(BF16)
    grad_value = grad_kv_sum[:, HD:].astype(BF16)
    grad_normed_attn = gn_attn_sum + dot_t(grad_key, wk) + dot_t(grad_value, wv)
    gain_attn_term, grad_from_attn = norm_backward(grad_normed_attn, unit_attn, rms_attn, gain_attn)
    grad_rows = (grad_middle + grad_from_attn).astype(BF16)

    (grad_kv_group,), = communicate(
        topo, "gather_kv", 6,
        Gather(topo, "dp", jnp.concatenate([grad_key, grad_value], axis=1), [(0, rows, "xc")]),
    )
    grad_kv_group = grad_kv_group.reshape(groups * rows, 2 * HD)
    normed_group = normed_all.reshape(groups * rows, width)
    query_low = matmul(normed_group, query_adapt).astype(BF16)
    grad_out_low = dot_t(grad_attn_all, out_expand).astype(BF16)
    d_rows, r_rows = width // n_seq, rank // n_seq
    per_dev_d, per_dev_r = d_rows // groups, r_rows // groups
    cols = lax.dynamic_slice_in_dim(normed_group, dp * (width // groups), width // groups, 1)
    my_kv_ranks = lambda a: lax.dynamic_slice_in_dim(a, dp * (rank // groups), rank // groups, 1)
    key_low = matmul(normed_group, my_kv_ranks(key_adapt)).astype(BF16)
    value_low = matmul(normed_group, my_kv_ranks(value_adapt)).astype(BF16)
    kv_weight = t_dot(cols, grad_kv_group)
    kv_expand = jnp.concatenate(
        [t_dot(key_low, grad_kv_group[:, :HD]), t_dot(value_low, grad_kv_group[:, HD:])], axis=1
    )
    by_seq = lambda a: a.reshape(n_seq, -1, a.shape[-1])
    widen = lambda a: jnp.pad(a, ((0, 0), (0, 0), (0, 2 * HD - a.shape[-1])))
    fold = lambda a: a if a.shape[-1] == 2 * HD else widen(a)
    gains = jnp.stack([gain_attn_term, gain_mlp_term]).reshape(2, n_seq, d_rows).transpose(1, 0, 2)
    gains = jnp.pad(gains, ((0, 0), (0, 6), (0, 2 * HD - d_rows)))
    pieces = [
        fold(by_seq(t_dot(normed_group, grad_query))),
        fold(by_seq(t_dot(query_low, grad_query))),
        fold(by_seq(t_dot(grad_attn_all, heads_out))),
        fold(by_seq(t_dot(grad_out_low, heads_out))),
        by_seq(kv_weight),
        by_seq(kv_expand),
        gains,
    ]
    sizes = [p.shape[1] for p in pieces]
    fill = -sum(sizes) % 16
    stacked = jnp.concatenate(
        [p.astype(BF16) for p in pieces] + [jnp.zeros((n_seq, fill, 2 * HD), BF16)], axis=1
    )
    (weights,), = communicate(
        topo, "sum_weights", 7,
        Scatter(topo, "seq", stacked, row_parts(stacked.shape[1], ("blh", "lhb"), (9, 4))),
    )
    starts = [sum(sizes[:i]) for i in range(len(sizes))]
    grad_wq, grad_qe, grad_wo, grad_oa, grad_wkv, grad_kve, gains = [
        weights[a : a + s] for a, s in zip(starts, sizes)
    ]
    grad_wq, grad_qe = grad_wq[:, :head_cols], grad_qe[:, :head_cols]
    grad_wo, grad_oa = grad_wo[:, :head_cols].T, grad_oa[:, :head_cols].T

    def unfold(a):
        full = a.astype(F32).transpose(1, 0, 2).reshape(d_rows + r_rows, quad * units)
        return full[:d_rows], full[d_rows:]

    grad_wg, grad_ge = unfold(dg)
    grad_wu, grad_ue = unfold(du)
    grad_wd_t, grad_da_t = unfold(dd)
    grad_wd, grad_da = grad_wd_t.T, grad_da_t.T

    adapt = jnp.stack(
        [
            dot_t(grad_wg.astype(BF16), gate_expand),
            dot_t(grad_wu.astype(BF16), up_expand),
            dot_t(grad_wq.astype(BF16), query_expand),
        ]
    )
    expand = jnp.stack(
        [
            matmul(down_adapt.T, grad_wd.astype(BF16)),
            matmul(out_adapt.T, grad_wo.astype(BF16)),
        ]
    )
    adapt = adapt.reshape(3, groups, per_dev_d, rank).transpose(1, 0, 2, 3).reshape(groups, -1, rank)
    expand = expand.reshape(2, groups, rank // groups, d_rows).transpose(1, 0, 2, 3).reshape(groups, -1, d_rows)
    expand = jnp.pad(expand, ((0, 0), (0, 0), (0, rank - d_rows)))
    small_gains = jnp.pad(
        gains[:, :d_rows].reshape(8, groups, per_dev_d).transpose(1, 0, 2), ((0, 0), (0, 8), (0, rank - per_dev_d))
    )
    small = jnp.concatenate([adapt, small_gains, expand], axis=1).astype(BF16)
    n_adapt = 3 * per_dev_d
    (small_sum,), = communicate(
        topo, "sum_small", 8, Scatter(topo, "dp", small, [(0, small.shape[1], "cx")])
    )
    per_seq = rank // groups // n_seq
    across = small_sum[n_adapt + 16 :, :d_rows].reshape(2, n_seq, per_seq, d_rows).transpose(1, 0, 2, 3)
    across = across.reshape(n_seq, 2 * per_seq, d_rows)
    (own_adapt, own_expand), = communicate(
        topo, "finish", 9, Finish(topo, small_sum[: n_adapt + 16], across)
    )
    grad_ga, grad_ua, grad_qa = own_adapt[:n_adapt].reshape(3, per_dev_d, rank)
    grad_gain_attn = own_adapt[n_adapt, :per_dev_d]
    grad_gain_mlp = own_adapt[n_adapt + 1, :per_dev_d]
    own_expand = own_expand.reshape(n_seq, 2, per_seq, d_rows).transpose(1, 2, 0, 3).reshape(2, per_seq, width)
    grad_de, grad_oe = own_expand[0], own_expand[1]
    grad_wk, grad_wv = grad_wkv[:, :HD], grad_wkv[:, HD:]
    grad_ka = dot_t(grad_wk.astype(BF16), key_expand)
    grad_va = dot_t(grad_wv.astype(BF16), value_expand)
    grad_ke, grad_ve = grad_kve[:, :HD], grad_kve[:, HD:]
    return (
        result_rows[None, None], grad_rows[None, None],
        grad_gain_attn, grad_gain_mlp,
        grad_wq, grad_wk, grad_wv, grad_wo, grad_wg, grad_wu, grad_wd,
        grad_qa, grad_qe, grad_ka, grad_ke, grad_va, grad_ve, grad_oa, grad_oe,
        grad_ga, grad_ge, grad_ua, grad_ue, grad_da, grad_de,
    )


def solution(mesh):
    topo = Topo(mesh.shape["dp"], mesh.shape["seq"])
    both = ("dp", "seq")
    in_specs = (
        P(None, "dp", "seq", None), P(None, "dp", "seq"), P(None, "dp", "seq", None),
        P(), P(), P(None, "dp"), P(), P(), P("dp", None), P(None, "dp"), P(None, "dp"), P("dp", None),
        P(), P(None, "dp"), P(), P(), P(), P(), P("dp", None), P(),
        P(), P(None, "dp"), P(), P(None, "dp"), P("dp", None), P(),
    )
    out_specs = (
        P(None, "dp", "seq", None), P(None, "dp", "seq", None), P(both), P(both),
        P("seq", "dp"), P(both, None), P(both, None), P("dp", "seq"), P("seq", "dp"), P("seq", "dp"), P("dp", "seq"),
        P(both, None), P("seq", "dp"), P(both, None), P(both, None), P(both, None), P(both, None),
        P("dp", "seq"), P(both, None), P(both, None), P("seq", "dp"), P(both, None), P("seq", "dp"),
        P("dp", "seq"), P(both, None),
    )
    return jax.shard_map(
        lambda *args: local(topo, *args), mesh=mesh, in_specs=in_specs, out_specs=out_specs, check_vma=False
    )
```

time: 3590 us -> 917 us (0.26)
  waiting for transfers between devices: 3070 us -> 0 us
  Pallas kernels: 0 us -> 669 us
  matrix products: 276 us -> 84.5 us
  blocking collectives: 156 us -> 0 us
  local copies, waits for them, and re-layouts: 14.2 us -> 124 us
    reduce_scatter x34 -> x0, waiting for transfers between devices: 3030 us -> none  [the longest x1 282 us: reduce_shard(): lax.psum_scatter(terms[4].astype(jnp.bfloat16), 'seq', scatter_dimension=...]
    pallas_call x0 -> x11, Pallas kernels: none -> 669 us  [the longest x10 508 us: communicate(): pl.pallas_call(kernel, name=name, out_shape=[s for op in ops for s in op....]
    dot_general x48 -> x6, matrix products: 192 us -> 10.3 us  [contract(): return jnp.einsum(form, left, right, preferred_element_type=jnp.float32)]
    all_gather x8 -> x0, blocking collectives: 115 us -> none  [the longest x1 68.8 us: local(): lax.all_gather(segment_ids, ('dp', 'seq'), axis=2, tiled=True)]
    dot_general x21 -> x14, matrix products: 84.7 us -> 36.1 us  [matmul(): return jnp.dot(left, right, preferred_element_type=jnp.float32)]
    all_gather x6 -> x0, waiting for transfers between devices: 47.2 us -> none  [the longest x1 20 us: local(): lax.all_gather(grad_branch[None], 'dp', axis=0, tiled=True)]
    unnamed x1 -> x0, blocking collectives: 40.4 us -> none
    slice x1 -> x19, local copies, waits for them, and re-layouts: 1.27 us -> 41.2 us  [the longest x11 31.2 us: unfold(): return (full[:d_rows], full[d_rows:])]
  transfers between devices with their start and end apart: 40 -> 0, of which waited for: 33 -> 0; matrix products, arithmetic and copies ran while one was open for 7% -> 0% of each run, Pallas kernels for 0% -> 0%
where the time goes in v1:
time: 917 us; the launch traced here: 911 us
  Pallas kernels  669 us (73%)
  local copies, waits for them, and re-layouts  124 us (14%)
  matrix products  84.5 us (9%)
  other arithmetic  30.8 us (3%)
    pallas_call x10, Pallas kernels, communicate(): pl.pallas_call(kernel, name=name, out_shape=[s for op in ops for s in op....  508 us
    pallas_call x1, Pallas kernels, feed_forward(): pl.pallas_call(kernel, name='feed_forward', grid_spec=pltpu.PrefetchScala...  161 us
    dot_general x14, matrix products, matmul(): return jnp.dot(left, right, preferred_element_type=jnp.float32)  36.1 us
    unnamed x159, local copies, waits for them, and re-layouts  34.9 us
    slice x11, local copies, waits for them, and re-layouts, unfold(): return (full[:d_rows], full[d_rows:])  31.2 us
    dot_general x10, matrix products, dot_t(): lax.dot_general(left, right, (((1,), (1,)), ((), ())), preferred_element_...  19.2 us
    dot_general x7, matrix products, t_dot(): lax.dot_general(left, right, (((0,), (0,)), ((), ())), preferred_element_...  18.9 us

profile of v1, /device:TPU:0, one launch (start us, length us, event | category | flops | bytes accessed | tf_op | source)
XLA Modules:
  0.0 911.1 jit_solution(16248890845275700031)
XLA Ops:
  4.6 2.2 fusion.7
  10.3 107.9 %gather_attention.1 = (bf16[4,128,2048]{2,1,0:T(8,128)(2,1)}, bf16[32,128,512]{2,1,0:T(8,128)(2,1)}, f32[32,16,128]{2,1,0:T(8,128)}, bf16[32,128,2048]{2,1,0:T(8,128)(2,1)}) custom-call(bf16[128,2048]{1,0:T(8,128)(2,1)} %copy-done.14, bf16[128,512]{1,0:T(8,128)(2,1)} %pad_maximum_fusion.6.refs_1_, f32[16,128]{1,0:T(8,128)} %scatter.4.refs_2_, ...), custom_call_target="tpu_custom_call" | custom-call | tf_op jit(solution)/shard_map/gather_attention/pallas_call | solution.py:437
  121.2 1.6 compare_and_fusion
  122.8 3.9 copy.69
  126.7 2.8 add_convert_fusion.2
  131.1 1.8 copy-done.72
  135.6 2.3 fusion.32
  139.4 2.7 add_convert_fusion.1
  142.1 2.6 convolution_convert_fusion.1
  144.7 18.0 %sum_attention.1 = f32[128,2048]{1,0:T(8,128)} custom-call(bf16[4,128,2048]{2,1,0:T(8,128)(2,1)} %bitcast.296), custom_call_target="tpu_custom_call" | custom-call | tf_op jit(solution)/shard_map/sum_attention/pallas_call | solution.py:437
  166.2 81.0 %gather_mlp.1 = bf16[32,128,2048]{2,1,0:T(8,128)(2,1)} custom-call(bf16[128,2048]{1,0:T(8,128)(2,1)} %multiply_convert_fusion.refs_0_), custom_call_target="tpu_custom_call" | custom-call | tf_op jit(solution)/shard_map/gather_mlp/pallas_call | solution.py:437
  250.5 5.7 add_convert_fusion.wd_ref
  256.1 5.6 fusion.wu_ref
  261.7 5.6 fusion.1.wg_ref
  267.3 160.7 %feed_forward.1 = (bf16[2048,2048]{1,0:T(8,128)(2,1)}, bf16[2048,2048]{1,0:T(8,128)(2,1)}, bf16[4,288,1024]{2,1,0:T(8,128)(2,1)}, bf16[4,288,1024]{2,1,0:T(8,128)(2,1)}, bf16[4,288,1024]{2,1,0:T(8,128)(2,1)}) custom-call(s32[1]{0:T(128)} %bitcast.16.high_ref, bf16[4096,2048]{1,0:T(8,128)(2,1)} %bitcast.280, bf16[4096,2048]{1,0:T(8,128)(2,1)} %bitcast.333, ...), custom_call_target="tpu_custom_call" | custom-call | flops 154618822656 | bytes 33554432 | tf_op jit(solution)/shard_map/feed_forward/pallas_call | solution.py:613
  428.1 72.2 %sum_mlp.1 = (f32[128,2048]{1,0:T(8,128)}, f32[128,2048]{1,0:T(8,128)}) custom-call(bf16[16,128,2048]{2,1,0:T(8,128)(2,1)} %bitcast.285, bf16[16,128,2048]{2,1,0:T(8,128)(2,1)} %bitcast.286), custom_call_target="tpu_custom_call" | custom-call | tf_op jit(solution)/shard_map/sum_mlp/pallas_call | solution.py:437
  501.9 2.3 fusion.115.refs_0_
  504.3 79.9 %gather_back.1 = (bf16[4,128,2048]{2,1,0:T(8,128)(2,1)}, bf16[4,288,1024]{2,1,0:T(8,128)(2,1)}, bf16[4,288,1024]{2,1,0:T(8,128)(2,1)}, bf16[4,288,1024]{2,1,0:T(8,128)(2,1)}) custom-call(bf16[128,2048]{1,0:T(8,128)(2,1)} %fusion.115.refs_0_, bf16[4,288,1024]{2,1,0:T(8,128)(2,1)} %get-tuple-element.64.refs_1_, ...), custom_call_target="tpu_custom_call" | custom-call | tf_op jit(solution)/shard_map/gather_back/pallas_call | solution.py:437
  584.2 3.7 convolution_convert_fusion.3
  587.9 2.0 reshape.407
  589.9 4.5 fusion.3
  597.9 2.5 pad_maximum_fusion.refs_1_
  604.2 2.6 convolution_convert_fusion
  606.9 47.6 %sum_back.1 = (f32[128,2048]{1,0:T(8,128)}, f32[128,512]{1,0:T(8,128)}) custom-call(bf16[4,128,2048]{2,1,0:T(8,128)(2,1)} %bitcast.295, bf16[32,128,512]{2,1,0:T(8,128)(2,1)} %pad_maximum_fusion.refs_1_), custom_call_target="tpu_custom_call" | custom-call | tf_op jit(solution)/shard_map/sum_back/pallas_call | solution.py:437
  655.7 1.7 convolution_add_fusion.3
  657.5 3.0 fusion.60
  662.1 7.0 gather_kv.1
  669.1 2.8 fusion.53
  671.9 2.8 fusion.52
  674.7 2.2 reshape.428
  676.9 3.9 copy.83
  680.8 4.4 convert_dynamic-update-slice_fusion.1
  687.0 3.9 copy.84
  690.9 2.2 reshape.429
  693.1 4.4 convert_dynamic-update-slice_fusion
  699.5 1.9 dynamic-slice_bitcast_fusion
  701.4 2.0 copy.85
  703.5 2.5 fusion.30
  707.2 66.1 %sum_weights.1 = f32[656,512]{1,0:T(8,128)} custom-call(bf16[8,656,512]{2,1,0:T(8,128)(2,1)} %pad_dynamic-update-slice_fusion.refs_0_), custom_call_target="tpu_custom_call" | custom-call | tf_op jit(solution)/shard_map/sum_weights/pallas_call | solution.py:437
  773.3 2.1 slice_bitcast_fusion.17
  776.7 2.2 copy-done.1
  779.2 2.9 copy.82
  782.1 4.7 convert_element_type.260
  786.8 2.5 fusion.46
  789.9 2.2 copy-done.2
  792.4 2.9 copy.81
  795.3 4.5 convert_element_type.258
  799.8 3.1 fusion.49
  803.0 2.0 convolution_convert_fusion.8
  805.5 2.2 copy-done.5
  807.8 2.3 slice.214
  810.1 5.4 copy.90
  815.4 3.8 fusion.35
  823.4 1.8 fusion.63.refs_0_
  825.2 9.2 %sum_small.1 = f32[336,256]{1,0:T(8,128)} custom-call(bf16[4,336,256]{2,1,0:T(8,128)(2,1)} %fusion.63.refs_0_), custom_call_target="tpu_custom_call" | custom-call | tf_op jit(solution)/shard_map/sum_small/pallas_call | solution.py:437
  837.6 19.6 %finish.1 = (f32[208,256]{1,0:T(8,128)}, f32[8,16,256]{2,1,0:T(8,128)}) custom-call(f32[208,256]{1,0:T(8,128)} %slice.180.refs_0_, f32[8,16,256]{2,1,0:T(8,128)} %bitcast.318), custom_call_target="tpu_custom_call" | custom-call | tf_op jit(solution)/shard_map/finish/pallas_call | solution.py:437
  861.6 2.0 copy.99
  869.7 3.6 fusion.65
  873.4 4.8 slice.209
  878.2 5.4 copy.94
  883.5 5.6 copy.100
  889.1 4.8 slice.210
  893.9 5.4 copy.95
  899.3 5.6 copy.101
  (227 shorter events, 66.0 us)
Async XLA Ops:
  0.7 255.5 %copy-start = (bf16[256,4096]{1,0:T(8,128)(2,1)S(1)}, bf16[256,4096]{1,0:T(8,128)(2,1)}, u32[]{:S(2)}) copy-start(bf16[256,4096]{1,0:T(8,128)(2,1)} %param.51) | copy-start | bytes 6291460
  0.7 7.5 copy-start.45
  0.7 7.5 copy-start.34
  0.7 7.5 copy-start.35
  1.2 6.9 copy-start.68
  4.6 4.1 copy-start.14
  6.8 1.3 copy-start.12
  6.8 2.8 copy-start.74
  8.2 122.7 %copy-start.42 = (f32[128,128]{1,0:T(8,128)}, f32[128,128]{1,0:T(8,128)S(1)}, u32[]{:S(2)}) copy-start(f32[128,128]{1,0:T(8,128)S(1)} %get-tuple-element.160) | copy-start | bytes 196612
  8.6 120.9 %copy-start.10 = (bf16[2048,256]{1,0:T(8,128)(2,1)}, bf16[2048,256]{1,0:T(8,128)(2,1)S(1)}, u32[]{:S(2)}) copy-start(bf16[2048,256]{1,0:T(8,128)(2,1)S(1)} %fusion.8) | copy-start | bytes 3145732
  8.7 118.0 %copy-start.38 = (bf16[256,512]{1,0:T(8,128)(2,1)S(1)}, bf16[256,512]{1,0:T(8,128)(2,1)}, u32[]{:S(2)}) copy-start(bf16[256,512]{1,0:T(8,128)(2,1)} %param.41) | copy-start | bytes 786436
  126.7 2.8 copy-start.20
  129.5 1.5 copy-start.26
  129.5 1.5 copy-start.15
  129.6 3.3 copy-start.72
  131.0 2.6 copy-start.51
  131.0 2.6 copy-start.53
  133.6 2.0 copy-start.6
  134.6 3.3 copy-start.61
  135.6 3.7 copy-start.40
  139.3 5.4 copy-start.18
  142.1 2.6 copy-start.29
  142.1 20.6 %copy-start.8 = (bf16[1,1,128,2048]{3,2,1,0:T(8,128)(2,1)S(1)}, bf16[1,1,128,2048]{3,2,1,0:T(8,128)(2,1)}, u32[]{:S(2)}) copy-start(bf16[1,1,128,2048]{3,2,1,0:T(8,128)(2,1)} %param.28) | copy-start | bytes 1572868
  144.7 20.5 %copy-start.58 = (f32[2048]{0:T(1024)S(1)}, f32[2048]{0:T(1024)}, u32[]{:S(2)}) copy-start(f32[2048]{0:T(1024)} %param.32) | copy-start | bytes 24580
  247.1 2.5 copy-start.25
  250.5 5.7 copy-start.49
  256.1 5.6 copy-start.50
  428.0 72.3 %copy-start.4 = (f32[128,2048]{1,0:T(8,128)S(1)}, f32[128,2048]{1,0:T(8,128)}, u32[]{:S(2)}) copy-start(f32[128,2048]{1,0:T(8,128)} %copy-done.3) | copy-start | bytes 3145732
  428.0 72.3 %copy-start.59 = (f32[2048]{0:T(1024)S(1)}, f32[2048]{0:T(1024)}, u32[]{:S(2)}) copy-start(f32[2048]{0:T(1024)} %param.32) | copy-start | bytes 24580
  428.1 72.3 %copy-start.64 = (f32[128]{0:T(128)S(1)}, f32[128]{0:T(128)}, u32[]{:S(2)}) copy-start(f32[128]{0:T(128)} %copy-done.63) | copy-start | bytes 1540
  428.1 73.8 %copy-start.17 = (bf16[1,1,128,2048]{3,2,1,0:T(8,128)(2,1)S(1)}, bf16[1,1,128,2048]{3,2,1,0:T(8,128)(2,1)}, u32[]{:S(2)}) copy-start(bf16[1,1,128,2048]{3,2,1,0:T(8,128)(2,1)} %param.30) | copy-start | bytes 1572868
  501.9 82.3 %copy-start.67 = (f32[128]{0:T(128)}, f32[128]{0:T(128)S(1)}, u32[]{:S(2)}) copy-start(f32[128]{0:T(128)S(1)} %broadcast_multiply_fusion.1) | copy-start | bytes 1540
  504.3 79.9 %copy-start.30 = (bf16[512,2048]{1,0:T(8,128)(2,1)S(1)}, bf16[512,2048]{1,0:T(8,128)(2,1)}, u32[]{:S(2)}) copy-start(bf16[512,2048]{1,0:T(8,128)(2,1)} %copy-done.29) | copy-start | bytes 6291460
  584.2 5.6 copy-start.62
  589.9 4.5 copy-start.7
  589.9 4.5 copy-start.16
  594.4 1.3 copy-start.52
  597.9 3.7 copy-start.73
  601.6 2.6 copy-start.27
  606.8 47.7 %copy-start.69 = (f32[128]{0:T(128)S(1)}, f32[128]{0:T(128)}, u32[]{:S(2)}) copy-start(f32[128]{0:T(128)} %copy-done.68) | copy-start | bytes 1540
  606.8 47.7 %copy-start.71 = (f32[128]{0:T(128)S(1)}, f32[128]{0:T(128)}, u32[]{:S(2)}) copy-start(f32[128]{0:T(128)} %copy-done.70) | copy-start | bytes 1540
  606.8 48.9 %copy-start.13 = (bf16[2048,256]{1,0:T(8,128)(2,1)S(1)}, bf16[2048,256]{1,0:T(8,128)(2,1)}, u32[]{:S(2)}) copy-start(bf16[2048,256]{1,0:T(8,128)(2,1)} %copy-done.12) | copy-start | bytes 3145732
  606.8 50.6 %copy-start.9 = (bf16[1,1,128,2048]{3,2,1,0:T(8,128)(2,1)S(1)}, bf16[1,1,128,2048]{3,2,1,0:T(8,128)(2,1)}, u32[]{:S(2)}) copy-start(bf16[1,1,128,2048]{3,2,1,0:T(8,128)(2,1)} %param.28) | copy-start | bytes 1572868
  606.8 50.6 %copy-start.11 = (bf16[2048,256]{1,0:T(8,128)(2,1)S(1)}, bf16[2048,256]{1,0:T(8,128)(2,1)}, u32[]{:S(2)}) copy-start(bf16[2048,256]{1,0:T(8,128)(2,1)} %copy-done.10) | copy-start | bytes 3145732
  606.8 50.6 %copy-start.60 = (f32[2048]{0:T(1024)S(1)}, f32[2048]{0:T(1024)}, u32[]{:S(2)}) copy-start(f32[2048]{0:T(1024)} %param.31) | copy-start | bytes 24580
  606.8 50.6 %copy-start.66 = (f32[128]{0:T(128)S(1)}, f32[128]{0:T(128)}, u32[]{:S(2)}) copy-start(f32[128]{0:T(128)} %copy-done.65) | copy-start | bytes 1540
  680.8 4.4 copy-start.21
  680.8 4.4 copy-start.36
  680.8 5.2 copy-start.33
  693.1 4.4 copy-start.28
  693.1 4.4 copy-start.37
  707.2 68.2 %copy-start.39 = (bf16[256,512]{1,0:T(8,128)(2,1)S(1)}, bf16[256,512]{1,0:T(8,128)(2,1)}, u32[]{:S(2)}) copy-start(bf16[256,512]{1,0:T(8,128)(2,1)} %param.41) | copy-start | bytes 786436
  707.2 68.9 %copy-start.24 = (bf16[4,288,1024]{2,1,0:T(8,128)(2,1)S(1)}, bf16[4,288,1024]{2,1,0:T(8,128)(2,1)}, u32[]{:S(2)}) copy-start(bf16[4,288,1024]{2,1,0:T(8,128)(2,1)} %get-tuple-element.71) | copy-start | bytes 7077892
  776.7 2.2 copy-start.1
  786.8 2.5 copy-start.23
  789.9 2.2 copy-start.2
  799.8 3.2 copy-start.41
  799.8 5.2 copy-start.22
  805.5 2.2 copy-start.5
  815.4 3.8 copy-start.48
  825.2 39.4 %copy-start.44 = (bf16[256,256]{1,0:T(8,128)(2,1)S(1)}, bf16[256,256]{1,0:T(8,128)(2,1)}, u32[]{:S(2)}) copy-start(bf16[256,256]{1,0:T(8,128)(2,1)} %param.43) | copy-start | bytes 393220
  825.2 40.2 %copy-start.46 = (bf16[256,256]{1,0:T(8,128)(2,1)S(1)}, bf16[256,256]{1,0:T(8,128)(2,1)}, u32[]{:S(2)}) copy-start(bf16[256,256]{1,0:T(8,128)(2,1)} %param.45) | copy-start | bytes 393220
  864.6 13.6 %copy-start.55 = (f32[64,256]{1,0:T(8,128)}, f32[64,256]{1,0:T(8,128)S(1)}, u32[]{:S(2)}) copy-start(f32[64,256]{1,0:T(8,128)S(1)} %get-tuple-element.137) | copy-start | bytes 196612
  864.6 13.6 %copy-start.56 = (f32[64,256]{1,0:T(8,128)}, f32[64,256]{1,0:T(8,128)S(1)}, u32[]{:S(2)}) copy-start(f32[64,256]{1,0:T(8,128)S(1)} %get-tuple-element.138) | copy-start | bytes 196612
  (11 other events, 10.4 us)

commit v2 on v1

--- a/solution.py
+++ b/solution.py
@@ -90,11 +90,13 @@
 
 
 class Gather:
-    def __init__(self, topo, group, x, parts):
-        self.topo, self.group, self.parts = topo, group, parts
+    def __init__(self, topo, group, x, parts, beyond=None, need=None):
+        self.topo, self.group, self.parts, self.beyond = topo, group, parts, beyond
+        self.slots = "half" if beyond else group
+        self.need = need or (lambda dims, key: 0)
         self.inputs = [x]
         rows, cols = x.shape
-        self.outputs = [jax.ShapeDtypeStruct((topo.group_size(group), rows, cols), x.dtype)]
+        self.outputs = [jax.ShapeDtypeStruct((topo.group_size(self.slots), rows, cols), x.dtype)]
         self.out_specs = [pl.BlockSpec(memory_space=pl.ANY)]
         self.in_specs = [pl.BlockSpec(memory_space=pl.ANY)]
         n = topo.group_size(group)
@@ -109,13 +111,29 @@
             ((dim, d),) for dim in GROUP_DIMS[self.group] for d in range(1, self.topo.size[dim])
         }
 
+    def work(self):
+        work = []
+        for part, (row, rows, order) in enumerate(self.parts):
+            for key in itertools.product(*[range(self.topo.size[dim]) for dim in order]):
+                if not any(key) or self.keeps(order, key):
+                    hops = sum(1 for o in key if o)
+                    last = max([i for i, o in enumerate(key) if o], default=-1)
+                    work.append((self.need(order, key), hops, last, part, key))
+        work.sort()
+        return [(w[3], w[4]) for w in work]
+
+    def keeps(self, order, key):
+        return not self.beyond or key[order.index(self.beyond)] != 0
+
     def run(self, ins, outs, scratch):
         topo = self.topo
         (x_ref,), (out_ref,) = ins, outs
         send_sem, recv_sem, own_sem = scratch
         at = topo.here()
-        own = pltpu.make_async_copy(x_ref, out_ref.at[topo.index(at, self.group)], own_sem)
-        own.start()
+        own = None
+        if not self.beyond:
+            own = pltpu.make_async_copy(x_ref, out_ref.at[topo.index(at, self.slots)], own_sem)
+            own.start()
         started = []
 
         def key_index(order, key):
@@ -126,7 +144,7 @@
 
         def copy(part, order, row, rows, key, stage, d):
             origin = topo.moved(at, order, key, -1)
-            slot = topo.index(origin, self.group)
+            slot = topo.index(origin, self.slots)
             new_key = tuple(d if i == stage else o for i, o in enumerate(key))
             src = (
                 x_ref.at[pl.ds(row, rows)]
@@ -143,30 +161,29 @@
                 target,
             )
 
-        work = []
-        for part, (row, rows, order) in enumerate(self.parts):
-            sizes = [topo.size[dim] for dim in order]
-            keys = list(itertools.product(*[range(s) for s in sizes]))
-            last = {k: max([i for i, o in enumerate(k) if o], default=-1) for k in keys}
-            hops = {k: sum(1 for o in k if o) for k in keys}
-            for k in keys:
-                work.append((hops[k], last[k], part, row, rows, order, k))
-        work.sort(key=lambda w: (w[0], w[1], w[2]))
-        for hops, last, part, row, rows, order, key in work:
-            if hops:
-                slot = topo.index(topo.moved(at, order, key, -1), self.group)
+        for part, key in self.work():
+            row, rows, order = self.parts[part]
+            if any(key):
+                slot = topo.index(topo.moved(at, order, key, -1), self.slots)
                 k = key_index(order, key)
                 dst = out_ref.at[slot, pl.ds(row, rows)]
                 remote(dst, dst, send_sem.at[part, k], recv_sem.at[part, k], topo.device(at)).wait_recv()
+            last = max([i for i, o in enumerate(key) if o], default=-1)
+            sends = []
             for stage in range(last + 1, len(order)):
                 for d in range(1, topo.size[order[stage]]):
-                    cp = copy(part, order, row, rows, key, stage, d)
-                    cp.start()
-                    started.append(cp)
+                    new_key = tuple(d if i == stage else o for i, o in enumerate(key))
+                    if self.keeps(order, new_key):
+                        sends.append((self.need(order, new_key), stage, d))
+            for _, stage, d in sorted(sends):
+                cp = copy(part, order, row, rows, key, stage, d)
+                cp.start()
+                started.append(cp)
             yield
         for cp in started:
             cp.wait_send()
-        own.wait()
+        if own is not None:
+            own.wait()
 
 
 class Scatter:
@@ -285,6 +302,148 @@
             cp.wait_send()
 
 
+class SlimScatter:
+    def __init__(self, topo, group, shape, dtype, parts):
+        self.topo, self.group, self.parts = topo, group, parts
+        n, rows, cols = shape
+        self.dtype = dtype
+        self.outputs = [jax.ShapeDtypeStruct((rows, cols), F32)]
+        self.out_specs = [pl.BlockSpec(memory_space=pltpu.VMEM)]
+        self.scratch = []
+        terms = 1 + sum(topo.size[d] - 1 for d in GROUP_DIMS[group])
+        most = max(p[1] for p in parts)
+        self.terms, self.most, self.cols = terms, most, cols
+        for row, nrows, order in parts:
+            sizes = [topo.size[dim] for dim in order]
+            for k, s in enumerate(sizes):
+                rest = math.prod(sizes[k + 1 :])
+                m = max(s - 1, 1)
+                self.outputs.append(jax.ShapeDtypeStruct((m, rest, nrows, cols), dtype))
+                self.out_specs.append(pl.BlockSpec(memory_space=pl.ANY))
+                self.scratch.append(pltpu.SemaphoreType.DMA((m, rest)))
+                self.scratch.append(pltpu.SemaphoreType.DMA((m, rest)))
+
+    RING = 4
+
+    def shared_scratch(self):
+        return [
+            pltpu.VMEM((2, self.terms, self.most, self.cols), self.dtype),
+            pltpu.SemaphoreType.DMA((2, self.terms)),
+            pltpu.VMEM((self.RING, self.most, self.cols), self.dtype),
+        ]
+
+    def peers(self):
+        return {
+            ((dim, d),) for dim in GROUP_DIMS[self.group] for d in range(1, self.topo.size[dim])
+        }
+
+    def run(self, x_ref, outs, scratch, shared):
+        topo = self.topo
+        outs, scratch = list(outs), list(scratch)
+        out_ref = outs.pop(0)
+        stage_buf, stage_sem, ring = shared
+        at = topo.here()
+        jobs, started = [], []
+        for part, (row, nrows, order) in enumerate(self.parts):
+            sizes = [topo.size[dim] for dim in order]
+            bufs = [(outs.pop(0), scratch.pop(0), scratch.pop(0)) for _ in sizes]
+            keys = list(itertools.product(*[range(s) for s in sizes]))
+            first = {k: min([i for i, o in enumerate(k) if o], default=len(sizes)) for k in keys}
+            keys.sort(key=lambda k: (first[k], [0 if o else 1 for o in k]))
+            for rank, key in enumerate(keys):
+                jobs.append((first[key], rank, part, row, nrows, order, sizes, bufs, key))
+        jobs.sort(key=lambda j: (j[0], j[1], j[2]))
+
+        def flat(key, start, sizes):
+            k = 0
+            for o, s in zip(key[start:], sizes[start:]):
+                k = k * s + o
+            return k
+
+        def out_copy(job, src):
+            stage, _, part, row, nrows, order, sizes, bufs, key = job
+            buf, send_sem, recv_sem = bufs[stage]
+            d, k = key[stage], flat(key, stage + 1, sizes)
+            target = topo.device(topo.moved(at, [order[stage]], [d]))
+            return remote(src, buf.at[d - 1, k], send_sem.at[d - 1, k], recv_sem.at[d - 1, k], target)
+
+        def block(job):
+            _, _, part, row, nrows, order, sizes, bufs, key = job
+            return x_ref.at[topo.index(topo.moved(at, order, key), self.group), pl.ds(row, nrows)]
+
+        for job in jobs:
+            if job[0] == 0:
+                cp = out_copy(job, block(job))
+                cp.start()
+                started.append(cp)
+        yield
+        jobs = [job for job in jobs if job[0] > 0]
+
+        def loads(job, slot, arrived):
+            first, _, part, row, nrows, order, sizes, bufs, key = job
+            copies = []
+            i = 0
+            sources = [block(job)]
+            for stage in range(first):
+                buf, send_sem, recv_sem = bufs[stage]
+                k = flat(key, stage + 1, sizes)
+                for d in range(1, sizes[stage]):
+                    ref = buf.at[d - 1, k]
+                    if not arrived:
+                        remote(ref, ref, send_sem.at[d - 1, k], recv_sem.at[d - 1, k], topo.device(at)).wait_recv()
+                    sources.append(ref)
+            for i, ref in enumerate(sources):
+                copies.append(
+                    pltpu.make_async_copy(ref, stage_buf.at[slot, i, pl.ds(0, nrows)], stage_sem.at[slot, i])
+                )
+            return copies
+
+        in_ring = [None] * self.RING
+        sent = 0
+        for cp in loads(jobs[0], 0, False):
+            cp.start()
+        yield
+        for n, job in enumerate(jobs):
+            first, _, part, row, nrows, order, sizes, bufs, key = job
+            slot = n % 2
+            copies = loads(job, slot, True)
+            for cp in copies:
+                cp.wait()
+            final = first == len(sizes)
+            if not final:
+                place = sent % self.RING
+                if in_ring[place] is not None:
+                    in_ring[place].wait_send()
+            step = 16 if nrows % 16 == 0 else 8
+
+            def add(r, _, slot=slot, count=len(copies), final=final, row=row, step=step):
+                r0 = pl.multiple_of(r * step, step)
+                total = stage_buf[slot, 0, pl.ds(r0, step), :].astype(F32)
+                for i in range(1, count):
+                    total = total + stage_buf[slot, i, pl.ds(r0, step), :].astype(F32)
+                if final:
+                    out_ref[pl.ds(row + r0, step), :] = total
+                else:
+                    ring[place, pl.ds(r0, step), :] = total.astype(ring.dtype)
+                return 0
+
+            lax.fori_loop(0, nrows // step, add, 0)
+            if not final:
+                cp = out_copy(job, ring.at[place, pl.ds(0, nrows)])
+                cp.start()
+                in_ring[place] = cp
+                sent += 1
+            if n + 1 < len(jobs):
+                for cp in loads(jobs[n + 1], 1 - slot, False):
+                    cp.start()
+            yield
+        for cp in started:
+            cp.wait_send()
+        for cp in in_ring:
+            if cp is not None:
+                cp.wait_send()
+
+
 class Exchange:
     def __init__(self, topo, group, x):
         self.topo, self.group = topo, group
@@ -519,126 +678,314 @@
     return v * half_up, slope
 
 
-def feed_forward(topo, normed_all, grad_all, w_gate, w_up, w_down, low_gu, low_d, high):
-    tokens, width = normed_all.shape
-    units = w_gate.shape[1]
-    ranks = low_d.shape[0]
+def feed_forward(
+    topo, collective_id, normed, grads, grads_half,
+    w_gate, w_up, w_down, gate_adapt, gate_expand, up_adapt, up_expand, down_adapt, down_expand,
+):
+    rows, width = normed.shape
     quad = topo.group_size("quad")
+    half = topo.group_size("half")
+    units = w_gate.shape[1] // quad
+    rank = gate_adapt.shape[1]
+    ranks = rank // 2
     half_width = width // 2
     d_rows, r_rows = half_width // quad, ranks // quad
+    per_chunk = 512 // rows
     tile = 512
-    run = (topo.n_seq // 2) * 128 // tile
-    own = tokens // tile // 2
     block = 256
 
-    def chunk(t, high_ref):
-        mine = t < own
-        k = jnp.where(mine, t, t - own)
-        side = jnp.where(mine, high_ref[0], 1 - high_ref[0])
-        return lax.div(k, run) * 2 * run + side * run + lax.rem(k, run)
-
-    def kernel(
-        high_ref, n_ref, g_ref, wg_ref, wu_ref, wd_ref, lgu_ref, ld_ref,
-        down_ref, gn_ref, dg_ref, du_ref, dd_ref,
-        acc_g, acc_u, acc_d, mix_s, gg_s, gu_s,
-    ):
-        t = pl.program_id(0)
-
-        @pl.when(t == 0)
-        def _():
-            acc_g[...] = jnp.zeros_like(acc_g)
-            acc_u[...] = jnp.zeros_like(acc_u)
-            acc_d[...] = jnp.zeros_like(acc_d)
-
-        low = matmul(n_ref[...], lgu_ref[...])
-        low_g = low[:, :ranks].astype(BF16)
-        low_u = low[:, ranks:].astype(BF16)
-        low_b = dot_t(g_ref[...], ld_ref[...]).astype(BF16)
-
-        def one(i, _):
-            cols = pl.ds(pl.multiple_of(i * block, block), block)
-            gate = matmul(n_ref[...], wg_ref[:, cols])
-            up = matmul(n_ref[...], wu_ref[:, cols])
-            act, slope = gelu_parts(gate)
-            gm = dot_t(g_ref[...], wd_ref[cols, :])
-            mix_s[:, cols] = (act * up).astype(BF16)
-            gg_s[:, cols] = (gm * up * slope).astype(BF16)
-            gu_s[:, cols] = (gm * act).astype(BF16)
-            return 0
-
-        lax.fori_loop(0, units // block, one, 0)
-
-        @pl.when(t < own)
-        def _():
-            def two(i, _):
+    dims = "hxclb"
+    keys = list(itertools.product(*[range(topo.size[d]) for d in dims]))
+    chunks = [keys[i : i + per_chunk] for i in range(0, len(keys), per_chunk)]
+    own = len(chunks) // 2
+    chunk_of = {key: i for i, keys_of in enumerate(chunks) for key in keys_of}
+
+    def need(order, key):
+        at_dim = dict(zip(order, key))
+        return chunk_of[tuple(at_dim[d] for d in dims)]
+
+    gather_n = Gather(topo, "all", normed, row_parts(rows, ("lhbxc", "xlhbc"), (7, 4)), need=need)
+    gather_g = Gather(
+        topo, "all", grads, row_parts(rows, ("hxlbc", "hlbxc", "hbxlc"), (1, 1, 1)), beyond="h", need=need
+    )
+    thirds = row_parts(rows, ("cxbl", "cblx", "clxb"), (1, 1, 1))
+    sum_n = SlimScatter(topo, "half", (half, rows, width), BF16, thirds)
+    sum_d = SlimScatter(topo, "half", (half, rows, width), BF16, thirds)
+    comm = [gather_n, gather_g, sum_n, sum_d]
+
+    inputs = [
+        normed, grads, grads_half, w_gate, w_up, w_down,
+        gate_adapt, gate_expand, up_adapt, up_expand, down_adapt, down_expand,
+    ]
+    part = jax.ShapeDtypeStruct((half, rows, width), BF16)
+    grad = jax.ShapeDtypeStruct((quad, d_rows + r_rows, units), BF16)
+    any_spec = pl.BlockSpec(memory_space=pl.ANY)
+    out_shape = [part, part, grad, grad, grad]
+    out_specs = [any_spec] * 5
+    scratch = [
+        pltpu.VMEM((width, units), BF16), pltpu.VMEM((width, units), BF16), pltpu.VMEM((units, width), BF16),
+        pltpu.VMEM((width, rank), BF16), pltpu.VMEM((rank, units), BF16),
+        pltpu.VMEM((width, rank), BF16), pltpu.VMEM((rank, units), BF16),
+        pltpu.VMEM((units, rank), BF16), pltpu.VMEM((rank, width), BF16),
+        pltpu.VMEM((half_width + ranks, units), F32),
+        pltpu.VMEM((half_width + ranks, units), F32),
+        pltpu.VMEM((half_width + ranks, units), F32),
+        pltpu.VMEM((3, tile, units), BF16),
+        pltpu.VMEM((2, tile, width), BF16), pltpu.VMEM((2, tile, width), BF16),
+        pltpu.VMEM((tile, width), BF16), pltpu.VMEM((tile, width), BF16),
+        pltpu.SemaphoreType.DMA((9,)),
+        pltpu.SemaphoreType.DMA((2, 2, per_chunk)),
+        pltpu.SemaphoreType.DMA((2, per_chunk)),
+        pltpu.SemaphoreType.DMA((3,)),
+    ]
+    n_own = len(scratch)
+    shared = sum_n.shared_scratch()
+    scratch = scratch + shared
+    for op in comm:
+        out_shape = out_shape + op.outputs
+        out_specs = out_specs + op.out_specs
+        scratch = scratch + op.scratch
+
+    def kernel(*refs):
+        refs = list(refs)
+        (
+            n_hbm, g_hbm, g_half, wg_hbm, wu_hbm, wd_hbm, ga_hbm, ge_hbm, ua_hbm, ue_hbm, da_hbm, de_hbm,
+        ) = [refs.pop(0) for _ in inputs]
+        down_part, gn_part, dg_out, du_out, dd_out = [refs.pop(0) for _ in range(5)]
+        op_outs = [[refs.pop(0) for _ in op.outputs] for op in comm]
+        (
+            wg, wu, wd, ga, ge, ua, ue, da, de, acc_g, acc_u, acc_d, acts, n_buf, g_buf, down_st, gn_st,
+            w_sem, load_sem, store_sem, grad_sem,
+        ) = [refs.pop(0) for _ in range(n_own)]
+        shared_refs = [refs.pop(0) for _ in shared]
+        op_scratch = [[refs.pop(0) for _ in op.scratch] for op in comm]
+        mix_s, gg_s, gu_s = acts.at[0], acts.at[1], acts.at[2]
+        at = topo.here()
+        high = at["h"]
+        member = topo.index(at, "quad")
+        unit_at = pl.multiple_of(member * units, units)
+
+        w_copies = [
+            pltpu.make_async_copy(src, dst, w_sem.at[i])
+            for i, (src, dst) in enumerate(
+                (
+                    (de_hbm, de),
+                    (da_hbm.at[pl.ds(unit_at, units), :], da),
+                    (wd_hbm.at[pl.ds(unit_at, units), :], wd),
+                    (ga_hbm, ga),
+                    (ge_hbm.at[:, pl.ds(unit_at, units)], ge),
+                    (wg_hbm.at[:, pl.ds(unit_at, units)], wg),
+                    (ua_hbm, ua),
+                    (ue_hbm.at[:, pl.ds(unit_at, units)], ue),
+                    (wu_hbm.at[:, pl.ds(unit_at, units)], wu),
+                )
+            )
+        ]
+        for cp in w_copies:
+            cp.start()
+
+        peers = sorted(set().union(*[op.peers() for op in comm]))
+        barrier = pltpu.get_barrier_semaphore()
+        for peer in peers:
+            there = topo.device(topo.moved(at, [p[0] for p in peer], [p[1] for p in peer]))
+            pl.semaphore_signal(barrier, inc=1, device_id=there, device_id_type=MESH)
+        pl.semaphore_wait(barrier, len(peers))
+
+        steps_n = gather_n.run([n_hbm], op_outs[0], op_scratch[0])
+        steps_g = gather_g.run([g_hbm], op_outs[1], op_scratch[1])
+        order_n = [need(gather_n.parts[p][2], k) for p, k in gather_n.work()]
+        order_g = [need(gather_g.parts[p][2], k) if any(k) else own for p, k in gather_g.work()]
+        arrivals = sorted(
+            [(c, i / len(order_n), 0) for i, c in enumerate(order_n)]
+            + [(c, i / len(order_g), 1) for i, c in enumerate(order_g)],
+            key=lambda w: w[0],
+        )
+        first_g = [w for w in arrivals if w[2] == 1][:len(gather_g.parts)]
+        for w in first_g:
+            arrivals.remove(w)
+        per_part = len(gather_n.parts)
+        arrivals = arrivals[:per_part] + first_g + arrivals[per_part:]
+        done = [0]
+
+        def advance(count=None, upto=None):
+            while done[0] < len(arrivals):
+                if count is not None:
+                    if count == 0:
+                        return
+                    count -= 1
+                elif not any(w[0] <= upto for w in arrivals[done[0]:]):
+                    return
+                next((steps_n, steps_g)[arrivals[done[0]][2]], None)
+                done[0] += 1
+
+        acc_g[...] = jnp.zeros_like(acc_g)
+        acc_u[...] = jnp.zeros_like(acc_u)
+        acc_d[...] = jnp.zeros_like(acc_d)
+        advance(count=per_part + len(first_g))
+
+        def merge_rows(weight, adapt, expand, total):
+            def one(i, _):
+                r = pl.ds(pl.multiple_of(i * block, block), block)
+                weight[r, :] = (weight[r, :].astype(F32) + matmul(adapt[r, :], expand[...])).astype(BF16)
+                return 0
+
+            lax.fori_loop(0, total // block, one, 0)
+
+        for cp in w_copies[:3]:
+            cp.wait()
+        merge_rows(wd, da, de, units)
+        for cp in w_copies[3:6]:
+            cp.wait()
+        merge_rows(wg, ga, ge, width)
+        for cp in w_copies[6:]:
+            cp.wait()
+        merge_rows(wu, ua, ue, width)
+
+        def chunk_copies(c, slot):
+            copies = []
+            for i, key in enumerate(chunks[c]):
+                origin = topo.moved(at, dims, key, -1)
+                r = pl.ds(i * rows, rows)
+                in_half = topo.index(origin, "half")
+                g_src = g_half if key[0] == 0 else op_outs[1][0]
+                n_src = op_outs[0][0].at[topo.index(origin, "all")] if any(key) else n_hbm
+                copies.append(pltpu.make_async_copy(n_src, n_buf.at[slot, r], load_sem.at[slot, 0, i]))
+                copies.append(
+                    pltpu.make_async_copy(g_src.at[in_half], g_buf.at[slot, r], load_sem.at[slot, 1, i])
+                )
+            return copies
+
+        def store_copies(c):
+            copies = []
+            for i, key in enumerate(chunks[c]):
+                slot = topo.index(topo.moved(at, dims, key, -1), "half")
+                r = pl.ds(i * rows, rows)
+                copies.append(pltpu.make_async_copy(down_st.at[r], down_part.at[slot], store_sem.at[0, i]))
+                copies.append(pltpu.make_async_copy(gn_st.at[r], gn_part.at[slot], store_sem.at[1, i]))
+            return copies
+
+        sums = []
+
+        def sum_steps(count):
+            for _ in range(count):
+                if not sums:
+                    return
+                try:
+                    next(sums[0])
+                except StopIteration:
+                    sums.pop(0)
+
+        advance(upto=0)
+        for cp in chunk_copies(0, 0):
+            cp.start()
+        low_cols = pl.ds(pl.multiple_of(high * ranks, ranks), ranks)
+        half_at = high * half_width
+
+        def poll(c):
+            if c < own:
+                advance(count=POLL)
+            else:
+                sum_steps(SUM_POLL)
+
+        for c in range(len(chunks)):
+            slot = c % 2
+            nb, gb = n_buf.at[slot], g_buf.at[slot]
+            for cp in chunk_copies(c, slot):
+                cp.wait()
+            low_g = matmul(nb[...], ga[:, low_cols]).astype(BF16)
+            low_u = matmul(nb[...], ua[:, low_cols]).astype(BF16)
+            low_b = dot_t(gb[...], de[low_cols, :]).astype(BF16)
+
+            def one(i, _, nb=nb, gb=gb):
                 cols = pl.ds(pl.multiple_of(i * block, block), block)
-                down_ref[:, cols] = matmul(mix_s[...], wd_ref[:, cols]).astype(BF16)
-                gn_ref[:, cols] = (
-                    dot_t(gg_s[...], wg_ref[cols, :]) + dot_t(gu_s[...], wu_ref[cols, :])
-                ).astype(BF16)
+                gate = matmul(nb[...], wg[:, cols])
+                up = matmul(nb[...], wu[:, cols])
+                act, slope = gelu_parts(gate)
+                gm = dot_t(gb[...], wd[cols, :])
+                mix_s[:, cols] = (act * up).astype(BF16)
+                gg_s[:, cols] = (gm * up * slope).astype(BF16)
+                gu_s[:, cols] = (gm * act).astype(BF16)
                 return 0
 
-            lax.fori_loop(0, width // block, two, 0)
-
-        for acc, low_rows, grads in ((acc_g, low_g, gg_s), (acc_u, low_u, gu_s), (acc_d, low_b, mix_s)):
-            acc[half_width:, :] += t_dot(low_rows, grads[...])
-
-        def three(i, _):
-            rows = pl.ds(pl.multiple_of(i * block, block), block)
-            cols = pl.ds(pl.multiple_of(high_ref[0] * half_width + i * block, block), block)
-            acc_g[rows, :] += t_dot(n_ref[:, cols], gg_s[...])
-            acc_u[rows, :] += t_dot(n_ref[:, cols], gu_s[...])
-            acc_d[rows, :] += t_dot(g_ref[:, cols], mix_s[...])
-            return 0
-
-        lax.fori_loop(0, half_width // block, three, 0)
-
-        @pl.when(t == pl.num_programs(0) - 1)
-        def _():
-            for acc, out in ((acc_g, dg_ref), (acc_u, du_ref), (acc_d, dd_ref)):
-                for q in range(quad):
-                    out[q, :d_rows, :] = acc[q * d_rows : (q + 1) * d_rows, :].astype(BF16)
-                    out[q, d_rows:, :] = acc[
-                        half_width + q * r_rows : half_width + (q + 1) * r_rows, :
-                    ].astype(BF16)
-
-    whole = lambda t, h: (0, 0)
-    once = pl.Buffered(1)
-    grads = jax.ShapeDtypeStruct((quad, d_rows + r_rows, units), BF16)
-    grad_spec = pl.BlockSpec((quad, d_rows + r_rows, units), lambda t, h: (0, 0, 0), pipeline_mode=once)
-    part = jax.ShapeDtypeStruct((tokens // 2, width), BF16)
-    part_spec = pl.BlockSpec((tile, width), lambda t, h: (jnp.minimum(t, own - 1), 0))
-    row_spec = pl.BlockSpec((tile, width), lambda t, h: (chunk(t, h), 0))
-    flops = 2 * tokens * units * width * 9
-    return pl.pallas_call(
+            lax.fori_loop(0, units // block, one, 0)
+            poll(c)
+            if c < own:
+                if c > 0:
+                    for cp in store_copies(c - 1):
+                        cp.wait()
+
+                def two(i, _):
+                    cols = pl.ds(pl.multiple_of(i * block, block), block)
+                    down_st[:, cols] = matmul(mix_s[...], wd[:, cols]).astype(BF16)
+                    gn_st[:, cols] = (dot_t(gg_s[...], wg[cols, :]) + dot_t(gu_s[...], wu[cols, :])).astype(BF16)
+                    return 0
+
+                lax.fori_loop(0, width // block, two, 0)
+                for cp in store_copies(c):
+                    cp.start()
+            for acc, low_rows, grads_s in ((acc_g, low_g, gg_s), (acc_u, low_u, gu_s), (acc_d, low_b, mix_s)):
+                acc[half_width:, :] += t_dot(low_rows, grads_s[...])
+            if c + 1 < len(chunks):
+                advance(upto=c + 1)
+                for cp in chunk_copies(c + 1, 1 - slot):
+                    cp.start()
+
+            def three(i, _, nb=nb, gb=gb):
+                r = pl.ds(pl.multiple_of(i * block, block), block)
+                cols = pl.ds(pl.multiple_of(half_at + i * block, block), block)
+                acc_g[r, :] += t_dot(nb[:, cols], gg_s[...])
+                acc_u[r, :] += t_dot(nb[:, cols], gu_s[...])
+                acc_d[r, :] += t_dot(gb[:, cols], mix_s[...])
+                return 0
+
+            lax.fori_loop(0, half_width // block, three, 0)
+            if c == own - 1:
+                for cp in store_copies(c):
+                    cp.wait()
+                sums.append(sum_n.run(gn_part, op_outs[2], op_scratch[2], shared_refs))
+                sums.append(sum_d.run(down_part, op_outs[3], op_scratch[3], shared_refs))
+            poll(c)
+
+        pending = []
+        for q in range(quad):
+            for k, (acc, out) in enumerate(((acc_g, dg_out), (acc_u, du_out), (acc_d, dd_out))):
+                if len(pending) >= 3:
+                    pending.pop(0).wait()
+                acts[k, :d_rows, :] = acc[q * d_rows : (q + 1) * d_rows, :].astype(BF16)
+                acts[k, d_rows : d_rows + r_rows, :] = acc[
+                    half_width + q * r_rows : half_width + (q + 1) * r_rows, :
+                ].astype(BF16)
+                cp = pltpu.make_async_copy(acts.at[k, pl.ds(0, d_rows + r_rows)], out.at[q], grad_sem.at[k])
+                cp.start()
+                pending.append(cp)
+        for cp in pending:
+            cp.wait()
+        sum_steps(10000)
+        for _ in steps_n:
+            pass
+        for _ in steps_g:
+            pass
+
+    flops = 2 * rows * topo.n_dp * topo.n_seq * units * width * 9
+    results = pl.pallas_call(
         kernel,
         name="feed_forward",
-        grid_spec=pltpu.PrefetchScalarGridSpec(
-            num_scalar_prefetch=1,
-            grid=(2 * own,),
-            in_specs=[
-                row_spec,
-                row_spec,
-                pl.BlockSpec((width, units), whole, pipeline_mode=once),
-                pl.BlockSpec((width, units), whole, pipeline_mode=once),
-                pl.BlockSpec((units, width), whole, pipeline_mode=once),
-                pl.BlockSpec((width, 2 * ranks), whole, pipeline_mode=once),
-                pl.BlockSpec((ranks, width), whole, pipeline_mode=once),
-            ],
-            out_specs=[part_spec, part_spec, grad_spec, grad_spec, grad_spec],
-            scratch_shapes=[
-                pltpu.VMEM((half_width + ranks, units), F32),
-                pltpu.VMEM((half_width + ranks, units), F32),
-                pltpu.VMEM((half_width + ranks, units), F32),
-                pltpu.VMEM((tile, units), BF16),
-                pltpu.VMEM((tile, units), BF16),
-                pltpu.VMEM((tile, units), BF16),
-            ],
+        out_shape=out_shape,
+        in_specs=[any_spec] * len(inputs),
+        out_specs=out_specs,
+        scratch_shapes=scratch,
+        compiler_params=pltpu.CompilerParams(
+            collective_id=collective_id, has_side_effects=True, vmem_limit_bytes=60 << 20
         ),
-        out_shape=[part, part, grads, grads, grads],
-        compiler_params=pltpu.CompilerParams(vmem_limit_bytes=60 << 20),
-        cost_estimate=pl.CostEstimate(flops=flops, bytes_accessed=4 * tokens * width, transcendentals=0),
-    )(high, normed_all, grad_all, w_gate, w_up, w_down, low_gu, low_d)
+        cost_estimate=pl.CostEstimate(flops=flops, bytes_accessed=1 << 27, transcendentals=0),
+    )(*inputs)
+    dg, du, dd = results[2:5]
+    skip = 5 + len(gather_n.outputs) + len(gather_g.outputs)
+    return results[skip + len(sum_n.outputs)], results[skip], dg, du, dd
+
+
+POLL = 6
+SUM_POLL = 12
 
 
 def local(
@@ -658,30 +1005,14 @@
     units = w_gate.shape[1] // quad
     seq = lax.axis_index("seq")
     dp = lax.axis_index("dp")
-    high = lax.div(seq, quad)
-    member = lax.rem(seq, quad)
 
     def merged(weight, adapt, expand):
         return (weight.astype(F32) + matmul(adapt, expand)).astype(BF16)
-
-    def unit_cols(a):
-        return lax.dynamic_slice_in_dim(a, member * units, units, 1)
-
-    def unit_rows(a):
-        return lax.dynamic_slice_in_dim(a, member * units, units, 0)
 
     wq = merged(w_query, query_adapt, query_expand)
     wk = merged(w_key, key_adapt, key_expand)
     wv = merged(w_value, value_adapt, value_expand)
     wo = merged(w_out, out_adapt, out_expand)
-    wg = merged(unit_cols(w_gate), gate_adapt, unit_cols(gate_expand))
-    wu = merged(unit_cols(w_up), up_adapt, unit_cols(up_expand))
-    wd = merged(unit_rows(w_down), unit_rows(down_adapt), down_expand)
-    half_rank = rank // 2
-    my_ranks = lambda a, axis: lax.dynamic_slice_in_dim(a, high * half_rank, half_rank, axis)
-    low_gu = jnp.concatenate([my_ranks(gate_adapt, 1), my_ranks(up_adapt, 1)], axis=1)
-    low_d = my_ranks(down_expand, 0)
-
     token_rows = tokens[0, 0].astype(F32)
     grad_rows_in = out_grad[0, 0]
     normed, unit_attn, rms_attn = normalize(token_rows, gain_attn)
@@ -695,12 +1026,12 @@
     seg_rows = jnp.zeros((16, rows), F32).at[0].set(segment_ids[0, 0].astype(F32))
 
     zyx, xzy = "lhbxc", "xlhbc"
-    (normed_all,), (kv_all,), (seg_all,), (grad_all,) = communicate(
+    (normed_all,), (kv_all,), (seg_all,), (grad_half,) = communicate(
         topo, "gather_attention", 0,
         Gather(topo, "dp", normed_attn, [(0, rows, "xc")]),
         Gather(topo, "all", key_value, row_parts(rows, (zyx, xzy), (7, 4))),
         Gather(topo, "all", seg_rows, [(0, 16, zyx)]),
-        Gather(topo, "all", grad_rows_in, row_parts(rows, (zyx, xzy), (7, 4))),
+        Gather(topo, "half", grad_rows_in, row_parts(rows, ("xlbc", "lbxc", "bxlc"), (1, 1, 1))),
     )
     kv_all = kv_all.reshape(groups, length, 2 * HD)
     keys_all, values_all = kv_all[..., :HD], kv_all[..., HD:]
@@ -726,23 +1057,10 @@
     middle = token_rows + out_sum
     normed, unit_mlp, rms_mlp = normalize(middle, gain_mlp)
     normed_mlp = normed.astype(BF16)
-    (mlp_all,), = communicate(
-        topo, "gather_mlp", 2, Gather(topo, "all", normed_mlp, row_parts(rows, (zyx, xzy), (7, 4)))
-    )
-    flat = lambda a: a.reshape(-1, width)
-    down_part, gn_part, dg, du, dd = feed_forward(
-        topo, flat(mlp_all), flat(grad_all), wg, wu, wd, low_gu, low_d, high.reshape(1)
-    )
-    half = topo.group_size("half")
-    blocks = lambda a: a.reshape(half, rows, width)
-    thirds = row_parts(rows, ("cxbl", "cblx", "clxb"), (1, 1, 1))
-    down_op = Scatter(topo, "half", blocks(down_part), thirds)
-    gn_op = Scatter(topo, "half", blocks(gn_part), thirds)
-    if half > 16:
-        (gn_sum,), = communicate(topo, "sum_mlp", 3, gn_op)
-        (down_sum,), = communicate(topo, "sum_down", 10, down_op)
-    else:
-        (down_sum,), (gn_sum,) = communicate(topo, "sum_mlp", 3, down_op, gn_op)
+    down_sum, gn_sum, dg, du, dd = feed_forward(
+        topo, 2, normed_mlp, grad_rows_in, grad_half,
+        w_gate, w_up, w_down, gate_adapt, gate_expand, up_adapt, up_expand, down_adapt, down_expand,
+    )
     result_rows = (middle + down_sum).astype(BF16)
     gain_mlp_term, grad_from_mlp = norm_backward(gn_sum, unit_mlp, rms_mlp, gain_mlp)
     grad_middle = grad_rows_in.astype(F32) + grad_from_mlp

time: 917 us -> 856 us (0.933)
  Pallas kernels: 669 us -> 633 us
  matrix products: 84.5 us -> 66.7 us
    pallas_call x10 -> x8, Pallas kernels: 508 us -> 313 us  [communicate(): pl.pallas_call(kernel, name=name, out_shape=[s for op in ops for s in op....]
    pallas_call x1, Pallas kernels: 161 us -> 321 us  [feed_forward(): pl.pallas_call(kernel, name='feed_forward', out_shape=out_shape, in_specs...]
    dot_general x14 -> x11, matrix products: 36.1 us -> 18.6 us  [matmul(): return jnp.dot(left, right, preferred_element_type=jnp.float32)]
    unnamed x159 -> x157, local copies, waits for them, and re-layouts: 34.9 us -> 35.1 us
where the time goes in v2:
time: 856 us; the launch traced here: 849 us
  Pallas kernels  633 us (74%)
  local copies, waits for them, and re-layouts  120 us (14%)
  matrix products  66.7 us (8%)
  other arithmetic  26.4 us (3%)
    pallas_call x1, Pallas kernels, feed_forward(): pl.pallas_call(kernel, name='feed_forward', out_shape=out_shape, in_specs...  321 us
    pallas_call x8, Pallas kernels, communicate(): pl.pallas_call(kernel, name=name, out_shape=[s for op in ops for s in op....  313 us
    unnamed x157, local copies, waits for them, and re-layouts  35.1 us
    slice x11, local copies, waits for them, and re-layouts, unfold(): return (full[:d_rows], full[d_rows:])  31.2 us
    dot_general x7, matrix products, t_dot(): lax.dot_general(left, right, (((0,), (0,)), ((), ())), preferred_element_...  19 us
    dot_general x10, matrix products, dot_t(): lax.dot_general(left, right, (((1,), (1,)), ((), ())), preferred_element_...  18.9 us
    dot_general x11, matrix products, matmul(): return jnp.dot(left, right, preferred_element_type=jnp.float32)  18.6 us

profile of v2, /device:TPU:0, one launch (start us, length us, event | category | flops | bytes accessed | tf_op | source)
XLA Modules:
  0.0 848.8 jit_solution(4109885299436943916)
XLA Ops:
  3.8 2.2 fusion.5
  9.5 65.1 %gather_attention.1 = (bf16[4,128,2048]{2,1,0:T(8,128)(2,1)}, bf16[32,128,512]{2,1,0:T(8,128)(2,1)}, f32[32,16,128]{2,1,0:T(8,128)}, bf16[16,128,2048]{2,1,0:T(8,128)(2,1)}) custom-call(bf16[128,2048]{1,0:T(8,128)(2,1)} %copy-done.15, bf16[128,512]{1,0:T(8,128)(2,1)} %pad_maximum_fusion.5.refs_1_, f32[16,128]{1,0:T(8,128)} %scatter.4.refs_2_, ...), custom_call_target="tpu_custom_call" | custom-call | tf_op jit(solution)/shard_map/gather_attention/pallas_call | solution.py:596
  76.6 4.1 copy.67
  80.8 2.5 add_convert_fusion.1
  84.8 1.6 copy-done.71
  89.2 2.3 fusion.30
  91.5 1.4 copy.70
  93.1 2.4 add_convert_fusion
  95.5 2.6 convolution_convert_fusion.1
  98.1 17.6 %sum_attention.1 = f32[128,2048]{1,0:T(8,128)} custom-call(bf16[4,128,2048]{2,1,0:T(8,128)(2,1)} %bitcast.278), custom_call_target="tpu_custom_call" | custom-call | tf_op jit(solution)/shard_map/sum_attention/pallas_call | solution.py:596
  115.7 1.4 multiply_reduce_fusion.2
  119.1 320.6 %feed_forward.1 = (bf16[16,128,2048]{2,1,0:T(8,128)(2,1)}, bf16[16,128,2048]{2,1,0:T(8,128)(2,1)}, bf16[4,288,1024]{2,1,0:T(8,128)(2,1)}, bf16[4,288,1024]{2,1,0...) custom-call(bf16[128,2048]{1,0:T(8,128)(2,1)} %multiply_convert_fusi, ...), custom_call_target="tpu_custom_call" | custom-call | flops 154618822656 | bytes 134217728 | tf_op jit(solution)/shard_map/feed_forward/pallas_call | solution.py:970
  439.8 1.7 multiply_reduce_fusion
  442.6 79.5 %gather_back.1 = (bf16[4,128,2048]{2,1,0:T(8,128)(2,1)}, bf16[4,288,1024]{2,1,0:T(8,128)(2,1)}, bf16[4,288,1024]{2,1,0:T(8,128)(2,1)}, bf16[4,288,1024]{2,1,0:T(8,128)(2,1)}) custom-call(bf16[128,2048]{1,0:T(8,128)(2,1)} %fusion.107.refs_0_, bf16[4,288,1024]{2,1,0:T(8,128)(2,1)} %get-tuple-element.60.refs_1_, ...), custom_call_target="tpu_custom_call" | custom-call | tf_op jit(solution)/shard_map/gather_back/pallas_call | solution.py:596
  522.2 3.7 convolution_convert_fusion.3
  526.0 2.0 reshape.387
  527.9 4.4 fusion.1
  535.9 2.5 pad_maximum_fusion.refs_1_
  542.2 2.6 convolution_convert_fusion
  544.8 48.6 %sum_back.1 = (f32[128,2048]{1,0:T(8,128)}, f32[128,512]{1,0:T(8,128)}) custom-call(bf16[4,128,2048]{2,1,0:T(8,128)(2,1)} %bitcast.277, bf16[32,128,512]{2,1,0:T(8,128)(2,1)} %pad_maximum_fusion.refs_1_), custom_call_target="tpu_custom_call" | custom-call | tf_op jit(solution)/shard_map/sum_back/pallas_call | solution.py:596
  594.8 1.7 convolution_add_fusion.3
  596.6 2.0 fusion.58
  599.3 6.9 gather_kv.1
  606.2 2.8 fusion.51
  609.0 2.8 fusion.50
  611.8 2.2 reshape.408
  614.0 3.9 copy.79
  617.9 4.4 convert_dynamic-update-slice_fusion.1
  624.4 3.9 copy.80
  628.3 2.2 reshape.409
  630.5 4.5 convert_dynamic-update-slice_fusion
  637.0 1.9 dynamic-slice_bitcast_fusion
  638.9 2.0 copy.81
  640.9 2.4 fusion.28
  644.6 66.4 %sum_weights.1 = f32[656,512]{1,0:T(8,128)} custom-call(bf16[8,656,512]{2,1,0:T(8,128)(2,1)} %pad_dynamic-update-slice_fusion.refs_0_), custom_call_target="tpu_custom_call" | custom-call | tf_op jit(solution)/shard_map/sum_weights/pallas_call | solution.py:596
  711.1 2.2 slice_bitcast_fusion.17
  714.7 2.2 copy-done.1
  717.2 2.9 copy.78
  720.1 4.5 convert_element_type.236
  724.6 3.1 fusion.44
  728.2 2.2 copy-done.2
  730.7 2.9 copy.77
  733.7 4.5 convert_element_type.234
  738.1 3.1 fusion.47
  741.3 2.0 convolution_convert_fusion.8
  743.9 2.2 copy-done.5
  746.1 2.3 slice.214
  748.4 5.4 copy.86
  753.8 3.8 fusion.33
  761.7 1.8 fusion.61.refs_0_
  763.5 9.2 %sum_small.1 = f32[336,256]{1,0:T(8,128)} custom-call(bf16[4,336,256]{2,1,0:T(8,128)(2,1)} %fusion.61.refs_0_), custom_call_target="tpu_custom_call" | custom-call | tf_op jit(solution)/shard_map/sum_small/pallas_call | solution.py:596
  774.4 1.6 slice.180.refs_0_
  776.0 19.3 %finish.1 = (f32[208,256]{1,0:T(8,128)}, f32[8,16,256]{2,1,0:T(8,128)}) custom-call(f32[208,256]{1,0:T(8,128)} %slice.180.refs_0_, f32[8,16,256]{2,1,0:T(8,128)} %bitcast.300), custom_call_target="tpu_custom_call" | custom-call | tf_op jit(solution)/shard_map/finish/pallas_call | solution.py:596
  795.3 1.6 fusion.110
  796.9 1.5 fusion.111
  799.6 2.0 copy.95
  804.2 1.5 slice_bitcast_fusion.18
  807.7 3.3 fusion.63
  811.1 4.8 slice.209
  815.9 5.4 copy.90
  821.2 5.6 copy.96
  826.8 4.8 slice.210
  831.6 5.4 copy.91
  837.0 5.6 copy.97
  (217 shorter events, 50.9 us)
Async XLA Ops:
  0.7 80.1 %copy-start = (bf16[2048,256]{1,0:T(8,128)(2,1)S(1)}, bf16[2048,256]{1,0:T(8,128)(2,1)}, u32[]{:S(2)}) copy-start(bf16[2048,256]{1,0:T(8,128)(2,1)} %param.40) | copy-start | bytes 3145732
  0.7 5.7 copy-start.67
  3.8 4.1 copy-start.15
  3.8 3.6 copy-start.34
  3.8 3.6 copy-start.35
  3.8 3.6 copy-start.44
  6.1 1.3 copy-start.12
  6.5 1.8 copy-start.69
  7.4 77.2 %copy-start.42 = (f32[128,128]{1,0:T(8,128)}, f32[128,128]{1,0:T(8,128)S(1)}, u32[]{:S(2)}) copy-start(f32[128,128]{1,0:T(8,128)S(1)} %get-tuple-element.156) | copy-start | bytes 196612
  7.4 1.5 copy-start.73
  7.9 72.9 %copy-start.10 = (bf16[2048,256]{1,0:T(8,128)(2,1)}, bf16[2048,256]{1,0:T(8,128)(2,1)S(1)}, u32[]{:S(2)}) copy-start(bf16[2048,256]{1,0:T(8,128)(2,1)S(1)} %fusion.6) | copy-start | bytes 3145732
  75.7 5.1 copy-start.38
  76.6 11.6 %copy-start.16 = (pred[4,128,1024]{1,2,0:T(8,128)(4,1)}, pred[4,128,1024]{1,2,0:T(8,128)(4,1)S(1)}, u32[]{:S(2)}) copy-start(pred[4,128,1024]{1,2,0:T(8,128)(4,1)S(1)} %compare_and_fusion) | copy-start | bytes 1572868
  80.8 2.5 copy-start.21
  83.3 1.3 copy-start.26
  83.3 3.1 copy-start.71
  84.8 2.4 copy-start.50
  84.8 2.4 copy-start.52
  87.2 2.0 copy-start.6
  88.2 3.3 copy-start.60
  89.2 3.8 copy-start.40
  91.5 1.6 copy-start.36
  93.0 2.5 copy-start.19
  95.5 2.6 copy-start.29
  98.1 17.6 %copy-start.8 = (bf16[1,1,128,2048]{3,2,1,0:T(8,128)(2,1)S(1)}, bf16[1,1,128,2048]{3,2,1,0:T(8,128)(2,1)}, u32[]{:S(2)}) copy-start(bf16[1,1,128,2048]{3,2,1,0:T(8,128)(2,1)} %param.28) | copy-start | bytes 1572868
  98.1 20.1 %copy-start.57 = (f32[2048]{0:T(1024)S(1)}, f32[2048]{0:T(1024)}, u32[]{:S(2)}) copy-start(f32[2048]{0:T(1024)} %param.32) | copy-start | bytes 24580
  117.2 1.9 copy-start.62
  119.1 320.7 %copy-start.4 = (f32[128,2048]{1,0:T(8,128)S(1)}, f32[128,2048]{1,0:T(8,128)}, u32[]{:S(2)}) copy-start(f32[128,2048]{1,0:T(8,128)} %copy-done.3) | copy-start | bytes 3145732
  119.1 320.7 %copy-start.58 = (f32[2048]{0:T(1024)S(1)}, f32[2048]{0:T(1024)}, u32[]{:S(2)}) copy-start(f32[2048]{0:T(1024)} %param.32) | copy-start | bytes 24580
  119.1 320.7 %copy-start.63 = (f32[128]{0:T(128)S(1)}, f32[128]{0:T(128)}, u32[]{:S(2)}) copy-start(f32[128]{0:T(128)} %copy-done.62) | copy-start | bytes 1540
  439.7 1.7 copy-start.14
  439.7 1.7 copy-start.18
  441.5 80.7 %copy-start.66 = (f32[128]{0:T(128)}, f32[128]{0:T(128)S(1)}, u32[]{:S(2)}) copy-start(f32[128]{0:T(128)S(1)} %broadcast_multiply_fusion.1) | copy-start | bytes 1540
  442.6 79.6 %copy-start.30 = (bf16[512,2048]{1,0:T(8,128)(2,1)S(1)}, bf16[512,2048]{1,0:T(8,128)(2,1)}, u32[]{:S(2)}) copy-start(bf16[512,2048]{1,0:T(8,128)(2,1)} %copy-done.29) | copy-start | bytes 6291460
  522.2 5.7 copy-start.17
  522.2 5.7 copy-start.61
  527.9 4.5 copy-start.7
  532.4 1.3 copy-start.51
  535.9 3.7 copy-start.72
  540.6 1.7 copy-start.27
  544.8 48.6 %copy-start.68 = (f32[128]{0:T(128)S(1)}, f32[128]{0:T(128)}, u32[]{:S(2)}) copy-start(f32[128]{0:T(128)} %copy-done.67) | copy-start | bytes 1540
  544.8 48.6 %copy-start.70 = (f32[128]{0:T(128)S(1)}, f32[128]{0:T(128)}, u32[]{:S(2)}) copy-start(f32[128]{0:T(128)} %copy-done.69) | copy-start | bytes 1540
  544.8 50.0 %copy-start.13 = (bf16[2048,256]{1,0:T(8,128)(2,1)S(1)}, bf16[2048,256]{1,0:T(8,128)(2,1)}, u32[]{:S(2)}) copy-start(bf16[2048,256]{1,0:T(8,128)(2,1)} %copy-done.12) | copy-start | bytes 3145732
  593.4 3.1 copy-start.9
  593.4 3.1 copy-start.11
  593.4 3.1 copy-start.49
  593.4 3.1 copy-start.59
  593.4 3.1 copy-start.65
  617.9 4.4 copy-start.22
  630.5 4.5 copy-start.28
  630.5 4.5 copy-start.37
  644.6 68.7 %copy-start.39 = (bf16[256,512]{1,0:T(8,128)(2,1)S(1)}, bf16[256,512]{1,0:T(8,128)(2,1)}, u32[]{:S(2)}) copy-start(bf16[256,512]{1,0:T(8,128)(2,1)} %param.41) | copy-start | bytes 786436
  711.1 3.0 copy-start.25
  714.7 2.2 copy-start.1
  724.6 3.1 copy-start.24
  728.2 2.2 copy-start.2
  738.1 3.2 copy-start.41
  738.1 5.2 copy-start.23
  743.9 2.2 copy-start.5
  753.8 3.8 copy-start.48
  763.5 39.0 %copy-start.45 = (bf16[256,256]{1,0:T(8,128)(2,1)S(1)}, bf16[256,256]{1,0:T(8,128)(2,1)}, u32[]{:S(2)}) copy-start(bf16[256,256]{1,0:T(8,128)(2,1)} %param.45) | copy-start | bytes 393220
  763.5 39.9 %copy-start.46 = (bf16[256,256]{1,0:T(8,128)(2,1)S(1)}, bf16[256,256]{1,0:T(8,128)(2,1)}, u32[]{:S(2)}) copy-start(bf16[256,256]{1,0:T(8,128)(2,1)} %param.43) | copy-start | bytes 393220
  802.6 8.5 %copy-start.54 = (f32[64,256]{1,0:T(8,128)}, f32[64,256]{1,0:T(8,128)S(1)}, u32[]{:S(2)}) copy-start(f32[64,256]{1,0:T(8,128)S(1)} %get-tuple-element.133) | copy-start | bytes 196612
  802.6 8.5 copy-start.55
  (10 other events, 9.3 us)

commit v3 on v2

v3 whole, which is shorter than its diff:
```python
import itertools
import math

import jax
import jax.numpy as jnp
from jax import lax
from jax.experimental import pallas as pl
from jax.experimental.pallas import tpu as pltpu
from jax.sharding import PartitionSpec as P

HD = 256
EPSILON = 1e-06
ROTARY_BASE = 10000.0
MASKED = -1e30

MESH = pl.DeviceIdType.MESH
BF16 = jnp.bfloat16
F32 = jnp.float32


class Topo:
    def __init__(self, n_dp, n_seq):
        self.n_dp, self.n_seq = n_dp, n_seq
        self.size = {"c": 2, "x": n_dp // 2, "b": n_seq // 4, "l": 2, "h": 2}

    def here(self):
        dp, seq = lax.axis_index("dp"), lax.axis_index("seq")
        nb = self.size["b"]
        outer = lax.div(seq, nb)
        return {
            "c": lax.rem(dp, 2),
            "x": lax.div(dp, 2),
            "b": lax.rem(seq, nb),
            "l": lax.rem(outer, 2),
            "h": lax.div(outer, 2),
        }

    def moved(self, at, dims, offsets, sign=1):
        new = dict(at)
        for dim, offset in zip(dims, offsets):
            n = self.size[dim]
            if not (isinstance(offset, int) and offset == 0):
                new[dim] = lax.rem(at[dim] + (offset if sign > 0 else n - offset), n)
        return new

    def seq_of(self, at):
        return (at["h"] * 2 + at["l"]) * self.size["b"] + at["b"]

    def device(self, at):
        return (at["x"] * 2 + at["c"], self.seq_of(at))

    def index(self, at, group):
        dp, seq = self.device(at)
        if group == "all":
            return dp * self.n_seq + seq
        if group == "half":
            nb = self.size["b"]
            return dp * (2 * nb) + at["l"] * nb + at["b"]
        if group == "dp":
            return dp
        if group == "seq":
            return seq
        if group == "quad":
            return at["l"] * self.size["b"] + at["b"]
        raise ValueError(group)

    def group_size(self, group):
        nb = self.size["b"]
        return {
            "all": self.n_dp * self.n_seq,
            "half": self.n_dp * 2 * nb,
            "dp": self.n_dp,
            "seq": self.n_seq,
            "quad": 2 * nb,
        }[group]


GROUP_DIMS = {"all": "cxblh", "half": "cxbl", "dp": "cx", "seq": "blh", "quad": "bl"}


def remote(src, dst, send_sem, recv_sem, device):
    return pltpu.make_async_remote_copy(
        src_ref=src,
        dst_ref=dst,
        send_sem=send_sem,
        recv_sem=recv_sem,
        device_id=device,
        device_id_type=MESH,
    )


def peers_of(topo, group):
    return {((dim, d),) for dim in GROUP_DIMS[group] for d in range(1, topo.size[dim])}


def digits(key, sizes):
    k = 0
    for o, s in zip(key, sizes):
        k = k * s + o
    return k


def arrived(topo, at, ref, send_sem, recv_sem):
    remote(ref, ref, send_sem, recv_sem, topo.device(at)).wait_recv()


class Gather:
    def __init__(self, topo, group, x, parts, beyond=None, need=None):
        self.topo, self.group, self.parts, self.beyond = topo, group, parts, beyond
        self.slots = "half" if beyond else group
        self.need = need or (lambda dims, key: 0)
        self.inputs = [x]
        rows, cols = x.shape
        n = topo.group_size(group)
        self.outputs = [jax.ShapeDtypeStruct((topo.group_size(self.slots), rows, cols), x.dtype)]
        self.in_specs = [pl.BlockSpec(memory_space=pl.ANY)]
        self.out_specs = [pl.BlockSpec(memory_space=pl.ANY)]
        self.scratch = [
            pltpu.SemaphoreType.DMA((len(parts), n)),
            pltpu.SemaphoreType.DMA((len(parts), n)),
            pltpu.SemaphoreType.DMA(()),
        ]

    def peers(self):
        return peers_of(self.topo, self.group)

    def keeps(self, order, key):
        return not self.beyond or key[order.index(self.beyond)] != 0

    def work(self):
        work = []
        for part, (row, rows, order) in enumerate(self.parts):
            for key in itertools.product(*[range(self.topo.size[dim]) for dim in order]):
                if not any(key) or self.keeps(order, key):
                    hops = sum(1 for o in key if o)
                    last = max([i for i, o in enumerate(key) if o], default=-1)
                    work.append((hops, self.need(order, key), last, part, key))
        work.sort()
        return [(w[3], w[4]) for w in work]

    def steps(self, at, ins, outs, scratch):
        topo = self.topo
        (x_ref,), (out_ref,) = ins, outs
        send_sem, recv_sem, own_sem = scratch
        size_of = lambda order: [topo.size[dim] for dim in order]

        def copy(part, key, stage, d):
            row, rows, order = self.parts[part]
            slot = topo.index(topo.moved(at, order, key, -1), self.slots)
            new_key = tuple(d if i == stage else o for i, o in enumerate(key))
            place = out_ref.at[slot, pl.ds(row, rows)]
            k = digits(new_key, size_of(order))
            target = topo.device(topo.moved(at, [order[stage]], [d]))
            source = place if any(key) else x_ref.at[pl.ds(row, rows)]
            return remote(source, place, send_sem.at[part, k], recv_sem.at[part, k], target)

        def own():
            return pltpu.make_async_copy(x_ref, out_ref.at[topo.index(at, self.slots)], own_sem)

        sent, steps = [], []
        for n, (part, key) in enumerate(self.work()):
            row, rows, order = self.parts[part]
            last = max([i for i, o in enumerate(key) if o], default=-1)
            sends = []
            for stage in range(last + 1, len(order)):
                for d in range(1, topo.size[order[stage]]):
                    new_key = tuple(d if i == stage else o for i, o in enumerate(key))
                    if self.keeps(order, new_key):
                        sends.append((self.need(order, new_key), stage, d))
            sends = [(part, key, stage, d) for _, stage, d in sorted(sends)]
            sent += sends

            def step(n=n, part=part, key=key, sends=sends):
                row, rows, order = self.parts[part]
                if n == 0 and not self.beyond:
                    own().start()
                if any(key):
                    slot = topo.index(topo.moved(at, order, key, -1), self.slots)
                    k = digits(key, size_of(order))
                    arrived(topo, at, out_ref.at[slot, pl.ds(row, rows)], send_sem.at[part, k], recv_sem.at[part, k])
                for send in sends:
                    copy(*send).start()

            steps.append(step)

        def end():
            for send in sent:
                copy(*send).wait_send()
            if not self.beyond:
                own().wait()

        return steps, [end]


TILE = 512


class Reduce:
    def __init__(self, topo, group, shape, dtype, parts):
        self.topo, self.group, self.parts, self.dtype = topo, group, parts, dtype
        n, rows, cols = shape
        assert n == topo.group_size(group), (n, group)
        self.tile = math.gcd(cols, TILE)

    def peers(self):
        return peers_of(self.topo, self.group)

    def stages(self, part):
        sizes = self.sizes(part)
        return [(max(s - 1, 1), math.prod(sizes[k + 1 :])) for k, s in enumerate(sizes)]

    def sizes(self, part):
        return [self.topo.size[dim] for dim in self.parts[part][2]]

    def jobs(self):
        jobs = []
        for part in range(len(self.parts)):
            sizes = self.sizes(part)
            keys = list(itertools.product(*[range(s) for s in sizes]))
            first = {k: min([i for i, o in enumerate(k) if o], default=len(sizes)) for k in keys}
            keys.sort(key=lambda k: (first[k], [0 if o else 1 for o in k]))
            jobs += [(first[key], rank, part, key) for rank, key in enumerate(keys)]
        jobs.sort()
        return [(first, part, key) for first, _, part, key in jobs]

    def block(self, at, part, key):
        return self.topo.index(self.topo.moved(at, self.parts[part][2], key), self.group)

    def target(self, at, part, key, stage):
        return self.topo.device(self.topo.moved(at, [self.parts[part][2][stage]], [key[stage]]))

    def place(self, part, key, stage):
        return key[stage] - 1, digits(key[stage + 1 :], self.sizes(part)[stage + 1 :])

    def terms(self, part, key, first):
        sizes = self.sizes(part)
        return [
            (stage, d - 1, digits(key[stage + 1 :], sizes[stage + 1 :]))
            for stage in range(first)
            for d in range(1, sizes[stage])
        ]


class VScatter(Reduce):
    def __init__(self, topo, group, shape, dtype, parts):
        super().__init__(topo, group, shape, dtype, parts)
        self.scratch = []
        for part, (row, nrows, order) in enumerate(parts):
            self.scratch.append(pltpu.VMEM((math.prod(self.sizes(part)[1:]), nrows, shape[2]), dtype))
            for m, rest in self.stages(part):
                self.scratch.append(pltpu.VMEM((m, rest, nrows, shape[2]), dtype))
                self.scratch.append(pltpu.SemaphoreType.DMA((m, rest)))
                self.scratch.append(pltpu.SemaphoreType.DMA((m, rest)))

    def steps(self, at, x_ref, out_ref, scratch):
        topo, tile = self.topo, self.tile
        scratch = list(scratch)
        bufs = []
        for part in range(len(self.parts)):
            acc = scratch.pop(0)
            bufs.append((acc, [tuple(scratch.pop(0) for _ in range(3)) for _ in self.sizes(part)]))
        jobs = self.jobs()

        def send(first, part, key):
            row, nrows, order = self.parts[part]
            acc, stages = bufs[part]
            buf, send_sem, recv_sem = stages[first]
            d, k = self.place(part, key, first)
            if first == 0:
                source = x_ref.at[self.block(at, part, key), pl.ds(row, nrows)]
            else:
                source = acc.at[digits(key[1:], self.sizes(part)[1:])]
            return remote(
                source, buf.at[d, k], send_sem.at[d, k], recv_sem.at[d, k], self.target(at, part, key, first)
            )

        def start():
            for job in jobs:
                if job[0] == 0:
                    send(*job).start()

        steps = [start]
        for job in jobs:
            if job[0] == 0:
                continue

            def step(job=job):
                first, part, key = job
                row, nrows, order = self.parts[part]
                acc, stages = bufs[part]
                terms = self.terms(part, key, first)
                for stage, d, k in terms:
                    buf, send_sem, recv_sem = stages[stage]
                    arrived(topo, at, buf.at[d, k], send_sem.at[d, k], recv_sem.at[d, k])
                block, kk = self.block(at, part, key), digits(key[1:], self.sizes(part)[1:])
                final = first == len(order)

                tiles = x_ref.shape[-1] // tile

                def add(n, _):
                    r0 = pl.multiple_of(lax.div(n, tiles) * 16, 16)
                    cols = pl.ds(pl.multiple_of(lax.rem(n, tiles) * tile, tile), tile)
                    r1 = pl.ds(pl.multiple_of(row + r0, 16), 16)
                    total = x_ref[block, r1, cols].astype(F32)
                    for stage, d, k in terms:
                        total = total + stages[stage][0][d, k, pl.ds(r0, 16), cols].astype(F32)
                    if final:
                        out_ref[r1, cols] = total.astype(out_ref.dtype)
                    else:
                        acc[kk, pl.ds(r0, 16), cols] = total.astype(acc.dtype)
                    return 0

                lax.fori_loop(0, nrows // 16 * tiles, add, 0)
                if not final:
                    send(*job).start()

            steps.append(step)

        def end():
            for job in jobs:
                if job[0] < len(self.parts[job[1]][2]):
                    send(*job).wait_send()

        return steps, [end]


class SlimScatter(Reduce):
    RING = 4

    def __init__(self, topo, group, shape, dtype, parts):
        super().__init__(topo, group, shape, dtype, parts)
        rows, cols = shape[1:]
        self.outputs = [jax.ShapeDtypeStruct((rows, cols), F32)]
        self.out_specs = [pl.BlockSpec(memory_space=pltpu.VMEM)]
        self.scratch = []
        self.most, self.cols = max(p[1] for p in parts), cols
        self.count = 1 + sum(topo.size[d] - 1 for d in GROUP_DIMS[group])
        for part, (row, nrows, order) in enumerate(parts):
            for m, rest in self.stages(part):
                self.outputs.append(jax.ShapeDtypeStruct((m, rest, nrows, cols), dtype))
                self.out_specs.append(pl.BlockSpec(memory_space=pl.ANY))
                self.scratch.append(pltpu.SemaphoreType.DMA((m, rest)))
                self.scratch.append(pltpu.SemaphoreType.DMA((m, rest)))

    def shared_scratch(self):
        return [
            pltpu.VMEM((2, self.count, self.most, self.cols), self.dtype),
            pltpu.SemaphoreType.DMA((2, self.count)),
            pltpu.VMEM((self.RING, self.most, self.cols), self.dtype),
        ]

    def steps(self, at, x_ref, outs, scratch, shared):
        topo, tile = self.topo, self.tile
        outs, scratch = list(outs), list(scratch)
        out_ref = outs.pop(0)
        stage_buf, stage_sem, ring = shared
        bufs = [
            [(outs.pop(0), scratch.pop(0), scratch.pop(0)) for _ in self.sizes(part)]
            for part in range(len(self.parts))
        ]
        jobs = self.jobs()
        later = [job for job in jobs if job[0] > 0]
        passed = [job for job in later if job[0] < len(self.parts[job[1]][2])]

        def own(part, key):
            row, nrows, order = self.parts[part]
            return x_ref.at[self.block(at, part, key), pl.ds(row, nrows)]

        def send(first, part, key, source=None):
            row, nrows, order = self.parts[part]
            buf, send_sem, recv_sem = bufs[part][first]
            d, k = self.place(part, key, first)
            if source is None:
                source = own(part, key) if first == 0 else ring.at[0, pl.ds(0, nrows)]
            return remote(
                source, buf.at[d, k], send_sem.at[d, k], recv_sem.at[d, k], self.target(at, part, key, first)
            )

        def loads(n):
            first, part, key = later[n]
            nrows = self.parts[part][1]
            sources = [own(part, key)] + [
                bufs[part][stage][0].at[d, k] for stage, d, k in self.terms(part, key, first)
            ]
            return [
                pltpu.make_async_copy(ref, stage_buf.at[n % 2, i, pl.ds(0, nrows)], stage_sem.at[n % 2, i])
                for i, ref in enumerate(sources)
            ]

        def fetch(n):
            first, part, key = later[n]
            for stage, d, k in self.terms(part, key, first):
                buf, send_sem, recv_sem = bufs[part][stage]
                arrived(topo, at, buf.at[d, k], send_sem.at[d, k], recv_sem.at[d, k])
            for cp in loads(n):
                cp.start()

        def start():
            for job in jobs:
                if job[0] == 0:
                    send(*job).start()

        steps = [start, lambda: fetch(0)]
        for n in range(len(later)):

            def step(n=n):
                first, part, key = later[n]
                row, nrows, order = self.parts[part]
                copies = loads(n)
                for cp in copies:
                    cp.wait()
                final = first == len(order)
                if not final:
                    sent = passed.index(later[n])
                    if sent >= self.RING:
                        send(*passed[sent - self.RING]).wait_send()

                tiles = self.cols // tile

                def add(n_tile, _):
                    r0 = pl.multiple_of(lax.div(n_tile, tiles) * 16, 16)
                    cols = pl.ds(pl.multiple_of(lax.rem(n_tile, tiles) * tile, tile), tile)
                    total = stage_buf[n % 2, 0, pl.ds(r0, 16), cols].astype(F32)
                    for i in range(1, len(copies)):
                        total = total + stage_buf[n % 2, i, pl.ds(r0, 16), cols].astype(F32)
                    if final:
                        out_ref[pl.ds(pl.multiple_of(row + r0, 16), 16), cols] = total
                    else:
                        ring[sent % self.RING, pl.ds(r0, 16), cols] = total.astype(ring.dtype)
                    return 0

                lax.fori_loop(0, nrows // 16 * tiles, add, 0)
                if not final:
                    send(first, part, key, ring.at[sent % self.RING, pl.ds(0, nrows)]).start()
                if n + 1 < len(later):
                    fetch(n + 1)

            steps.append(step)

        def end():
            for job in jobs:
                if job[0] == 0:
                    send(*job).wait_send()
            for job in passed[-self.RING :]:
                send(*job).wait_send()

        return steps, [end]


class Exchange:
    def __init__(self, topo, group, x):
        self.topo, self.group = topo, group
        self.inputs = [x]
        n = x.shape[0]
        assert n == topo.group_size(group)
        self.outputs = [jax.ShapeDtypeStruct(x.shape, x.dtype)]
        self.in_specs = [pl.BlockSpec(memory_space=pl.ANY)]
        self.out_specs = [pl.BlockSpec(memory_space=pl.ANY)]
        self.scratch = [
            pltpu.SemaphoreType.DMA((n,)),
            pltpu.SemaphoreType.DMA((n,)),
            pltpu.SemaphoreType.DMA(()),
        ]

    def offsets(self):
        dims = GROUP_DIMS[self.group]
        return dims, [
            o for o in itertools.product(*[range(self.topo.size[d]) for d in dims]) if any(o)
        ]

    def peers(self):
        dims, offsets = self.offsets()
        return {tuple((dim, o) for dim, o in zip(dims, off) if o) for off in offsets}

    def steps(self, at, ins, outs, scratch):
        topo = self.topo
        (x_ref,), (out_ref,) = ins, outs
        send_sem, recv_sem, own_sem = scratch
        dims, offsets = self.offsets()
        me = topo.index(at, self.group)

        def own():
            return pltpu.make_async_copy(x_ref.at[me], out_ref.at[me], own_sem)

        def send(i):
            there = topo.moved(at, dims, offsets[i])
            source = x_ref.at[topo.index(there, self.group)]
            return remote(source, out_ref.at[me], send_sem.at[i], recv_sem.at[i], topo.device(there))

        def start():
            own().start()
            for i in range(len(offsets)):
                send(i).start()

        def wait(i):
            ref = out_ref.at[topo.index(topo.moved(at, dims, offsets[i], -1), self.group)]
            arrived(topo, at, ref, send_sem.at[i], recv_sem.at[i])

        def end():
            for i in range(len(offsets)):
                send(i).wait_send()
            own().wait()

        return [start] + [lambda i=i: wait(i) for i in range(len(offsets))], [end]


class Finish:
    def __init__(self, topo, x, y):
        self.topo = topo
        self.inputs = [x, y]
        self.outputs = [
            jax.ShapeDtypeStruct(x.shape, x.dtype),
            jax.ShapeDtypeStruct(y.shape, y.dtype),
        ]
        self.in_specs = [pl.BlockSpec(memory_space=pl.ANY)] * 2
        self.out_specs = [pl.BlockSpec(memory_space=pl.ANY)] * 2
        self.inner = Exchange(topo, "seq", y)
        self.scratch = self.inner.scratch + [pltpu.SemaphoreType.DMA(())] * 3

    def peers(self):
        return self.inner.peers()

    def route(self):
        topo = self.topo
        dp, seq = lax.axis_index("dp"), lax.axis_index("seq")
        n = seq * topo.n_dp + dp
        target = (lax.div(n, topo.n_seq), lax.rem(n, topo.n_seq))
        m = dp * topo.n_seq + seq
        source = (lax.rem(m, topo.n_dp), lax.div(m, topo.n_dp))
        stays = (target[0] == dp) & (target[1] == seq)
        return target, source, stays

    def greet(self, barrier):
        target, source, stays = self.route()

        @pl.when(jnp.logical_not(stays))
        def _():
            pl.semaphore_signal(barrier, inc=1, device_id=source, device_id_type=MESH)

        return jnp.where(stays, 0, 1)

    def steps(self, at, ins, outs, scratch):
        (x_ref, y_ref), (x_out, y_out) = ins, outs
        send_sem, recv_sem, own_sem = scratch[3:]
        target, source, stays = self.route()
        cp = remote(x_ref, x_out, send_sem, recv_sem, target)
        own = pltpu.make_async_copy(x_ref, x_out, own_sem)
        inner, ends = self.inner.steps(at, [y_ref], [y_out], scratch[:3])

        def start():
            pl.when(stays)(own.start)
            pl.when(jnp.logical_not(stays))(cp.start)

        def end():
            pl.when(stays)(own.wait)
            pl.when(jnp.logical_not(stays))(cp.wait)

        return [start] + inner, ends + [end]


def greet(topo, ops):
    at = topo.here()
    peers = sorted(set().union(*[op.peers() for op in ops]))
    barrier = pltpu.get_barrier_semaphore()
    for peer in peers:
        there = topo.device(topo.moved(at, [p[0] for p in peer], [p[1] for p in peer]))
        pl.semaphore_signal(barrier, inc=1, device_id=there, device_id_type=MESH)
    count = len(peers)
    for op in ops:
        if hasattr(op, "greet"):
            count = count + op.greet(barrier)
    pl.semaphore_wait(barrier, count)
    return at


class Steps:
    def __init__(self, steps):
        self.todo = steps[0] + steps[1]

    def run(self, count=1):
        for _ in range(count):
            if self.todo:
                self.todo.pop(0)()

    def finish(self):
        self.run(len(self.todo))


def run_slot(t, slots):
    def tree(low, high):
        if not any(slots[low:high]):
            return
        if high - low == 1:
            for step in slots[low]:
                step()
            return
        middle = (low + high) // 2
        left, right = any(slots[low:middle]), any(slots[middle:high])
        if left and right:
            lax.cond(t < middle, lambda: tree(low, middle), lambda: tree(middle, high))
        elif left:
            pl.when(t < middle)(lambda: tree(low, middle))
        else:
            pl.when(t >= middle)(lambda: tree(middle, high))

    tree(0, len(slots))


def communicate(topo, name, collective_id, *ops):
    n_in = [len(op.inputs) for op in ops]
    n_out = [len(op.outputs) for op in ops]
    n_scratch = [len(op.scratch) for op in ops]

    def kernel(*refs):
        refs = list(refs)
        take = lambda counts: [[refs.pop(0) for _ in range(k)] for k in counts]
        ins, outs, scratch = take(n_in), take(n_out), take(n_scratch)
        at = greet(topo, ops)
        running = [Steps(op.steps(at, i, o, s)) for op, i, o, s in zip(ops, ins, outs, scratch)]
        while any(r.todo for r in running):
            for r in running:
                r.run()

    results = pl.pallas_call(
        kernel,
        name=name,
        out_shape=[s for op in ops for s in op.outputs],
        in_specs=[s for op in ops for s in op.in_specs],
        out_specs=[s for op in ops for s in op.out_specs],
        scratch_shapes=[s for op in ops for s in op.scratch],
        compiler_params=pltpu.CompilerParams(
            collective_id=collective_id, has_side_effects=True, vmem_limit_bytes=58 << 20
        ),
    )(*[x for op in ops for x in op.inputs])
    results = list(results)
    return [[results.pop(0) for _ in range(k)] for k in n_out]


class Scatter(VScatter):
    def __init__(self, topo, group, x, parts):
        super().__init__(topo, group, x.shape, x.dtype, parts)
        self.inputs = [x]
        self.outputs = [jax.ShapeDtypeStruct(x.shape[1:], F32)]
        self.in_specs = [pl.BlockSpec(memory_space=pltpu.VMEM)]
        self.out_specs = [pl.BlockSpec(memory_space=pltpu.VMEM)]

    def steps(self, at, ins, outs, scratch):
        return super().steps(at, ins[0], outs[0], scratch)


def row_parts(rows, orders, weights, step=16):
    parts, row, total = [], 0, sum(weights)
    for i, (order, weight) in enumerate(zip(orders, weights)):
        n = rows - row if i == len(orders) - 1 else min(rows - row, int(round(rows * weight / total / step)) * step)
        if n:
            parts.append((row, n, order))
            row += n
    return parts


def matmul(left, right):
    return jnp.dot(left, right, preferred_element_type=jnp.float32)


def contract(form, left, right):
    return jnp.einsum(form, left, right, preferred_element_type=jnp.float32)


def rotary(positions, size):
    half_size = size // 2
    frequency = ROTARY_BASE ** (-(jnp.arange(half_size, dtype=jnp.float32) * 2.0) / size)
    angles = positions.astype(jnp.float32)[:, None] * frequency[None, :]
    return (jnp.cos(angles), jnp.sin(angles))


def rotate(values, cosine_table, sine_table):
    half_size = values.shape[-1] // 2
    first_half = values[..., :half_size]
    second_half = values[..., half_size:]
    return jnp.concatenate(
        [
            first_half * cosine_table - second_half * sine_table,
            second_half * cosine_table + first_half * sine_table,
        ],
        axis=-1,
    )


def normalize(values, gain_vector):
    inverse_rms = lax.rsqrt(jnp.mean(values * values, axis=-1, keepdims=True) + EPSILON)
    unit_rows = values * inverse_rms
    return (unit_rows * gain_vector, unit_rows, inverse_rms)


def norm_backward(grad_normed, unit_rows, inverse_rms, gain_vector):
    gain_term = jnp.sum(grad_normed * unit_rows, axis=0)
    grad_unit = grad_normed * gain_vector
    inner = jnp.mean(grad_unit * unit_rows, axis=-1, keepdims=True)
    return (gain_term, inverse_rms * (grad_unit - unit_rows * inner))


def dot_t(left, right):
    return lax.dot_general(left, right, (((1,), (1,)), ((), ())), preferred_element_type=F32)


def t_dot(left, right):
    return lax.dot_general(left, right, (((0,), (0,)), ((), ())), preferred_element_type=F32)


GELU_C = math.sqrt(2.0 / math.pi)


def gelu_parts(v):
    square = v * v
    t = jnp.tanh(GELU_C * (v + 0.044715 * v * square))
    half_up = 0.5 * (1.0 + t)
    slope = half_up + 0.5 * v * (1.0 - t * t) * (GELU_C * (1.0 + 3.0 * 0.044715 * square))
    return v * half_up, slope


def feed_forward(
    topo, collective_id, normed, grads, grads_half,
    w_gate, w_up, w_down, gate_adapt, gate_expand, up_adapt, up_expand, down_adapt, down_expand,
):
    rows, width = normed.shape
    quad = topo.group_size("quad")
    half = topo.group_size("half")
    units = w_gate.shape[1] // quad
    rank = gate_adapt.shape[1]
    ranks = rank // 2
    half_width = width // 2
    d_rows, r_rows = half_width // quad, ranks // quad
    per_chunk = 512 // rows
    tile = 512
    block = 256

    dims = "hxclb"
    keys = list(itertools.product(*[range(topo.size[d]) for d in dims]))
    chunks = [keys[i : i + per_chunk] for i in range(0, len(keys), per_chunk)]
    own = len(chunks) // 2
    chunk_of = {key: i for i, keys_of in enumerate(chunks) for key in keys_of}

    def need(order, key):
        at_dim = dict(zip(order, key))
        return chunk_of[tuple(at_dim.get(d, 0) for d in dims)]

    near = row_parts(rows, ("xlbc", "lbxc", "bxlc"), (1, 1, 1))
    far = row_parts(rows, ("hxlbc", "hlbxc", "hbxlc"), (1, 1, 1))
    gather_n = Gather(topo, "half", normed, near, need=need)
    far_n = Gather(topo, "all", normed, far, beyond="h", need=need)
    far_g = Gather(topo, "all", grads, far, beyond="h", need=need)
    thirds = row_parts(rows, ("cxbl", "cblx", "clxb"), (1, 1, 1))
    sum_n = SlimScatter(topo, "half", (half, rows, width), BF16, thirds)
    sum_d = SlimScatter(topo, "half", (half, rows, width), BF16, thirds)
    comm = [gather_n, far_n, far_g, sum_n, sum_d]

    inputs = [
        normed, grads, grads_half, w_gate, w_up, w_down,
        gate_adapt, gate_expand, up_adapt, up_expand, down_adapt, down_expand,
    ]
    part = jax.ShapeDtypeStruct((half, rows, width), BF16)
    grad = jax.ShapeDtypeStruct((quad, d_rows + r_rows, units), BF16)
    any_spec = pl.BlockSpec(memory_space=pl.ANY)
    out_shape = [part, part, grad, grad, grad]
    out_specs = [any_spec] * 5
    scratch = [
        pltpu.VMEM((width, units), BF16), pltpu.VMEM((width, units), BF16), pltpu.VMEM((units, width), BF16),
        pltpu.VMEM((width, rank), BF16), pltpu.VMEM((rank, units), BF16),
        pltpu.VMEM((width, rank), BF16), pltpu.VMEM((rank, units), BF16),
        pltpu.VMEM((units, rank), BF16), pltpu.VMEM((rank, width), BF16),
        pltpu.VMEM((half_width + ranks, units), F32),
        pltpu.VMEM((half_width + ranks, units), F32),
        pltpu.VMEM((half_width + ranks, units), F32),
        pltpu.VMEM((3, tile, units), BF16),
        pltpu.VMEM((3, tile, ranks), BF16),
        pltpu.VMEM((2, tile, width), BF16), pltpu.VMEM((2, tile, width), BF16),
        pltpu.VMEM((tile, width), BF16), pltpu.VMEM((tile, width), BF16),
        pltpu.SemaphoreType.DMA((9,)),
        pltpu.SemaphoreType.DMA((2, 2, per_chunk)),
        pltpu.SemaphoreType.DMA((2, per_chunk)),
        pltpu.SemaphoreType.DMA((3,)),
    ]
    n_own = len(scratch)
    shared = sum_n.shared_scratch() + sum_d.shared_scratch()
    scratch = scratch + shared
    for op in comm:
        out_shape = out_shape + op.outputs
        out_specs = out_specs + op.out_specs
        scratch = scratch + op.scratch

    def kernel(*refs):
        refs = list(refs)
        (
            n_hbm, g_hbm, g_half, wg_hbm, wu_hbm, wd_hbm, ga_hbm, ge_hbm, ua_hbm, ue_hbm, da_hbm, de_hbm,
        ) = [refs.pop(0) for _ in inputs]
        down_part, gn_part, dg_out, du_out, dd_out = [refs.pop(0) for _ in range(5)]
        op_outs = [[refs.pop(0) for _ in op.outputs] for op in comm]
        (
            wg, wu, wd, ga, ge, ua, ue, da, de, acc_g, acc_u, acc_d, acts, low_s, n_buf, g_buf, down_st, gn_st,
            w_sem, load_sem, store_sem, grad_sem,
        ) = [refs.pop(0) for _ in range(n_own)]
        shared_refs = [refs.pop(0) for _ in shared]
        op_scratch = [[refs.pop(0) for _ in op.scratch] for op in comm]
        mix_s, gg_s, gu_s = acts.at[0], acts.at[1], acts.at[2]
        at = topo.here()
        high = at["h"]
        member = topo.index(at, "quad")
        unit_at = pl.multiple_of(member * units, units)

        w_copies = [
            pltpu.make_async_copy(src, dst, w_sem.at[i])
            for i, (src, dst) in enumerate(
                (
                    (de_hbm, de),
                    (da_hbm.at[pl.ds(unit_at, units), :], da),
                    (wd_hbm.at[pl.ds(unit_at, units), :], wd),
                    (ga_hbm, ga),
                    (ge_hbm.at[:, pl.ds(unit_at, units)], ge),
                    (wg_hbm.at[:, pl.ds(unit_at, units)], wg),
                    (ua_hbm, ua),
                    (ue_hbm.at[:, pl.ds(unit_at, units)], ue),
                    (wu_hbm.at[:, pl.ds(unit_at, units)], wu),
                )
            )
        ]
        for cp in w_copies:
            cp.start()

        greet(topo, comm)
        gathers = (gather_n, far_n, far_g)
        all_steps = [
            op.steps(at, [x], o, sc) for op, x, o, sc in zip(gathers, (n_hbm, n_hbm, g_hbm), op_outs, op_scratch)
        ]
        ranked = []
        for g, (op, (steps_g, _)) in enumerate(zip(gathers, all_steps)):
            for i, (f, (p, k)) in enumerate(zip(steps_g, op.work())):
                when = NEAR_US * i / len(steps_g) - 20.0 if g == 0 else FAR_AT + (g + 2 * i) * FAR_US
                ranked.append((when if any(k) or g else -1e3, g, i, f, need(op.parts[p][2], k)))
        ranked.sort(key=lambda w: w[:3])
        steps = [(f, chunk) for _, _, _, f, chunk in ranked]
        when_of = [w[0] for w in ranked]
        started = len(gather_n.parts)
        for f, _ in steps[:started]:
            f()

        def upto(chunk, done):
            last = [i for i, (_, c) in enumerate(steps) if c <= chunk and i >= started]
            return max([done] + [i + 1 for i in last])

        acc_g[...] = jnp.zeros_like(acc_g)
        acc_u[...] = jnp.zeros_like(acc_u)
        acc_d[...] = jnp.zeros_like(acc_d)

        def merge_rows(weight, adapt, expand, total):
            def one(i, _):
                r = pl.ds(pl.multiple_of(i * block, block), block)
                weight[r, :] = (weight[r, :].astype(F32) + matmul(adapt[r, :], expand[...])).astype(BF16)
                return 0

            lax.fori_loop(0, total // block, one, 0)

        for cp in w_copies[:3]:
            cp.wait()
        merge_rows(wd, da, de, units)
        for cp in w_copies[3:6]:
            cp.wait()
        merge_rows(wg, ga, ge, width)
        for cp in w_copies[6:]:
            cp.wait()
        merge_rows(wu, ua, ue, width)

        def key_of(c, i):
            k = c * per_chunk + i
            key = []
            for d in reversed(dims):
                key.append(lax.rem(k, topo.size[d]))
                k = lax.div(k, topo.size[d])
            return key[::-1]

        def chunk_copies(c, slot, other):
            copies = []
            for i in range(per_chunk):
                origin = topo.moved(at, dims, key_of(c, i), -1)
                r = pl.ds(i * rows, rows)
                in_half = topo.index(origin, "half")
                n_src, g_src = (op_outs[1][0], op_outs[2][0]) if other else (op_outs[0][0], g_half)
                copies.append(pltpu.make_async_copy(n_src.at[in_half], n_buf.at[slot, r], load_sem.at[slot, 0, i]))
                copies.append(pltpu.make_async_copy(g_src.at[in_half], g_buf.at[slot, r], load_sem.at[slot, 1, i]))
            return copies

        def first_copies():
            copies = chunk_copies(0, 0, False)
            r = pl.ds(0, rows)
            copies[0] = pltpu.make_async_copy(n_hbm, n_buf.at[0, r], load_sem.at[0, 0, 0])
            return copies

        def store_copies(c):
            copies = []
            for i in range(per_chunk):
                slot = topo.index(topo.moved(at, dims, key_of(c, i), -1), "half")
                r = pl.ds(i * rows, rows)
                copies.append(pltpu.make_async_copy(down_st.at[r], down_part.at[slot], store_sem.at[0, i]))
                copies.append(pltpu.make_async_copy(gn_st.at[r], gn_part.at[slot], store_sem.at[1, i]))
            return copies

        n_one, n_two, n_three = units // block, width // block, half_width // block
        scale = units / 1024
        kinds = {
            False: [("one", n_one, 1.9), ("two", n_two, 1.0 * scale), ("pre", 1, 2.0 * scale), ("three", n_three, 0.7 * scale)],
            True: [("one", n_one, 1.9), ("pre", 1, 2.0 * scale), ("three", n_three, 0.7 * scale)],
        }
        slots = {(other, kind): [[] for _ in range(own * n)] for other in (False, True) for kind, n, _ in kinds[other]}
        done = upto(0, started)
        for f, _ in steps[started:done]:
            f()
        clock = 0.0
        for c in range(len(chunks)):
            other = c >= own
            for kind, n, cost in kinds[other]:
                for i in range(n):
                    clock += cost
                    target = max(done, sum(1 for w in when_of if w <= clock))
                    if kind == "pre" and c + 1 < len(chunks):
                        target = upto(c + 1, target)
                    slots[other, kind][(c - own if other else c) * n + i] += [f for f, _ in steps[done:target]]
                    done = target
        sum_a = sum_n.steps(at, gn_part, op_outs[3], op_scratch[3], shared_refs[:3])
        sum_b = sum_d.steps(at, down_part, op_outs[4], op_scratch[4], shared_refs[3:])
        sums = [sum_a[0][0], sum_b[0][0]]
        for i in range(1, max(len(sum_a[0]), len(sum_b[0]))):
            sums += sum_a[0][i : i + 1] + sum_b[0][i : i + 1]
        clock, summed = 0.0, 0
        for c in range(own):
            for kind, n, cost in kinds[True]:
                for i in range(n):
                    clock += cost
                    target = min(len(sums), 2 + int(max(clock - 3.0, 0.0) / SUM_US))
                    if kind != "pre":
                        slots[True, kind][c * n + i] += sums[summed:target]
                        summed = target

        for cp in first_copies():
            cp.start()
        low_cols = pl.ds(pl.multiple_of(high * ranks, ranks), ranks)
        half_at = high * half_width

        def chunk_loop(other):
            first = own if other else 0

            def body(k, _):
                c = first + k
                slot = lax.rem(c, 2)
                nb, gb = n_buf.at[slot], g_buf.at[slot]
                for cp in chunk_copies(c, slot, other):
                    cp.wait()
                low_s[0] = matmul(nb[...], ga[:, low_cols]).astype(BF16)
                low_s[1] = matmul(nb[...], ua[:, low_cols]).astype(BF16)
                low_s[2] = dot_t(gb[...], de[low_cols, :]).astype(BF16)

                def one(i, _):
                    cols = pl.ds(pl.multiple_of(i * block, block), block)
                    gate = matmul(nb[...], wg[:, cols])
                    up = matmul(nb[...], wu[:, cols])
                    act, slope = gelu_parts(gate)
                    gm = dot_t(gb[...], wd[cols, :])
                    mix_s[:, cols] = (act * up).astype(BF16)
                    gg_s[:, cols] = (gm * up * slope).astype(BF16)
                    gu_s[:, cols] = (gm * act).astype(BF16)
                    run_slot(k * n_one + i, slots[other, "one"])
                    return 0

                lax.fori_loop(0, n_one, one, 0)
                if not other:

                    @pl.when(c > 0)
                    def _():
                        for cp in store_copies(c - 1):
                            cp.wait()

                    def two(i, _):
                        cols = pl.ds(pl.multiple_of(i * block, block), block)
                        down_st[:, cols] = matmul(mix_s[...], wd[:, cols]).astype(BF16)
                        gn_st[:, cols] = (dot_t(gg_s[...], wg[cols, :]) + dot_t(gu_s[...], wu[cols, :])).astype(BF16)
                        run_slot(k * n_two + i, slots[other, "two"])
                        return 0

                    lax.fori_loop(0, n_two, two, 0)
                    for cp in store_copies(c):
                        cp.start()
                for i, (acc, grads_s) in enumerate(((acc_g, gg_s), (acc_u, gu_s), (acc_d, mix_s))):
                    acc[half_width:, :] += t_dot(low_s[i], grads_s[...])
                run_slot(k, slots[other, "pre"])
                if other:

                    @pl.when(c + 1 < len(chunks))
                    def _():
                        for cp in chunk_copies(c + 1, 1 - slot, True):
                            cp.start()

                else:

                    @pl.when(c + 1 < own)
                    def _():
                        for cp in chunk_copies(c + 1, 1 - slot, False):
                            cp.start()

                    @pl.when(c + 1 == own)
                    def _():
                        for cp in chunk_copies(c + 1, 1 - slot, True):
                            cp.start()

                def three(i, _):
                    r = pl.ds(pl.multiple_of(i * block, block), block)
                    cols = pl.ds(pl.multiple_of(half_at + i * block, block), block)
                    acc_g[r, :] += t_dot(nb[:, cols], gg_s[...])
                    acc_u[r, :] += t_dot(nb[:, cols], gu_s[...])
                    acc_d[r, :] += t_dot(gb[:, cols], mix_s[...])
                    run_slot(k * n_three + i, slots[other, "three"])
                    return 0

                lax.fori_loop(0, n_three, three, 0)
                return 0

            lax.fori_loop(0, own, body, 0)

        chunk_loop(False)
        for cp in store_copies(own - 1):
            cp.wait()
        chunk_loop(True)

        pending = []
        for q in range(quad):
            for k, (acc, out) in enumerate(((acc_g, dg_out), (acc_u, du_out), (acc_d, dd_out))):
                if len(pending) >= 3:
                    pending.pop(0).wait()
                acts[k, :d_rows, :] = acc[q * d_rows : (q + 1) * d_rows, :].astype(BF16)
                acts[k, d_rows : d_rows + r_rows, :] = acc[
                    half_width + q * r_rows : half_width + (q + 1) * r_rows, :
                ].astype(BF16)
                cp = pltpu.make_async_copy(acts.at[k, pl.ds(0, d_rows + r_rows)], out.at[q], grad_sem.at[k])
                cp.start()
                pending.append(cp)
        for f in steps[done:]:
            f[0]()
        for f in sums[summed:]:
            f()
        for cp in pending:
            cp.wait()
        for f in [f for _, end in all_steps for f in end] + sum_a[1] + sum_b[1]:
            f()

    flops = 2 * rows * topo.n_dp * topo.n_seq * units * width * 9
    results = pl.pallas_call(
        kernel,
        name="feed_forward",
        out_shape=out_shape,
        in_specs=[any_spec] * len(inputs),
        out_specs=out_specs,
        scratch_shapes=scratch,
        compiler_params=pltpu.CompilerParams(
            collective_id=collective_id, has_side_effects=True, vmem_limit_bytes=60 << 20
        ),
        cost_estimate=pl.CostEstimate(flops=flops, bytes_accessed=1 << 27, transcendentals=0),
    )(*inputs)
    dg, du, dd = results[2:5]
    skip = 5 + sum(len(op.outputs) for op in (gather_n, far_n, far_g))
    return results[skip + len(sum_n.outputs)], results[skip], dg, du, dd


NEAR_US = 45.0
FAR_AT = 5.0
FAR_US = 0.55
SUM_US = 1.1


def attention_back(
    topo, collective_id, grad_branch, grad_middle, query_rot, heads_out, key_value, log_total, own_segs, key_segs,
    normed_all, unit_attn, rms_attn, gain_attn, gain_mlp_term, cosine, sine, wo, wq, wk, wv,
    query_adapt, out_expand, key_adapt, value_adapt, dg, du, dd,
):
    groups, rows, width = normed_all.shape
    n_seq = topo.n_seq
    length = rows * n_seq
    head_cols = heads_out.shape[1]
    heads = head_cols // HD
    tokens = groups * rows
    rank = query_adapt.shape[1]
    scale = HD ** (-0.5)
    d_rows, r_rows = width // n_seq, rank // n_seq
    share_d, share_r = width // groups, rank // groups
    kv_d, kv_r = d_rows // groups, r_rows // groups
    kv_pad = -(-kv_r // 16) * 16
    kv_rows = kv_d + kv_pad + 16

    gather_g = Gather(topo, "dp", grad_branch, [(0, rows, "xc")])
    gather_kv = Gather(topo, "dp", jax.ShapeDtypeStruct((rows, 2 * HD), BF16), [(0, rows, "xc")])
    swaps = [Exchange(topo, "quad", a) for a in (dg, du, dd)]
    seq_parts = lambda n: row_parts(n, ("blh", "lhb"), (9, 5))
    w_shape = (n_seq, d_rows + r_rows, head_cols)
    sum_o = VScatter(topo, "seq", w_shape, BF16, seq_parts(d_rows + r_rows))
    sum_q = VScatter(topo, "seq", w_shape, BF16, seq_parts(d_rows + r_rows))
    sum_k = VScatter(topo, "seq", (n_seq, kv_rows, 2 * HD), BF16, seq_parts(kv_rows))
    kv_shape = (groups * n_seq, rows, 2 * HD)
    sum_kv = VScatter(topo, "all", kv_shape, BF16, row_parts(rows, ("cxblh", "cblhx"), (1, 1)))
    sum_n = VScatter(topo, "dp", (groups, rows, width), BF16, [(0, rows, "cx")])

    inputs = [
        grad_branch, grad_middle, query_rot, heads_out, key_value, log_total, own_segs, key_segs,
        normed_all, unit_attn, rms_attn, gain_attn, gain_mlp_term, cosine, sine, wo, wq, wk, wv,
        query_adapt, out_expand, key_adapt, value_adapt, dg, du, dd,
    ]
    vmem, anywhere = pl.BlockSpec(memory_space=pltpu.VMEM), pl.BlockSpec(memory_space=pl.ANY)
    big = groups * n_seq > 32
    in_specs = [anywhere] + [vmem] * (len(inputs) - 4) + [anywhere] * 3
    if big:
        in_specs[4] = anywhere
    out_shape = [
        jax.ShapeDtypeStruct((rows, width), BF16),
        jax.ShapeDtypeStruct((d_rows + r_rows, head_cols), F32),
        jax.ShapeDtypeStruct((d_rows + r_rows, head_cols), F32),
        jax.ShapeDtypeStruct((kv_rows, 2 * HD), F32),
    ] + [op.outputs[0] for op in swaps]
    out_specs = [vmem] * 4 + [anywhere] * 3
    if big:
        sum_kv = SlimScatter(topo, "all", kv_shape, BF16, row_parts(rows, ("cxblh", "cblhx"), (1, 1)))
        out_shape = out_shape + [jax.ShapeDtypeStruct(kv_shape, BF16)] + sum_kv.outputs
        out_specs = out_specs + [anywhere] + sum_kv.out_specs
    scratch = [
        pltpu.VMEM((groups, rows, width), BF16),
        pltpu.VMEM((tokens, head_cols), BF16),
        pltpu.VMEM((tokens, head_cols), BF16),
        pltpu.VMEM(w_shape, BF16),
        pltpu.VMEM(w_shape, BF16),
        pltpu.VMEM((n_seq, kv_rows, 2 * HD), BF16),
        pltpu.VMEM((length, 2 * HD) if big else kv_shape, BF16),
        pltpu.VMEM((groups, rows, width), BF16),
        pltpu.VMEM((rows, 2 * HD), F32),
        pltpu.VMEM((rows, width), F32),
        pltpu.VMEM((rows, 2 * HD), BF16),
        pltpu.VMEM((groups, rows, 2 * HD), BF16),
        pltpu.SemaphoreType.DMA((n_seq,)),
    ]
    n_own = len(scratch)
    shared = sum_kv.shared_scratch() + [pltpu.VMEM((length, 2 * HD), BF16)] if big else []
    scratch = scratch + shared
    ops = [gather_g, gather_kv] + swaps + [sum_o, sum_q, sum_k, sum_kv, sum_n]
    for op in ops:
        scratch = scratch + op.scratch

    def kernel(*refs):
        refs = list(refs)
        (
            gb_hbm, gmid, qrot, hout, kv, lse, own_seg, key_seg, norm_all, unit, rms, gain, gain_term, cos, sin,
            wo_r, wq_r, wk_r, wv_r, qa, oe, ka, va, dg_r, du_r, dd_r,
        ) = [refs.pop(0) for _ in inputs]
        grad_rows, so_out, sq_out, sk_out, dg_o, du_o, dd_o = [refs.pop(0) for _ in range(7)]
        kv_outs = [refs.pop(0) for _ in out_shape[7:]]
        (
            ga, gh, gq, xo, xq, xk, xkv, xn, kv_sum, n_sum, gkv, gkv_all, load_sem,
        ) = [refs.pop(0) for _ in range(n_own)]
        shared_refs = [refs.pop(0) for _ in shared]
        op_scratch = [[refs.pop(0) for _ in op.scratch] for op in ops]
        dp = lax.axis_index("dp")
        at = greet(topo, ops)
        get_g = Steps(gather_g.steps(at, [gb_hbm], [ga], op_scratch[0]))
        get_g.run()
        moves = [
            Steps(op.steps(at, [r], [o], sc))
            for op, r, o, sc in zip(swaps, (dg_r, du_r, dd_r), (dg_o, du_o, dd_o), op_scratch[2:5])
        ]
        moves[0].run()
        get_g.finish()
        flat = lambda ref: ref[...].reshape(tokens, ref.shape[-1])
        moves[1].run()

        gh[...] = dot_t(flat(ga), wo_r[...]).astype(BF16)
        for j in range(n_seq):
            part = t_dot(ga[:, :, j * d_rows : (j + 1) * d_rows].reshape(tokens, d_rows), hout[...])
            xo[j, :d_rows, :] = part.astype(BF16)
        low = dot_t(flat(ga), oe[...]).astype(BF16)
        part = t_dot(low, hout[...]).astype(BF16)
        for j in range(n_seq):
            xo[j, d_rows:, :] = part[j * r_rows : (j + 1) * r_rows, :]
        get_o = Steps(sum_o.steps(at, xo, so_out, op_scratch[5]))
        get_o.run()

        seq = lax.axis_index("seq")
        key_at = lax.broadcasted_iota(jnp.int32, (heads * rows, length), 1)
        row_at = lax.broadcasted_iota(jnp.int32, (heads * rows, length), 0)
        causal = key_at <= seq * rows + lax.rem(row_at, rows)
        for s in range(groups):
            r = slice(s * rows, (s + 1) * rows)
            stack = lambda ref: jnp.concatenate([ref[r, h * HD : (h + 1) * HD] for h in range(heads)], axis=0)
            q, d_o = stack(qrot), stack(gh)
            if big:
                one = shared_refs[3]
                cp = pltpu.make_async_copy(kv.at[pl.ds(s * length, length)], one, load_sem.at[0])
                cp.start()
                cp.wait()
            else:
                one = kv.at[pl.ds(s * length, length)]
            keys, values = one[:, :HD], one[:, HD:]
            mine = jnp.concatenate([own_seg[:, s : s + 1]] * heads, axis=0)
            allowed = causal & (mine == key_seg[s : s + 1, :])
            scores = jnp.where(allowed, dot_t(q, keys) * scale, MASKED)
            probs = jnp.exp(scores - lse[s])
            grad_probs = dot_t(d_o, values)
            delta = jnp.sum(probs * grad_probs, axis=-1, keepdims=True)
            grad_scores = (probs * (grad_probs - delta)).astype(BF16)
            d_q = matmul(grad_scores, keys) * scale
            d_k = (t_dot(grad_scores, q) * scale).astype(BF16)
            d_v = t_dot(probs.astype(BF16), d_o).astype(BF16)
            both = jnp.concatenate([d_k, d_v], axis=1)
            if big:
                xkv[...] = both
                copies = [
                    pltpu.make_async_copy(
                        xkv.at[pl.ds(j * rows, rows)], kv_outs[0].at[s * n_seq + j], load_sem.at[j]
                    )
                    for j in range(n_seq)
                ]
                for cp in copies:
                    cp.start()
                for cp in copies:
                    cp.wait()
            else:
                xkv[s * n_seq : (s + 1) * n_seq] = both.reshape(n_seq, rows, 2 * HD)
            for h in range(heads):
                gq[r, h * HD : (h + 1) * HD] = rotate(
                    d_q[h * rows : (h + 1) * rows], cos[...], -sin[...]
                ).astype(BF16)
            get_o.run(3)
        if big:
            get_kv = Steps(sum_kv.steps(at, kv_outs[0], kv_outs[1:], op_scratch[8], shared_refs[:3]))
        else:
            get_kv = Steps(sum_kv.steps(at, xkv, kv_sum, op_scratch[8]))
        get_kv.run()
        for s in range(groups):
            xn[s] = dot_t(gq[s * rows : (s + 1) * rows, :], wq_r[...]).astype(BF16)
        get_n = Steps(sum_n.steps(at, xn, n_sum, op_scratch[9]))
        get_n.run()

        for j in range(n_seq):
            part = t_dot(norm_all[:, :, j * d_rows : (j + 1) * d_rows].reshape(tokens, d_rows), gq[...])
            xq[j, :d_rows, :] = part.astype(BF16)
            if j % 2:
                get_kv.run(2)
                get_n.run(1)
        low = matmul(flat(norm_all), qa[...]).astype(BF16)
        part = t_dot(low, gq[...]).astype(BF16)
        for j in range(n_seq):
            xq[j, d_rows:, :] = part[j * r_rows : (j + 1) * r_rows, :]
        get_kv.finish()
        get_q = Steps(sum_q.steps(at, xq, sq_out, op_scratch[6]))
        get_q.run()
        moves[2].run()
        get_n.finish()

        total_kv = kv_outs[1] if big else kv_sum
        gk = rotate(total_kv[:, :HD], cos[...], -sin[...]).astype(BF16)
        gv = total_kv[:, HD:].astype(BF16)
        gkv[:, :HD] = gk
        gkv[:, HD:] = gv
        get_kv2 = Steps(gather_kv.steps(at, [gkv], [gkv_all], op_scratch[1]))
        get_kv2.run()
        grad_normed = n_sum[...] + dot_t(gk, wk_r[...]) + dot_t(gv, wv_r[...])
        u_rows = unit[...]
        gain_attn_term = jnp.sum(grad_normed * u_rows, axis=0, keepdims=True)
        grad_unit = grad_normed * gain[...]
        inner = jnp.mean(grad_unit * u_rows, axis=-1, keepdims=True)
        grad_rows[...] = (gmid[...] + rms[...] * (grad_unit - u_rows * inner)).astype(BF16)
        get_kv2.finish()
        mine = pl.ds(pl.multiple_of(dp * share_d, share_d), share_d)
        part_rows = norm_all[:, :, mine].reshape(tokens, share_d)
        low_k = matmul(flat(norm_all), ka[...]).astype(BF16)
        low_v = matmul(flat(norm_all), va[...]).astype(BF16)
        g_rows = flat(gkv_all)
        part = t_dot(part_rows, g_rows).astype(BF16)
        low = jnp.concatenate(
            [t_dot(low_k, g_rows[:, :HD]), t_dot(low_v, g_rows[:, HD:])], axis=1
        )
        zero_r = jnp.zeros((kv_pad - kv_r, 2 * HD), F32)
        terms = jnp.concatenate([gain_attn_term, gain_term[...], jnp.zeros((14, width), F32)], axis=0)
        zero_c = jnp.zeros((16, 2 * HD - d_rows), F32)
        for j in range(n_seq):
            xk[j, :kv_d, :] = part[j * kv_d : (j + 1) * kv_d, :]
            xk[j, kv_d : kv_d + kv_pad, :] = jnp.concatenate(
                [low[j * kv_r : (j + 1) * kv_r, :], zero_r], axis=0
            ).astype(BF16)
            xk[j, kv_d + kv_pad :, :] = jnp.concatenate(
                [terms[:, j * d_rows : (j + 1) * d_rows], zero_c], axis=1
            ).astype(BF16)
        get_k = Steps(sum_k.steps(at, xk, sk_out, op_scratch[7]))
        get_k.run()
        get_o.finish()
        get_q.finish()
        get_k.finish()
        for move in moves:
            move.finish()

    results = pl.pallas_call(
        kernel,
        name="attention_back",
        out_shape=out_shape,
        in_specs=in_specs,
        out_specs=out_specs,
        scratch_shapes=scratch,
        compiler_params=pltpu.CompilerParams(
            collective_id=collective_id, has_side_effects=True, vmem_limit_bytes=60 << 20
        ),
    )(*inputs)
    return results[:7]


def unfold(d_rows, dg, du, dd, gate_expand, up_expand, down_adapt):
    quad, total, units = dg.shape
    rank = gate_expand.shape[0]
    r_rows = total - d_rows

    def kernel(dg_ref, du_ref, dd_ref, ge_ref, ue_ref, da_ref, wg, eg, wu, eu, wd, ad, ga, ua, de):
        first = pl.program_id(0) == 0
        for src, w, e in ((dg_ref, wg, eg), (du_ref, wu, eu)):
            w[...] = src[0, :d_rows, :].astype(F32)
            e[...] = src[0, d_rows:, :].astype(F32)
        both = dd_ref[0].astype(F32).T
        wd[...] = both[:, :d_rows]
        ad[...] = both[:, d_rows:]
        for out, term in (
            (ga, dot_t(dg_ref[0, :d_rows, :], ge_ref[...])),
            (ua, dot_t(du_ref[0, :d_rows, :], ue_ref[...])),
            (de, matmul(dd_ref[0, :d_rows, :], da_ref[...])),
        ):
            out[...] = jnp.where(first, term, term + out[...])

    cols = lambda n: pl.BlockSpec((n, units), lambda q: (0, q))
    side = lambda n: pl.BlockSpec((units, n), lambda q: (q, 0))
    block = pl.BlockSpec((1, total, units), lambda q: (q, 0, 0))
    kept = pl.BlockSpec((d_rows, rank), lambda q: (0, 0))
    shape = lambda *s: jax.ShapeDtypeStruct(s, F32)
    all_units = quad * units
    return pl.pallas_call(
        kernel,
        name="unfold",
        grid=(quad,),
        in_specs=[block, block, block, cols(rank), cols(rank), side(rank)],
        out_specs=[cols(d_rows), cols(r_rows), cols(d_rows), cols(r_rows), side(d_rows), side(r_rows)] + [kept] * 3,
        out_shape=[
            shape(d_rows, all_units), shape(r_rows, all_units), shape(d_rows, all_units), shape(r_rows, all_units),
            shape(all_units, d_rows), shape(all_units, r_rows),
        ] + [shape(d_rows, rank)] * 3,
        compiler_params=pltpu.CompilerParams(vmem_limit_bytes=48 << 20),
    )(dg, du, dd, gate_expand, up_expand, down_adapt)


def local(
    topo,
    tokens, segment_ids, out_grad, gain_attn, gain_mlp, w_query, w_key, w_value, w_out, w_gate, w_up, w_down,
    query_adapt, query_expand, key_adapt, key_expand, value_adapt, value_expand, out_adapt, out_expand,
    gate_adapt, gate_expand, up_adapt, up_expand, down_adapt, down_expand,
):
    rows, width = tokens.shape[2], tokens.shape[3]
    groups, n_seq = topo.n_dp, topo.n_seq
    length = rows * n_seq
    heads_dev = w_query.shape[1] // HD
    head_cols = heads_dev * HD
    rank = query_adapt.shape[1]
    scale_qk = HD ** (-0.5)
    quad = topo.group_size("quad")
    units = w_gate.shape[1] // quad
    seq = lax.axis_index("seq")
    dp = lax.axis_index("dp")

    def merged(weight, adapt, expand):
        return (weight.astype(F32) + matmul(adapt, expand)).astype(BF16)

    wq = merged(w_query, query_adapt, query_expand)
    wk = merged(w_key, key_adapt, key_expand)
    wv = merged(w_value, value_adapt, value_expand)
    wo = merged(w_out, out_adapt, out_expand)
    token_rows = tokens[0, 0].astype(F32)
    grad_rows_in = out_grad[0, 0]
    normed, unit_attn, rms_attn = normalize(token_rows, gain_attn)
    normed_attn = normed.astype(BF16)
    positions = seq * rows + jnp.arange(rows, dtype=jnp.int32)
    cosine_table, sine_table = rotary(positions, HD)
    cosine_heads, sine_heads = cosine_table[:, None, :], sine_table[:, None, :]
    key_rot = rotate(matmul(normed_attn, wk), cosine_table, sine_table).astype(BF16)
    value_rows = matmul(normed_attn, wv).astype(BF16)
    key_value = jnp.concatenate([key_rot, value_rows], axis=1)
    seg_rows = jnp.zeros((16, rows), F32).at[0].set(segment_ids[0, 0].astype(F32))

    zyx, xzy = "lhbxc", "xlhbc"
    (normed_all,), (kv_all,), (seg_all,), (grad_half,) = communicate(
        topo, "gather_attention", 0,
        Gather(topo, "dp", normed_attn, [(0, rows, "xc")]),
        Gather(topo, "all", key_value, row_parts(rows, (zyx, xzy), (7, 4))),
        Gather(topo, "all", seg_rows, [(0, 16, zyx)]),
        Gather(topo, "half", grad_rows_in, row_parts(rows, ("xlbc", "lbxc", "bxlc"), (1, 1, 1))),
    )
    kv_all = kv_all.reshape(groups, length, 2 * HD)
    keys_all, values_all = kv_all[..., :HD], kv_all[..., HD:]
    segments = seg_all[:, 0, :].reshape(groups, length)
    own_segments = lax.dynamic_slice_in_dim(segments, seq * rows, rows, 1)
    key_positions = jnp.arange(length, dtype=jnp.int32)
    causal = (key_positions[None, :] <= positions[:, None])[None, :, :]
    allowed = (causal & (own_segments[:, :, None] == segments[:, None, :]))[:, None, :, :]

    queries = matmul(normed_all.reshape(groups * rows, width), wq)
    query_rot = rotate(queries.reshape(groups, rows, heads_dev, HD), cosine_heads, sine_heads).astype(BF16)
    scores = jnp.where(allowed, contract("sthd,sjd->shtj", query_rot, keys_all) * scale_qk, MASKED)
    row_top = jnp.max(scores, axis=-1, keepdims=True)
    log_total = row_top + jnp.log(jnp.sum(jnp.exp(scores - row_top), axis=-1, keepdims=True))
    prob_low = jnp.exp(scores - log_total).astype(BF16)
    heads_out = (
        contract("shtj,sjd->sthd", prob_low, values_all).reshape(groups * rows, head_cols).astype(BF16)
    )
    out_part = matmul(heads_out, wo).astype(BF16).reshape(groups, rows, width)
    (out_sum,), = communicate(
        topo, "sum_attention", 1, Scatter(topo, "dp", out_part, [(0, rows, "cx")])
    )
    middle = token_rows + out_sum
    normed, unit_mlp, rms_mlp = normalize(middle, gain_mlp)
    normed_mlp = normed.astype(BF16)
    down_sum, gn_sum, dg, du, dd = feed_forward(
        topo, 2, normed_mlp, grad_rows_in, grad_half,
        w_gate, w_up, w_down, gate_adapt, gate_expand, up_adapt, up_expand, down_adapt, down_expand,
    )
    result_rows = (middle + down_sum).astype(BF16)
    gain_mlp_term, grad_from_mlp = norm_backward(gn_sum, unit_mlp, rms_mlp, gain_mlp)
    grad_middle = grad_rows_in.astype(F32) + grad_from_mlp
    grad_branch_attn = grad_middle.astype(BF16)
    my_kv_ranks = lambda a: lax.dynamic_slice_in_dim(a, dp * (rank // groups), rank // groups, 1)
    grad_rows, so, sq, sk, dg, du, dd = attention_back(
        topo, 4, grad_branch_attn, grad_middle,
        query_rot.reshape(groups * rows, head_cols), heads_out, kv_all.reshape(groups * length, 2 * HD),
        log_total.reshape(groups, heads_dev * rows, 1), own_segments.T, segments,
        normed_all, unit_attn, rms_attn, gain_attn[None], gain_mlp_term[None], cosine_table, sine_table,
        wo, wq, wk, wv, query_adapt, out_expand, my_kv_ranks(key_adapt), my_kv_ranks(value_adapt), dg, du, dd,
    )
    d_rows, r_rows = width // n_seq, rank // n_seq
    per_dev_d, per_dev_r = d_rows // groups, r_rows // groups
    kv_pad = -(-per_dev_r // 16) * 16
    grad_wg, grad_ge, grad_wu, grad_ue, grad_wd, grad_da, part_ga, part_ua, part_de = unfold(
        d_rows, dg, du, dd, gate_expand, up_expand, down_adapt
    )
    grad_wq, grad_qe = sq[:d_rows], sq[d_rows:]
    grad_wo, grad_oa = so[:d_rows].T, so[d_rows:].T
    grad_wkv, grad_kve = sk[:per_dev_d], sk[per_dev_d : per_dev_d + per_dev_r]
    gains = jnp.pad(sk[per_dev_d + kv_pad : per_dev_d + kv_pad + 2, :d_rows], ((0, 6), (0, 0)))

    adapt = jnp.stack(
        [
            part_ga,
            part_ua,
            dot_t(grad_wq.astype(BF16), query_expand),
        ]
    )
    expand = jnp.stack(
        [
            part_de.T,
            matmul(so[:d_rows].astype(BF16), out_adapt).T,
        ]
    )
    adapt = adapt.reshape(3, groups, per_dev_d, rank).transpose(1, 0, 2, 3).reshape(groups, -1, rank)
    expand = expand.reshape(2, groups, rank // groups, d_rows).transpose(1, 0, 2, 3).reshape(groups, -1, d_rows)
    expand = jnp.pad(expand, ((0, 0), (0, 0), (0, rank - d_rows)))
    small_gains = jnp.pad(
        gains[:, :d_rows].reshape(8, groups, per_dev_d).transpose(1, 0, 2), ((0, 0), (0, 8), (0, rank - per_dev_d))
    )
    small = jnp.concatenate([adapt, small_gains, expand], axis=1).astype(BF16)
    n_adapt = 3 * per_dev_d
    (small_sum,), = communicate(
        topo, "sum_small", 8, Scatter(topo, "dp", small, [(0, small.shape[1], "cx")])
    )
    per_seq = rank // groups // n_seq
    across = small_sum[n_adapt + 16 :, :d_rows].reshape(2, n_seq, per_seq, d_rows).transpose(1, 0, 2, 3)
    across = across.reshape(n_seq, 2 * per_seq, d_rows)
    (own_adapt, own_expand), = communicate(
        topo, "finish", 9, Finish(topo, small_sum[: n_adapt + 16], across)
    )
    grad_ga, grad_ua, grad_qa = own_adapt[:n_adapt].reshape(3, per_dev_d, rank)
    grad_gain_attn = own_adapt[n_adapt, :per_dev_d]
    grad_gain_mlp = own_adapt[n_adapt + 1, :per_dev_d]
    own_expand = own_expand.reshape(n_seq, 2, per_seq, d_rows).transpose(1, 2, 0, 3).reshape(2, per_seq, width)
    grad_de, grad_oe = own_expand[0], own_expand[1]
    grad_wk, grad_wv = grad_wkv[:, :HD], grad_wkv[:, HD:]
    grad_ka = dot_t(grad_wk.astype(BF16), key_expand)
    grad_va = dot_t(grad_wv.astype(BF16), value_expand)
    grad_ke, grad_ve = grad_kve[:, :HD], grad_kve[:, HD:]
    return (
        result_rows[None, None], grad_rows[None, None],
        grad_gain_attn, grad_gain_mlp,
        grad_wq, grad_wk, grad_wv, grad_wo, grad_wg, grad_wu, grad_wd,
        grad_qa, grad_qe, grad_ka, grad_ke, grad_va, grad_ve, grad_oa, grad_oe,
        grad_ga, grad_ge, grad_ua, grad_ue, grad_da, grad_de,
    )


def solution(mesh):
    topo = Topo(mesh.shape["dp"], mesh.shape["seq"])
    both = ("dp", "seq")
    in_specs = (
        P(None, "dp", "seq", None), P(None, "dp", "seq"), P(None, "dp", "seq", None),
        P(), P(), P(None, "dp"), P(), P(), P("dp", None), P(None, "dp"), P(None, "dp"), P("dp", None),
        P(), P(None, "dp"), P(), P(), P(), P(), P("dp", None), P(),
        P(), P(None, "dp"), P(), P(None, "dp"), P("dp", None), P(),
    )
    out_specs = (
        P(None, "dp", "seq", None), P(None, "dp", "seq", None), P(both), P(both),
        P("seq", "dp"), P(both, None), P(both, None), P("dp", "seq"), P("seq", "dp"), P("seq", "dp"), P("dp", "seq"),
        P(both, None), P("seq", "dp"), P(both, None), P(both, None), P(both, None), P(both, None),
        P("dp", "seq"), P(both, None), P(both, None), P("seq", "dp"), P(both, None), P("seq", "dp"),
        P("dp", "seq"), P(both, None),
    )
    return jax.shard_map(
        lambda *args: local(topo, *args), mesh=mesh, in_specs=in_specs, out_specs=out_specs, check_vma=False
    )
```

time: 856 us -> 649 us (0.76)
  local copies, waits for them, and re-layouts: 120 us -> 33.7 us
  Pallas kernels: 633 us -> 573 us
  matrix products: 66.7 us -> 17 us
    pallas_call x0 -> x2, Pallas kernels: none -> 211 us  [the longest x1 202 us: attention_back(): pl.pallas_call(kernel, name='attention_back', out_shape=out_shape, in_spe...]
    pallas_call x8 -> x4, Pallas kernels: 313 us -> 114 us  [communicate(): pl.pallas_call(kernel, name=name, out_shape=[s for op in ops for s in op....]
    pallas_call x1, Pallas kernels: 321 us -> 247 us  [feed_forward(): pl.pallas_call(kernel, name='feed_forward', out_shape=out_shape, in_specs...]
    slice x13 -> x3, local copies, waits for them, and re-layouts: 32.5 us -> 2.21 us  [the longest x2 1.51 us: local(): grad_wq, grad_qe = (sq[:d_rows], sq[d_rows:])]
    unnamed x157 -> x111, local copies, waits for them, and re-layouts: 35.1 us -> 10.2 us
    dot_general x7 -> x0, matrix products: 19 us -> none  [t_dot(): lax.dot_general(left, right, (((0,), (0,)), ((), ())), preferred_element_...]
    dot_general x10 -> x3, matrix products: 18.9 us -> 1.89 us  [dot_t(): lax.dot_general(left, right, (((1,), (1,)), ((), ())), preferred_element_...]
    convert_element_type x6 -> x1, local copies, waits for them, and re-layouts: 17.5 us -> 0.54 us  [local(): rotate(queries.reshape(groups, rows, heads_dev, HD), cosine_heads, sine_h...]
where the time goes in v3:
time: 649 us; the launch traced here: 644 us
  Pallas kernels  573 us (88%)
  local copies, waits for them, and re-layouts  33.7 us (5%)
  other arithmetic  18.8 us (3%)
  matrix products  17 us (3%)
    pallas_call x1, Pallas kernels, feed_forward(): pl.pallas_call(kernel, name='feed_forward', out_shape=out_shape, in_specs...  247 us
    pallas_call x1, Pallas kernels, attention_back(): pl.pallas_call(kernel, name='attention_back', out_shape=out_shape, in_spe...  202 us
    pallas_call x4, Pallas kernels, communicate(): pl.pallas_call(kernel, name=name, out_shape=[s for op in ops for s in op....  114 us

profile of v3, /device:TPU:0, one launch (start us, length us, event | category | flops | bytes accessed | tf_op | source)
XLA Modules:
  0.0 644.0 jit_solution(2934897104449774113)
XLA Ops:
  0.7 1.4 fusion.15
  2.1 0.5 fusion.27
  2.6 2.2 convert_multiply_fusion
  4.9 0.4 fusion.1.refs_17_
  5.3 1.0 copy-done.8
  6.3 0.3 fusion.33
  6.6 0.3 multiply_cosine_fusion
  7.0 0.4 fusion.2.refs_18_
  7.5 0.9 copy-done.7
  8.4 0.3 convolution_convert_fusion.3
  8.8 0.7 pad_maximum_fusion.1.refs_1_
  9.4 0.6 scatter.4.refs_2_
  10.0 65.1 %gather_attention.1 = (bf16[4,128,2048]{2,1,0:T(8,128)(2,1)}, bf16[32,128,512]{2,1,0:T(8,128)(2,1)}, f32[32,16,128]{2,1,0:T(8,128)}, bf16[16,128,2048]{2,1,0:T(8,128)(2,1)}) custom-call(bf16[128,2048]{1,0:T(8,128)(2,1)} %copy-done.9, bf16[128,512]{1,0:T(8,128)(2,1)} %pad_maximum_fusion.1.refs_1_, f32[16,128]{1,0:T(8,128)} %scatter.4.refs_2_, ...), custom_call_target="tpu_custom_call" | custom-call | tf_op jit(solution)/shard_map/gather_attention/pallas_call | solution.py:624
  75.1 0.9 slice_reduce_fusion
  76.2 1.9 compare_and_fusion
  78.1 2.3 add_convert_fusion.1.refs_16_
  80.4 2.6 copy.112
  83.0 3.6 fusion.5
  86.9 0.8 fusion
  87.7 1.0 exponential_reduce_fusion
  88.7 0.6 copy-done.47
  89.3 2.3 fusion.14
  91.6 2.1 copy.91
  93.7 1.1 copy.113
  94.8 1.8 add_convert_fusion.refs_15_
  96.7 2.6 convolution_convert_fusion
  99.3 19.5 %sum_attention.1 = f32[128,2048]{1,0:T(8,128)} custom-call(bf16[4,128,2048]{2,1,0:T(8,128)(2,1)} %bitcast.142), custom_call_target="tpu_custom_call" | custom-call | tf_op jit(solution)/shard_map/sum_attention/pallas_call | solution.py:624
  118.8 1.4 multiply_reduce_fusion.2
  120.3 0.9 copy-done.5
  121.2 0.9 multiply_convert_fusion.refs_0_
  122.2 247.1 %feed_forward.1 = (bf16[16,128,2048]{2,1,0:T(8,128)(2,1)}, bf16[16,128,2048]{2,1,0:T(8,128)(2,1)}, bf16[4,288,1024]{2,1,0:T(8,128)(2,1)}, bf16[4,288,1024]{2,1,0...) custom-call(bf16[128,2048]{1,0:T(8,128)(2,1)} %multiply_convert_fusi, ...), custom_call_target="tpu_custom_call" | custom-call | flops 154618822656 | bytes 134217728 | tf_op jit(solution)/shard_map/feed_forward/pallas_call | solution.py:1053
  369.4 2.3 multiply_reduce_fusion
  371.7 3.0 fusion.28
  374.7 1.1 add.111.refs_5_
  375.9 0.5 copy.92
  376.5 0.9 copy.114
  377.4 0.7 fusion.53
  378.1 0.7 copy.94.refs_6_
  378.8 1.3 constant_dynamic-slice_fusion
  380.1 0.7 copy.95.refs_10_
  380.9 201.6 %attention_back.1 = (bf16[128,2048]{1,0:T(8,128)(2,1)}, f32[288,512]{1,0:T(8,128)}, f32[288,512]{1,0:T(8,128)}, f32[96,512]{1,0:T(8,128)}, bf16[4,288,1024]{2,1,...) custom-call(bf16[128,2048]{1,0:T(8,128)(2,1)} %get-tuple-element.168.refs_0_, ...), custom_call_target="tpu_custom_call" | custom-call | tf_op jit(solution)/shard_map/attention_back/pallas_call | solution.py:1301
  582.5 9.8 %unfold.1 = (f32[256,4096]{1,0:T(8,128)}, f32[32,4096]{1,0:T(8,128)}, f32[256,4096]{1,0:T(8,128)}, f32[32,4096]{1,0:T(8,128)}, f32[4096,256]{1,0:T(8,128)}, /*in...) custom-call(bf16[4,288,1024]{2,1,0:T(8,128)(2,1)} %get-tuple-element.74.dg_ref, ...), custom_call_target="tpu_custom_call" | custom-call | tf_op jit(solution)/shard_map/unfold/pallas_call | solution.py:1341
  592.3 1.3 copy-done.2
  594.1 0.8 pad_maximum_fusion
  595.0 0.3 convolution_convert_fusion.1
  595.3 0.7 copy.101
  596.1 0.7 slice.152
  596.9 2.0 fusion.17.refs_0_
  598.8 10.2 %sum_small.1 = f32[336,256]{1,0:T(8,128)} custom-call(bf16[4,336,256]{2,1,0:T(8,128)(2,1)} %fusion.17.refs_0_), custom_call_target="tpu_custom_call" | custom-call | tf_op jit(solution)/shard_map/sum_small/pallas_call | solution.py:624
  609.0 0.9 slice.108
  609.9 0.7 copy.117
  610.6 1.6 slice.107.refs_0_
  612.2 19.5 %finish.1 = (f32[208,256]{1,0:T(8,128)}, f32[8,16,256]{2,1,0:T(8,128)}) custom-call(f32[208,256]{1,0:T(8,128)} %slice.107.refs_0_, f32[8,16,256]{2,1,0:T(8,128)} %bitcast.153), custom_call_target="tpu_custom_call" | custom-call | tf_op jit(solution)/shard_map/finish/pallas_call | solution.py:624
  631.8 1.6 fusion.29
  633.4 1.5 fusion.32
  634.9 1.3 slice_bitcast_fusion.10
  636.2 1.4 copy.104
  637.6 1.0 copy.103
  638.6 0.8 fusion.20
  639.5 0.8 fusion.22
  640.3 1.5 slice.113
  641.8 0.6 slice_bitcast_fusion.9
  642.4 0.6 fusion.30
  643.0 0.8 copy.120
  (124 shorter events, 1.3 us)
Async XLA Ops:
  0.7 77.4 %copy-start = (bf16[256,512]{1,0:T(8,128)(2,1)S(1)}, bf16[256,512]{1,0:T(8,128)(2,1)}, u32[]{:S(2)}) copy-start(bf16[256,512]{1,0:T(8,128)(2,1)} %param.41) | copy-start | bytes 786436
  0.7 4.2 copy-start.26
  0.7 4.1 copy-start.18
  0.7 4.1 copy-start.38
  4.8 2.7 copy-start.9
  4.9 2.2 copy-start.16
  4.9 2.2 copy-start.27
  4.9 2.1 copy-start.36
  5.3 1.0 copy-start.8
  7.0 79.7 %copy-start.33 = (f32[128,128]{1,0:T(8,128)}, f32[128,128]{1,0:T(8,128)S(1)}, u32[]{:S(2)}) copy-start(f32[128,128]{1,0:T(8,128)S(1)} %get-tuple-element.190.refs_13_) | copy-start | bytes 196612
  7.0 79.7 %copy-start.34 = (f32[128,128]{1,0:T(8,128)}, f32[128,128]{1,0:T(8,128)S(1)}, u32[]{:S(2)}) copy-start(f32[128,128]{1,0:T(8,128)S(1)} %get-tuple-element.191.refs_14_) | copy-start | bytes 196612
  7.0 2.4 copy-start.52
  7.5 1.0 copy-start.7
  8.4 69.6 %copy-start.14 = (bf16[2048,256]{1,0:T(8,128)(2,1)S(1)}, bf16[2048,256]{1,0:T(8,128)(2,1)}, u32[]{:S(2)}) copy-start(bf16[2048,256]{1,0:T(8,128)(2,1)} %refs_19_.1) | copy-start | bytes 3145732
  76.1 2.0 copy-start.43
  80.4 6.3 copy-start.4
  83.0 3.9 copy-start.13
  83.0 3.9 copy-start.22
  86.9 0.8 copy-start.28
  86.9 0.8 copy-start.30
  88.7 0.6 copy-start.47
  89.3 5.5 copy-start.24
  91.6 3.3 copy-start.15
  94.8 1.9 copy-start.25
  96.7 2.6 copy-start.10
  99.3 19.5 %copy-start.11 = (bf16[1,1,128,2048]{3,2,1,0:T(8,128)(2,1)S(1)}, bf16[1,1,128,2048]{3,2,1,0:T(8,128)(2,1)}, u32[]{:S(2)}) copy-start(bf16[1,1,128,2048]{3,2,1,0:T(8,128)(2,1)} %param.28) | copy-start | bytes 1572868
  99.3 22.0 %copy-start.45 = (f32[2048]{0:T(1024)S(1)}, f32[2048]{0:T(1024)}, u32[]{:S(2)}) copy-start(f32[2048]{0:T(1024)} %param.32) | copy-start | bytes 24580
  120.3 1.0 copy-start.5
  120.3 1.9 copy-start.49
  122.2 247.2 %copy-start.6 = (f32[128,2048]{1,0:T(8,128)S(1)}, f32[128,2048]{1,0:T(8,128)}, u32[]{:S(2)}) copy-start(f32[128,2048]{1,0:T(8,128)} %copy-done.5) | copy-start | bytes 3145732
  122.2 247.2 %copy-start.46 = (f32[2048]{0:T(1024)S(1)}, f32[2048]{0:T(1024)}, u32[]{:S(2)}) copy-start(f32[2048]{0:T(1024)} %param.32) | copy-start | bytes 24580
  122.2 247.2 %copy-start.50 = (f32[128]{0:T(128)S(1)}, f32[128]{0:T(128)}, u32[]{:S(2)}) copy-start(f32[128]{0:T(128)} %copy-done.49) | copy-start | bytes 1540
  369.4 2.3 copy-start.12
  369.4 2.3 copy-start.21
  371.7 3.0 copy-start.48
  371.7 4.2 copy-start.29
  371.7 4.2 copy-start.31
  374.7 4.1 copy-start.17
  374.7 4.1 copy-start.19
  375.9 4.2 copy-start.51
  380.9 201.6 %copy-start.1 = (bf16[256,4096]{1,0:T(8,128)(2,1)S(1)}, bf16[256,4096]{1,0:T(8,128)(2,1)}, u32[]{:S(2)}) copy-start(bf16[256,4096]{1,0:T(8,128)(2,1)} %ge_ref.1) | copy-start | bytes 6291460
  582.5 11.2 %copy-start.35 = (f32[288,512]{1,0:T(8,128)S(1)}, f32[288,512]{1,0:T(8,128)}, u32[]{:S(2)}) copy-start(f32[288,512]{1,0:T(8,128)} %get-tuple-element.79) | copy-start | bytes 1769476
  592.3 1.3 copy-start.2
  593.7 1.3 copy-start.20
  593.7 1.3 copy-start.32
  593.8 5.1 copy-start.23
  595.3 40.8 %copy-start.3 = (f32[4096,32]{1,0:T(8,128)S(1)}, f32[4096,32]{1,0:T(8,128)}, u32[]{:S(2)}) copy-start(f32[4096,32]{1,0:T(8,128)} %copy-done.2) | copy-start | bytes 1572868
  636.2 2.4 copy-start.44
  636.2 2.5 copy-start.37
  636.2 3.3 copy-start.39
  637.6 5.4 copy-start.40
  638.6 5.2 copy-start.41
  638.6 5.2 copy-start.42

commit v4 on v3

--- a/solution.py
+++ b/solution.py
@@ -105,15 +105,16 @@
 
 
 class Gather:
-    def __init__(self, topo, group, x, parts, beyond=None, need=None):
+    def __init__(self, topo, group, x, parts, beyond=None, need=None, keep=True):
         self.topo, self.group, self.parts, self.beyond = topo, group, parts, beyond
+        self.keep = keep and not beyond
         self.slots = "half" if beyond else group
         self.need = need or (lambda dims, key: 0)
         self.inputs = [x]
         rows, cols = x.shape
         n = topo.group_size(group)
         self.outputs = [jax.ShapeDtypeStruct((topo.group_size(self.slots), rows, cols), x.dtype)]
-        self.in_specs = [pl.BlockSpec(memory_space=pl.ANY)]
+        self.in_specs = [pl.BlockSpec(memory_space=pltpu.VMEM)]
         self.out_specs = [pl.BlockSpec(memory_space=pl.ANY)]
         self.scratch = [
             pltpu.SemaphoreType.DMA((len(parts), n)),
@@ -172,7 +173,7 @@
 
             def step(n=n, part=part, key=key, sends=sends):
                 row, rows, order = self.parts[part]
-                if n == 0 and not self.beyond:
+                if n == 0 and self.keep:
                     own().start()
                 if any(key):
                     slot = topo.index(topo.moved(at, order, key, -1), self.slots)
@@ -186,7 +187,7 @@
         def end():
             for send in sent:
                 copy(*send).wait_send()
-            if not self.beyond:
+            if self.keep:
                 own().wait()
 
         return steps, [end]
@@ -448,8 +449,8 @@
 
 
 class Exchange:
-    def __init__(self, topo, group, x):
-        self.topo, self.group = topo, group
+    def __init__(self, topo, group, x, keep=True):
+        self.topo, self.group, self.keep = topo, group, keep
         self.inputs = [x]
         n = x.shape[0]
         assert n == topo.group_size(group)
@@ -488,7 +489,8 @@
             return remote(source, out_ref.at[me], send_sem.at[i], recv_sem.at[i], topo.device(there))
 
         def start():
-            own().start()
+            if self.keep:
+                own().start()
             for i in range(len(offsets)):
                 send(i).start()
 
@@ -499,7 +501,8 @@
         def end():
             for i in range(len(offsets)):
                 send(i).wait_send()
-            own().wait()
+            if self.keep:
+                own().wait()
 
         return [start] + [lambda i=i: wait(i) for i in range(len(offsets))], [end]
 
@@ -745,24 +748,23 @@
         return chunk_of[tuple(at_dim.get(d, 0) for d in dims)]
 
     near = row_parts(rows, ("xlbc", "lbxc", "bxlc"), (1, 1, 1))
-    far = row_parts(rows, ("hxlbc", "hlbxc", "hbxlc"), (1, 1, 1))
-    gather_n = Gather(topo, "half", normed, near, need=need)
-    far_n = Gather(topo, "all", normed, far, beyond="h", need=need)
-    far_g = Gather(topo, "all", grads, far, beyond="h", need=need)
-    thirds = row_parts(rows, ("cxbl", "cblx", "clxb"), (1, 1, 1))
-    sum_n = SlimScatter(topo, "half", (half, rows, width), BF16, thirds)
-    sum_d = SlimScatter(topo, "half", (half, rows, width), BF16, thirds)
-    comm = [gather_n, far_n, far_g, sum_n, sum_d]
+    both = jnp.concatenate([normed, grads], axis=0)
+    far = row_parts(2 * rows, ("hxlbc", "hlbxc", "hbxlc"), (1, 1, 1))
+    gather_n = Gather(topo, "half", normed, near, need=need, keep=False)
+    gather_far = Gather(topo, "all", both, far, beyond="h", need=need)
+    thirds = row_parts(2 * rows, ("cxlb", "cbxl", "clbx"), (1, 1, 1))
+    sum_both = SlimScatter(topo, "half", (half, 2 * rows, width), BF16, thirds)
+    comm = [gather_n, gather_far, sum_both]
 
     inputs = [
-        normed, grads, grads_half, w_gate, w_up, w_down,
+        normed, both, grads_half, w_gate, w_up, w_down,
         gate_adapt, gate_expand, up_adapt, up_expand, down_adapt, down_expand,
     ]
-    part = jax.ShapeDtypeStruct((half, rows, width), BF16)
+    part = jax.ShapeDtypeStruct((half, 2 * rows, width), BF16)
     grad = jax.ShapeDtypeStruct((quad, d_rows + r_rows, units), BF16)
     any_spec = pl.BlockSpec(memory_space=pl.ANY)
-    out_shape = [part, part, grad, grad, grad]
-    out_specs = [any_spec] * 5
+    out_shape = [part, grad, grad, grad]
+    out_specs = [any_spec] * 4
     scratch = [
         pltpu.VMEM((width, units), BF16), pltpu.VMEM((width, units), BF16), pltpu.VMEM((units, width), BF16),
         pltpu.VMEM((width, rank), BF16), pltpu.VMEM((rank, units), BF16),
@@ -781,7 +783,7 @@
         pltpu.SemaphoreType.DMA((3,)),
     ]
     n_own = len(scratch)
-    shared = sum_n.shared_scratch() + sum_d.shared_scratch()
+    shared = sum_both.shared_scratch()
     scratch = scratch + shared
     for op in comm:
         out_shape = out_shape + op.outputs
@@ -791,9 +793,9 @@
     def kernel(*refs):
         refs = list(refs)
         (
-            n_hbm, g_hbm, g_half, wg_hbm, wu_hbm, wd_hbm, ga_hbm, ge_hbm, ua_hbm, ue_hbm, da_hbm, de_hbm,
+            n_hbm, both_hbm, g_half, wg_hbm, wu_hbm, wd_hbm, ga_hbm, ge_hbm, ua_hbm, ue_hbm, da_hbm, de_hbm,
         ) = [refs.pop(0) for _ in inputs]
-        down_part, gn_part, dg_out, du_out, dd_out = [refs.pop(0) for _ in range(5)]
+        part_hbm, dg_out, du_out, dd_out = [refs.pop(0) for _ in range(4)]
         op_outs = [[refs.pop(0) for _ in op.outputs] for op in comm]
         (
             wg, wu, wd, ga, ge, ua, ue, da, de, acc_g, acc_u, acc_d, acts, low_s, n_buf, g_buf, down_st, gn_st,
@@ -827,14 +829,12 @@
             cp.start()
 
         greet(topo, comm)
-        gathers = (gather_n, far_n, far_g)
-        all_steps = [
-            op.steps(at, [x], o, sc) for op, x, o, sc in zip(gathers, (n_hbm, n_hbm, g_hbm), op_outs, op_scratch)
-        ]
+        gathers = (gather_n, gather_far)
+        all_steps = [op.steps(at, [x], o, sc) for op, x, o, sc in zip(gathers, (n_hbm, both_hbm), op_outs, op_scratch)]
         ranked = []
         for g, (op, (steps_g, _)) in enumerate(zip(gathers, all_steps)):
             for i, (f, (p, k)) in enumerate(zip(steps_g, op.work())):
-                when = NEAR_US * i / len(steps_g) - 20.0 if g == 0 else FAR_AT + (g + 2 * i) * FAR_US
+                when = NEAR_US * i / len(steps_g) - 20.0 if g == 0 else FAR_AT + i * FAR_US
                 ranked.append((when if any(k) or g else -1e3, g, i, f, need(op.parts[p][2], k)))
         ranked.sort(key=lambda w: w[:3])
         steps = [(f, chunk) for _, _, _, f, chunk in ranked]
@@ -883,9 +883,13 @@
                 origin = topo.moved(at, dims, key_of(c, i), -1)
                 r = pl.ds(i * rows, rows)
                 in_half = topo.index(origin, "half")
-                n_src, g_src = (op_outs[1][0], op_outs[2][0]) if other else (op_outs[0][0], g_half)
-                copies.append(pltpu.make_async_copy(n_src.at[in_half], n_buf.at[slot, r], load_sem.at[slot, 0, i]))
-                copies.append(pltpu.make_async_copy(g_src.at[in_half], g_buf.at[slot, r], load_sem.at[slot, 1, i]))
+                if other:
+                    n_src = op_outs[1][0].at[in_half, pl.ds(0, rows)]
+                    g_src = op_outs[1][0].at[in_half, pl.ds(rows, rows)]
+                else:
+                    n_src, g_src = op_outs[0][0].at[in_half], g_half.at[in_half]
+                copies.append(pltpu.make_async_copy(n_src, n_buf.at[slot, r], load_sem.at[slot, 0, i]))
+                copies.append(pltpu.make_async_copy(g_src, g_buf.at[slot, r], load_sem.at[slot, 1, i]))
             return copies
 
         def first_copies():
@@ -899,8 +903,9 @@
             for i in range(per_chunk):
                 slot = topo.index(topo.moved(at, dims, key_of(c, i), -1), "half")
                 r = pl.ds(i * rows, rows)
-                copies.append(pltpu.make_async_copy(down_st.at[r], down_part.at[slot], store_sem.at[0, i]))
-                copies.append(pltpu.make_async_copy(gn_st.at[r], gn_part.at[slot], store_sem.at[1, i]))
+                for k, source in enumerate((gn_st, down_st)):
+                    place = part_hbm.at[slot, pl.ds(k * rows, rows)]
+                    copies.append(pltpu.make_async_copy(source.at[r], place, store_sem.at[k, i]))
             return copies
 
         n_one, n_two, n_three = units // block, width // block, half_width // block
@@ -924,17 +929,13 @@
                         target = upto(c + 1, target)
                     slots[other, kind][(c - own if other else c) * n + i] += [f for f, _ in steps[done:target]]
                     done = target
-        sum_a = sum_n.steps(at, gn_part, op_outs[3], op_scratch[3], shared_refs[:3])
-        sum_b = sum_d.steps(at, down_part, op_outs[4], op_scratch[4], shared_refs[3:])
-        sums = [sum_a[0][0], sum_b[0][0]]
-        for i in range(1, max(len(sum_a[0]), len(sum_b[0]))):
-            sums += sum_a[0][i : i + 1] + sum_b[0][i : i + 1]
+        sums, sums_end = sum_both.steps(at, part_hbm, op_outs[2], op_scratch[2], shared_refs)
         clock, summed = 0.0, 0
         for c in range(own):
             for kind, n, cost in kinds[True]:
                 for i in range(n):
                     clock += cost
-                    target = min(len(sums), 2 + int(max(clock - 3.0, 0.0) / SUM_US))
+                    target = min(len(sums), 1 + int(max(clock - 3.0, 0.0) / SUM_US))
                     if kind != "pre":
                         slots[True, kind][c * n + i] += sums[summed:target]
                         summed = target
@@ -1046,7 +1047,7 @@
             f()
         for cp in pending:
             cp.wait()
-        for f in [f for _, end in all_steps for f in end] + sum_a[1] + sum_b[1]:
+        for f in [f for _, end in all_steps for f in end] + sums_end:
             f()
 
     flops = 2 * rows * topo.n_dp * topo.n_seq * units * width * 9
@@ -1062,15 +1063,16 @@
         ),
         cost_estimate=pl.CostEstimate(flops=flops, bytes_accessed=1 << 27, transcendentals=0),
     )(*inputs)
-    dg, du, dd = results[2:5]
-    skip = 5 + sum(len(op.outputs) for op in (gather_n, far_n, far_g))
-    return results[skip + len(sum_n.outputs)], results[skip], dg, du, dd
-
-
+    dg, du, dd = results[1:4]
+    total = results[4 + len(gather_n.outputs) + len(gather_far.outputs)]
+    return total[rows:], total[:rows], dg, du, dd
+
+
+KV_STEPS = 3
 NEAR_US = 45.0
 FAR_AT = 5.0
-FAR_US = 0.55
-SUM_US = 1.1
+FAR_US = 1.4
+SUM_US = 2.4
 
 
 def attention_back(
@@ -1094,14 +1096,14 @@
 
     gather_g = Gather(topo, "dp", grad_branch, [(0, rows, "xc")])
     gather_kv = Gather(topo, "dp", jax.ShapeDtypeStruct((rows, 2 * HD), BF16), [(0, rows, "xc")])
-    swaps = [Exchange(topo, "quad", a) for a in (dg, du, dd)]
-    seq_parts = lambda n: row_parts(n, ("blh", "lhb"), (9, 5))
+    swaps = [Exchange(topo, "quad", a, keep=False) for a in (dg, du, dd)]
+    seq_parts = lambda n: row_parts(n, ("blh", "lbh"), (2, 1))
     w_shape = (n_seq, d_rows + r_rows, head_cols)
     sum_o = VScatter(topo, "seq", w_shape, BF16, seq_parts(d_rows + r_rows))
     sum_q = VScatter(topo, "seq", w_shape, BF16, seq_parts(d_rows + r_rows))
     sum_k = VScatter(topo, "seq", (n_seq, kv_rows, 2 * HD), BF16, seq_parts(kv_rows))
     kv_shape = (groups * n_seq, rows, 2 * HD)
-    sum_kv = VScatter(topo, "all", kv_shape, BF16, row_parts(rows, ("cxblh", "cblhx"), (1, 1)))
+    sum_kv = VScatter(topo, "all", kv_shape, BF16, row_parts(rows, ("cxblh", "cblxh"), (1, 1)))
     sum_n = VScatter(topo, "dp", (groups, rows, width), BF16, [(0, rows, "cx")])
 
     inputs = [
@@ -1122,7 +1124,7 @@
     ] + [op.outputs[0] for op in swaps]
     out_specs = [vmem] * 4 + [anywhere] * 3
     if big:
-        sum_kv = SlimScatter(topo, "all", kv_shape, BF16, row_parts(rows, ("cxblh", "cblhx"), (1, 1)))
+        sum_kv = SlimScatter(topo, "all", kv_shape, BF16, row_parts(rows, ("cxblh", "cblxh"), (1, 1)))
         out_shape = out_shape + [jax.ShapeDtypeStruct(kv_shape, BF16)] + sum_kv.outputs
         out_specs = out_specs + [anywhere] + sum_kv.out_specs
     scratch = [
@@ -1171,9 +1173,9 @@
         moves[0].run()
         get_g.finish()
         flat = lambda ref: ref[...].reshape(tokens, ref.shape[-1])
-        moves[1].run()
 
         gh[...] = dot_t(flat(ga), wo_r[...]).astype(BF16)
+
         for j in range(n_seq):
             part = t_dot(ga[:, :, j * d_rows : (j + 1) * d_rows].reshape(tokens, d_rows), hout[...])
             xo[j, :d_rows, :] = part.astype(BF16)
@@ -1229,32 +1231,38 @@
                 gq[r, h * HD : (h + 1) * HD] = rotate(
                     d_q[h * rows : (h + 1) * rows], cos[...], -sin[...]
                 ).astype(BF16)
-            get_o.run(3)
+            if s + 2 >= groups:
+                get_o.run(4 if s + 2 == groups else 2)
         if big:
             get_kv = Steps(sum_kv.steps(at, kv_outs[0], kv_outs[1:], op_scratch[8], shared_refs[:3]))
         else:
             get_kv = Steps(sum_kv.steps(at, xkv, kv_sum, op_scratch[8]))
         get_kv.run()
+        moves[1].run()
         for s in range(groups):
             xn[s] = dot_t(gq[s * rows : (s + 1) * rows, :], wq_r[...]).astype(BF16)
         get_n = Steps(sum_n.steps(at, xn, n_sum, op_scratch[9]))
         get_n.run()
 
+        def poll():
+            get_kv.run(1)
+
         for j in range(n_seq):
             part = t_dot(norm_all[:, :, j * d_rows : (j + 1) * d_rows].reshape(tokens, d_rows), gq[...])
             xq[j, :d_rows, :] = part.astype(BF16)
-            if j % 2:
-                get_kv.run(2)
-                get_n.run(1)
+            poll()
         low = matmul(flat(norm_all), qa[...]).astype(BF16)
         part = t_dot(low, gq[...]).astype(BF16)
         for j in range(n_seq):
             xq[j, d_rows:, :] = part[j * r_rows : (j + 1) * r_rows, :]
-        get_kv.finish()
         get_q = Steps(sum_q.steps(at, xq, sq_out, op_scratch[6]))
         get_q.run()
+        get_n.run(2)
+        while get_kv.todo:
+            get_kv.run(KV_STEPS)
+            get_o.run()
+        get_n.finish()
         moves[2].run()
-        get_n.finish()
 
         total_kv = kv_outs[1] if big else kv_sum
         gk = rotate(total_kv[:, :HD], cos[...], -sin[...]).astype(BF16)
@@ -1268,8 +1276,11 @@
         gain_attn_term = jnp.sum(grad_normed * u_rows, axis=0, keepdims=True)
         grad_unit = grad_normed * gain[...]
         inner = jnp.mean(grad_unit * u_rows, axis=-1, keepdims=True)
+        get_o.run(2)
+        get_q.run(2)
         grad_rows[...] = (gmid[...] + rms[...] * (grad_unit - u_rows * inner)).astype(BF16)
         get_kv2.finish()
+        get_q.run(2)
         mine = pl.ds(pl.multiple_of(dp * share_d, share_d), share_d)
         part_rows = norm_all[:, :, mine].reshape(tokens, share_d)
         low_k = matmul(flat(norm_all), ka[...]).astype(BF16)
@@ -1292,9 +1303,10 @@
             ).astype(BF16)
         get_k = Steps(sum_k.steps(at, xk, sk_out, op_scratch[7]))
         get_k.run()
-        get_o.finish()
-        get_q.finish()
-        get_k.finish()
+        left = [get_o, get_q, get_k]
+        while any(g.todo for g in left):
+            for g in left:
+                g.run()
         for move in moves:
             move.finish()
 
@@ -1312,44 +1324,55 @@
     return results[:7]
 
 
-def unfold(d_rows, dg, du, dd, gate_expand, up_expand, down_adapt):
+def unfold(d_rows, member, owns, dg, du, dd, gate_expand, up_expand, down_adapt):
     quad, total, units = dg.shape
     rank = gate_expand.shape[0]
     r_rows = total - d_rows
 
-    def kernel(dg_ref, du_ref, dd_ref, ge_ref, ue_ref, da_ref, wg, eg, wu, eu, wd, ad, ga, ua, de):
+    def kernel(
+        me, dg_own, du_own, dd_own, dg_ref, du_ref, dd_ref, ge_ref, ue_ref, da_ref,
+        wg, eg, wu, eu, wd, ad, ga, ua, de, term_g, term_u, term_d,
+    ):
         first = pl.program_id(0) == 0
-        for src, w, e in ((dg_ref, wg, eg), (du_ref, wu, eu)):
-            w[...] = src[0, :d_rows, :].astype(F32)
-            e[...] = src[0, d_rows:, :].astype(F32)
-        both = dd_ref[0].astype(F32).T
+        mine = pl.program_id(0) == me[0]
+        for own, got, term in ((dg_own, dg_ref, term_g), (du_own, du_ref, term_u), (dd_own, dd_ref, term_d)):
+            term[...] = jnp.where(mine, own[0], got[0])
+        for src, w, e in ((term_g, wg, eg), (term_u, wu, eu)):
+            w[...] = src[:d_rows, :].astype(F32)
+            e[...] = src[d_rows:, :].astype(F32)
+        both = term_d[...].astype(F32).T
         wd[...] = both[:, :d_rows]
         ad[...] = both[:, d_rows:]
         for out, term in (
-            (ga, dot_t(dg_ref[0, :d_rows, :], ge_ref[...])),
-            (ua, dot_t(du_ref[0, :d_rows, :], ue_ref[...])),
-            (de, matmul(dd_ref[0, :d_rows, :], da_ref[...])),
+            (ga, dot_t(term_g[:d_rows, :], ge_ref[...])),
+            (ua, dot_t(term_u[:d_rows, :], ue_ref[...])),
+            (de, matmul(term_d[:d_rows, :], da_ref[...])),
         ):
             out[...] = jnp.where(first, term, term + out[...])
 
-    cols = lambda n: pl.BlockSpec((n, units), lambda q: (0, q))
-    side = lambda n: pl.BlockSpec((units, n), lambda q: (q, 0))
-    block = pl.BlockSpec((1, total, units), lambda q: (q, 0, 0))
-    kept = pl.BlockSpec((d_rows, rank), lambda q: (0, 0))
+    cols = lambda n: pl.BlockSpec((n, units), lambda q, me: (0, q))
+    side = lambda n: pl.BlockSpec((units, n), lambda q, me: (q, 0))
+    block = pl.BlockSpec((1, total, units), lambda q, me: (q, 0, 0))
+    own = pl.BlockSpec((1, total, units), lambda q, me: (me[0], 0, 0))
+    kept = pl.BlockSpec((d_rows, rank), lambda q, me: (0, 0))
     shape = lambda *s: jax.ShapeDtypeStruct(s, F32)
     all_units = quad * units
     return pl.pallas_call(
         kernel,
         name="unfold",
-        grid=(quad,),
-        in_specs=[block, block, block, cols(rank), cols(rank), side(rank)],
-        out_specs=[cols(d_rows), cols(r_rows), cols(d_rows), cols(r_rows), side(d_rows), side(r_rows)] + [kept] * 3,
+        grid_spec=pltpu.PrefetchScalarGridSpec(
+            num_scalar_prefetch=1,
+            grid=(quad,),
+            in_specs=[own] * 3 + [block] * 3 + [cols(rank), cols(rank), side(rank)],
+            out_specs=[cols(d_rows), cols(r_rows), cols(d_rows), cols(r_rows), side(d_rows), side(r_rows)] + [kept] * 3,
+            scratch_shapes=[pltpu.VMEM((total, units), BF16)] * 3,
+        ),
         out_shape=[
             shape(d_rows, all_units), shape(r_rows, all_units), shape(d_rows, all_units), shape(r_rows, all_units),
             shape(all_units, d_rows), shape(all_units, r_rows),
         ] + [shape(d_rows, rank)] * 3,
-        compiler_params=pltpu.CompilerParams(vmem_limit_bytes=48 << 20),
-    )(dg, du, dd, gate_expand, up_expand, down_adapt)
+        compiler_params=pltpu.CompilerParams(vmem_limit_bytes=56 << 20),
+    )(member, *owns, dg, du, dd, gate_expand, up_expand, down_adapt)
 
 
 def local(
@@ -1430,6 +1453,7 @@
     grad_middle = grad_rows_in.astype(F32) + grad_from_mlp
     grad_branch_attn = grad_middle.astype(BF16)
     my_kv_ranks = lambda a: lax.dynamic_slice_in_dim(a, dp * (rank // groups), rank // groups, 1)
+    owns = (dg, du, dd)
     grad_rows, so, sq, sk, dg, du, dd = attention_back(
         topo, 4, grad_branch_attn, grad_middle,
         query_rot.reshape(groups * rows, head_cols), heads_out, kv_all.reshape(groups * length, 2 * HD),
@@ -1441,7 +1465,7 @@
     per_dev_d, per_dev_r = d_rows // groups, r_rows // groups
     kv_pad = -(-per_dev_r // 16) * 16
     grad_wg, grad_ge, grad_wu, grad_ue, grad_wd, grad_da, part_ga, part_ua, part_de = unfold(
-        d_rows, dg, du, dd, gate_expand, up_expand, down_adapt
+        d_rows, lax.rem(seq, topo.group_size("quad")).reshape(1), owns, dg, du, dd, gate_expand, up_expand, down_adapt
     )
     grad_wq, grad_qe = sq[:d_rows], sq[d_rows:]
     grad_wo, grad_oa = so[:d_rows].T, so[d_rows:].T

time: 649 us -> 631 us (0.972)
  Pallas kernels: 573 us -> 555 us
    pallas_call x1, Pallas kernels: 202 us -> 177 us  [attention_back(): pl.pallas_call(kernel, name='attention_back', out_shape=out_shape, in_spe...]
where the time goes in v4:
time: 631 us; the launch traced here: 626 us
  Pallas kernels  555 us (88%)
  local copies, waits for them, and re-layouts  31.7 us (5%)
  other arithmetic  20.8 us (3%)
  matrix products  17.1 us (3%)
    pallas_call x1, Pallas kernels, feed_forward(): pl.pallas_call(kernel, name='feed_forward', out_shape=out_shape, in_specs...  251 us
    pallas_call x1, Pallas kernels, attention_back(): pl.pallas_call(kernel, name='attention_back', out_shape=out_shape, in_spe...  177 us
    pallas_call x4, Pallas kernels, communicate(): pl.pallas_call(kernel, name=name, out_shape=[s for op in ops for s in op....  115 us

profile of v4, /device:TPU:0, one launch (start us, length us, event | category | flops | bytes accessed | tf_op | source)
XLA Modules:
  0.0 626.3 jit_solution(8510404193813655687)
XLA Ops:
  0.7 1.4 fusion.15
  2.1 0.5 fusion.27
  2.6 2.3 convert_multiply_fusion
  4.9 0.4 fusion.1.refs_17_
  5.4 0.3 fusion.33
  5.7 0.3 multiply_cosine_fusion
  6.1 0.3 copy-done.5
  6.4 0.7 copy-done.26
  7.1 0.4 fusion.2.refs_18_
  7.5 1.0 copy-done.4
  8.5 0.3 convolution_convert_fusion.3
  8.8 0.7 pad_maximum_fusion.2.refs_1_
  9.5 0.6 scatter.4.refs_2_
  10.1 66.1 %gather_attention.1 = (bf16[4,128,2048]{2,1,0:T(8,128)(2,1)}, bf16[32,128,512]{2,1,0:T(8,128)(2,1)}, f32[32,16,128]{2,1,0:T(8,128)}, bf16[16,128,2048]{2,1,0:T(8,128)(2,1)}) custom-call(bf16[128,2048]{1,0:T(8,128)(2,1)} %copy-done.6, bf16[128,512]{1,0:T(8,128)(2,1)} %pad_maximum_fusion.2.refs_1_, f32[16,128]{1,0:T(8,128)} %scatter.4.refs_2_, ...), custom_call_target="tpu_custom_call" | custom-call | tf_op jit(solution)/shard_map/gather_attention/pallas_call | solution.py:627
  76.3 0.9 slice_reduce_fusion
  77.4 1.9 compare_and_fusion
  79.2 2.3 add_convert_fusion.1.refs_16_
  81.6 2.6 copy.112
  84.2 3.6 fusion.5
  88.1 0.8 fusion
  88.9 1.0 exponential_reduce_fusion
  89.9 0.6 copy-done.47
  90.5 2.3 fusion.14
  92.7 2.1 copy.91
  94.8 1.1 copy.113
  96.0 1.8 add_convert_fusion.refs_15_
  97.8 2.6 convolution_convert_fusion
  100.4 19.5 %sum_attention.1 = f32[128,2048]{1,0:T(8,128)} custom-call(bf16[4,128,2048]{2,1,0:T(8,128)(2,1)} %bitcast.143), custom_call_target="tpu_custom_call" | custom-call | tf_op jit(solution)/shard_map/sum_attention/pallas_call | solution.py:627
  120.0 1.5 multiply_reduce_fusion.2
  121.5 1.0 copy-done.2
  122.6 1.1 pad_maximum_fusion.refs_1_
  123.8 251.3 %feed_forward.1 = (bf16[16,256,2048]{2,1,0:T(8,128)(2,1)}, bf16[4,288,1024]{2,1,0:T(8,128)(2,1)}, bf16[4,288,1024]{2,1,0:T(8,128)(2,1)}, bf16[4,288,1024]{2,1,0:...) custom-call(bf16[128,2048]{1,0:T(8,128)(2,1)} %copy-done.23, ...), custom_call_target="tpu_custom_call" | custom-call | flops 154618822656 | bytes 134217728 | tf_op jit(solution)/shard_map/feed_forward/pallas_call | solution.py:1054
  375.1 2.2 multiply_reduce_fusion
  377.4 3.3 fusion.28
  380.7 1.1 add.111.refs_5_
  381.9 0.5 copy.92
  382.5 0.9 copy.114
  383.3 0.7 fusion.53
  384.0 0.7 copy.94.refs_6_
  384.8 1.3 constant_dynamic-slice_fusion
  386.1 0.7 copy.95.refs_10_
  386.8 176.9 %attention_back.1 = (bf16[128,2048]{1,0:T(8,128)(2,1)}, f32[288,512]{1,0:T(8,128)}, f32[288,512]{1,0:T(8,128)}, f32[96,512]{1,0:T(8,128)}, bf16[4,288,1024]{2,1,...) custom-call(bf16[128,2048]{1,0:T(8,128)(2,1)} %get-tuple-element.166.refs_0_, ...), custom_call_target="tpu_custom_call" | custom-call | tf_op jit(solution)/shard_map/attention_back/pallas_call | solution.py:1313
  563.8 11.8 %unfold.1 = (f32[256,4096]{1,0:T(8,128)}, f32[32,4096]{1,0:T(8,128)}, f32[256,4096]{1,0:T(8,128)}, f32[32,4096]{1,0:T(8,128)}, f32[4096,256]{1,0:T(8,128)}, /*in...) custom-call(s32[1]{0:T(128)} %bitcast.23.me, ...), custom_call_target="tpu_custom_call" | custom-call | tf_op jit(solution)/shard_map/unfold/pallas_call | solution.py:1360
  575.7 1.1 convert.47
  576.7 1.0 convert.48
  578.2 0.3 convolution_convert_fusion.1
  578.6 0.7 copy.101
  579.4 2.0 fusion.17.refs_0_
  581.4 9.5 %sum_small.1 = f32[336,256]{1,0:T(8,128)} custom-call(bf16[4,336,256]{2,1,0:T(8,128)(2,1)} %fusion.17.refs_0_), custom_call_target="tpu_custom_call" | custom-call | tf_op jit(solution)/shard_map/sum_small/pallas_call | solution.py:627
  590.9 0.9 slice.116
  591.9 0.7 copy.117
  592.5 1.6 slice.115.refs_0_
  594.1 19.7 %finish.1 = (f32[208,256]{1,0:T(8,128)}, f32[8,16,256]{2,1,0:T(8,128)}) custom-call(f32[208,256]{1,0:T(8,128)} %slice.115.refs_0_, f32[8,16,256]{2,1,0:T(8,128)} %bitcast.154), custom_call_target="tpu_custom_call" | custom-call | tf_op jit(solution)/shard_map/finish/pallas_call | solution.py:627
  613.9 1.6 fusion.29
  615.4 1.5 fusion.32
  617.0 1.3 slice_bitcast_fusion.10
  618.3 1.4 copy.104
  619.7 1.0 copy.103
  620.7 0.8 fusion.20
  621.5 0.8 fusion.22
  622.4 1.5 slice.121
  623.8 0.6 slice_bitcast_fusion.9
  624.5 0.6 fusion.30
  625.1 0.8 copy.120
  (125 shorter events, 1.4 us)
Async XLA Ops:
  0.7 78.6 %copy-start = (bf16[256,512]{1,0:T(8,128)(2,1)S(1)}, bf16[256,512]{1,0:T(8,128)(2,1)}, u32[]{:S(2)}) copy-start(bf16[256,512]{1,0:T(8,128)(2,1)} %param.41) | copy-start | bytes 786436
  0.7 4.2 copy-start.25
  0.7 4.2 copy-start.16
  0.7 4.2 copy-start.37
  4.9 2.6 copy-start.6
  4.9 1.5 copy-start.14
  4.9 2.1 copy-start.26
  4.9 2.1 copy-start.35
  5.4 1.0 copy-start.5
  6.1 81.8 %copy-start.32 = (f32[128,128]{1,0:T(8,128)}, f32[128,128]{1,0:T(8,128)S(1)}, u32[]{:S(2)}) copy-start(f32[128,128]{1,0:T(8,128)S(1)} %get-tuple-element.188.refs_13_) | copy-start | bytes 196612
  6.1 81.8 %copy-start.33 = (f32[128,128]{1,0:T(8,128)}, f32[128,128]{1,0:T(8,128)S(1)}, u32[]{:S(2)}) copy-start(f32[128,128]{1,0:T(8,128)S(1)} %get-tuple-element.189.refs_14_) | copy-start | bytes 196612
  7.1 2.4 copy-start.52
  7.5 1.0 copy-start.4
  8.5 70.7 %copy-start.12 = (bf16[2048,256]{1,0:T(8,128)(2,1)S(1)}, bf16[2048,256]{1,0:T(8,128)(2,1)}, u32[]{:S(2)}) copy-start(bf16[2048,256]{1,0:T(8,128)(2,1)} %refs_19_.1) | copy-start | bytes 3145732
  77.2 2.0 copy-start.43
  81.6 2.6 copy-start.1
  84.2 3.9 copy-start.11
  84.2 3.9 copy-start.20
  88.0 0.8 copy-start.27
  88.0 0.8 copy-start.29
  89.9 0.6 copy-start.47
  90.5 5.5 copy-start.22
  92.7 3.3 copy-start.13
  95.9 1.9 copy-start.24
  97.8 2.6 copy-start.7
  100.4 19.5 %copy-start.10 = (bf16[1,1,128,2048]{3,2,1,0:T(8,128)(2,1)S(1)}, bf16[1,1,128,2048]{3,2,1,0:T(8,128)(2,1)}, u32[]{:S(2)}) copy-start(bf16[1,1,128,2048]{3,2,1,0:T(8,128)(2,1)} %param.28) | copy-start | bytes 1572868
  119.9 2.5 copy-start.45
  120.0 2.7 copy-start.8
  121.5 1.0 copy-start.2
  121.5 1.0 copy-start.49
  122.6 1.1 copy-start.23
  123.8 251.3 %copy-start.3 = (f32[128,2048]{1,0:T(8,128)S(1)}, f32[128,2048]{1,0:T(8,128)}, u32[]{:S(2)}) copy-start(f32[128,2048]{1,0:T(8,128)} %copy-done.2) | copy-start | bytes 3145732
  123.8 251.3 %copy-start.46 = (f32[2048]{0:T(1024)S(1)}, f32[2048]{0:T(1024)}, u32[]{:S(2)}) copy-start(f32[2048]{0:T(1024)} %param.32) | copy-start | bytes 24580
  123.8 251.3 %copy-start.50 = (f32[128]{0:T(128)S(1)}, f32[128]{0:T(128)}, u32[]{:S(2)}) copy-start(f32[128]{0:T(128)} %copy-done.49) | copy-start | bytes 1540
  375.1 2.3 copy-start.9
  377.3 3.3 copy-start.48
  377.3 4.5 copy-start.28
  377.4 4.5 copy-start.30
  380.7 4.1 copy-start.15
  380.7 4.1 copy-start.17
  381.9 4.2 copy-start.51
  563.8 13.9 %copy-start.34 = (f32[288,512]{1,0:T(8,128)S(1)}, f32[288,512]{1,0:T(8,128)}, u32[]{:S(2)}) copy-start(f32[288,512]{1,0:T(8,128)} %get-tuple-element.77) | copy-start | bytes 1769476
  575.6 2.5 copy-start.40
  575.6 2.6 copy-start.18
  575.7 2.6 copy-start.31
  577.7 1.5 copy-start.21
  577.8 1.5 copy-start.44
  579.4 38.8 %copy-start.19 = (f32[4096,32]{1,0:T(8,128)S(1)}, f32[4096,32]{1,0:T(8,128)}, u32[]{:S(2)}) copy-start(f32[4096,32]{1,0:T(8,128)} %get-tuple-element.162) | copy-start | bytes 1572868
  618.2 2.5 copy-start.36
  618.2 3.3 copy-start.38
  619.6 5.4 copy-start.39
  620.7 5.2 copy-start.41
  620.7 5.2 copy-start.42

commit v5 on v4

--- a/solution.py
+++ b/solution.py
@@ -859,12 +859,23 @@
 
             lax.fori_loop(0, total // block, one, 0)
 
+        first_chunk = upto(0, started)
+        ready = [started]
+
+        def early(count):
+            last = min(ready[0] + count, first_chunk)
+            for f, _ in steps[ready[0] : last]:
+                f()
+            ready[0] = last
+
         for cp in w_copies[:3]:
             cp.wait()
         merge_rows(wd, da, de, units)
+        early(int(EARLY))
         for cp in w_copies[3:6]:
             cp.wait()
         merge_rows(wg, ga, ge, width)
+        early(int(EARLY))
         for cp in w_copies[6:]:
             cp.wait()
         merge_rows(wu, ua, ue, width)
@@ -915,8 +926,8 @@
             True: [("one", n_one, 1.9), ("pre", 1, 2.0 * scale), ("three", n_three, 0.7 * scale)],
         }
         slots = {(other, kind): [[] for _ in range(own * n)] for other in (False, True) for kind, n, _ in kinds[other]}
-        done = upto(0, started)
-        for f, _ in steps[started:done]:
+        done = first_chunk
+        for f, _ in steps[ready[0] : done]:
             f()
         clock = 0.0
         for c in range(len(chunks)):
@@ -1069,6 +1080,7 @@
 
 
 KV_STEPS = 3
+EARLY = 8
 NEAR_US = 45.0
 FAR_AT = 5.0
 FAR_US = 1.4
@@ -1094,7 +1106,7 @@
     kv_pad = -(-kv_r // 16) * 16
     kv_rows = kv_d + kv_pad + 16
 
-    gather_g = Gather(topo, "dp", grad_branch, [(0, rows, "xc")])
+    gather_g = Gather(topo, "dp", grad_branch, row_parts(rows, ("xc", "xc"), (1, 1)))
     gather_kv = Gather(topo, "dp", jax.ShapeDtypeStruct((rows, 2 * HD), BF16), [(0, rows, "xc")])
     swaps = [Exchange(topo, "quad", a, keep=False) for a in (dg, du, dd)]
     seq_parts = lambda n: row_parts(n, ("blh", "lbh"), (2, 1))
@@ -1104,7 +1116,7 @@
     sum_k = VScatter(topo, "seq", (n_seq, kv_rows, 2 * HD), BF16, seq_parts(kv_rows))
     kv_shape = (groups * n_seq, rows, 2 * HD)
     sum_kv = VScatter(topo, "all", kv_shape, BF16, row_parts(rows, ("cxblh", "cblxh"), (1, 1)))
-    sum_n = VScatter(topo, "dp", (groups, rows, width), BF16, [(0, rows, "cx")])
+    sum_n = VScatter(topo, "dp", (groups, rows, width), BF16, row_parts(rows, ("cx", "cx"), (1, 1)))
 
     inputs = [
         grad_branch, grad_middle, query_rot, heads_out, key_value, log_total, own_segs, key_segs,
@@ -1375,6 +1387,39 @@
     )(member, *owns, dg, du, dd, gate_expand, up_expand, down_adapt)
 
 
+def finish_small(topo, collective_id, small, n_moved, per_seq):
+    rows, rank = small.shape[1:]
+    n_seq = topo.n_seq
+    sums = VScatter(topo, "dp", small.shape, small.dtype, [(0, rows, "cx")])
+    moved = jax.ShapeDtypeStruct((n_moved, rank), F32)
+    spread = jax.ShapeDtypeStruct((n_seq, 2 * per_seq, rank), F32)
+    last = Finish(topo, moved, spread)
+    scratch = [pltpu.VMEM((rows, rank), F32), pltpu.VMEM(moved.shape, F32), pltpu.VMEM(spread.shape, F32)]
+
+    def kernel(x_ref, moved_out, spread_out, total, moved_in, spread_in, *refs):
+        at = greet(topo, [sums, last])
+        Steps(sums.steps(at, x_ref, total, refs[: len(sums.scratch)])).finish()
+        moved_in[...] = total[:n_moved, :]
+        for j in range(n_seq):
+            for k in range(2):
+                first = n_moved + (k * n_seq + j) * per_seq
+                spread_in[j, k * per_seq : (k + 1) * per_seq, :] = total[first : first + per_seq, :]
+        refs = refs[len(sums.scratch) :]
+        Steps(last.steps(at, [moved_in, spread_in], [moved_out, spread_out], refs)).finish()
+
+    return pl.pallas_call(
+        kernel,
+        name="finish_small",
+        out_shape=[moved, spread],
+        in_specs=[pl.BlockSpec(memory_space=pltpu.VMEM)],
+        out_specs=[pl.BlockSpec(memory_space=pl.ANY)] * 2,
+        scratch_shapes=scratch + sums.scratch + last.scratch,
+        compiler_params=pltpu.CompilerParams(
+            collective_id=collective_id, has_side_effects=True, vmem_limit_bytes=32 << 20
+        ),
+    )(small)
+
+
 def local(
     topo,
     tokens, segment_ids, out_grad, gain_attn, gain_mlp, w_query, w_key, w_value, w_out, w_gate, w_up, w_down,
@@ -1413,12 +1458,11 @@
     seg_rows = jnp.zeros((16, rows), F32).at[0].set(segment_ids[0, 0].astype(F32))
 
     zyx, xzy = "lhbxc", "xlhbc"
-    (normed_all,), (kv_all,), (seg_all,), (grad_half,) = communicate(
+    (normed_all,), (kv_all,), (seg_all,) = communicate(
         topo, "gather_attention", 0,
-        Gather(topo, "dp", normed_attn, [(0, rows, "xc")]),
+        Gather(topo, "dp", normed_attn, row_parts(rows, ("xc", "xc"), (1, 1))),
         Gather(topo, "all", key_value, row_parts(rows, (zyx, xzy), (7, 4))),
         Gather(topo, "all", seg_rows, [(0, 16, zyx)]),
-        Gather(topo, "half", grad_rows_in, row_parts(rows, ("xlbc", "lbxc", "bxlc"), (1, 1, 1))),
     )
     kv_all = kv_all.reshape(groups, length, 2 * HD)
     keys_all, values_all = kv_all[..., :HD], kv_all[..., HD:]
@@ -1438,8 +1482,10 @@
         contract("shtj,sjd->sthd", prob_low, values_all).reshape(groups * rows, head_cols).astype(BF16)
     )
     out_part = matmul(heads_out, wo).astype(BF16).reshape(groups, rows, width)
-    (out_sum,), = communicate(
-        topo, "sum_attention", 1, Scatter(topo, "dp", out_part, [(0, rows, "cx")])
+    (out_sum,), (grad_half,) = communicate(
+        topo, "sum_attention", 1,
+        Scatter(topo, "dp", out_part, row_parts(rows, ("cx", "cx"), (1, 1))),
+        Gather(topo, "half", grad_rows_in, row_parts(rows, ("xlbc", "lbxc", "bxlc"), (1, 1, 1))),
     )
     middle = token_rows + out_sum
     normed, unit_mlp, rms_mlp = normalize(middle, gain_mlp)
@@ -1493,19 +1539,12 @@
     )
     small = jnp.concatenate([adapt, small_gains, expand], axis=1).astype(BF16)
     n_adapt = 3 * per_dev_d
-    (small_sum,), = communicate(
-        topo, "sum_small", 8, Scatter(topo, "dp", small, [(0, small.shape[1], "cx")])
-    )
     per_seq = rank // groups // n_seq
-    across = small_sum[n_adapt + 16 :, :d_rows].reshape(2, n_seq, per_seq, d_rows).transpose(1, 0, 2, 3)
-    across = across.reshape(n_seq, 2 * per_seq, d_rows)
-    (own_adapt, own_expand), = communicate(
-        topo, "finish", 9, Finish(topo, small_sum[: n_adapt + 16], across)
-    )
+    own_adapt, own_expand = finish_small(topo, 8, small, n_adapt + 16, per_seq)
     grad_ga, grad_ua, grad_qa = own_adapt[:n_adapt].reshape(3, per_dev_d, rank)
     grad_gain_attn = own_adapt[n_adapt, :per_dev_d]
     grad_gain_mlp = own_adapt[n_adapt + 1, :per_dev_d]
-    own_expand = own_expand.reshape(n_seq, 2, per_seq, d_rows).transpose(1, 2, 0, 3).reshape(2, per_seq, width)
+    own_expand = own_expand[..., :d_rows].reshape(n_seq, 2, per_seq, d_rows).transpose(1, 2, 0, 3).reshape(2, per_seq, width)
     grad_de, grad_oe = own_expand[0], own_expand[1]
     grad_wk, grad_wv = grad_wkv[:, :HD], grad_wkv[:, HD:]
     grad_ka = dot_t(grad_wk.astype(BF16), key_expand)

time: 631 us -> 628 us (level)
    pallas_call x0 -> x1, Pallas kernels: none -> 27.5 us  [finish_small(): pl.pallas_call(kernel, name='finish_small', out_shape=[moved, spread], in...]
    pallas_call x4 -> x2, Pallas kernels: 115 us -> 88.4 us  [communicate(): pl.pallas_call(kernel, name=name, out_shape=[s for op in ops for s in op....]
where the time goes in v5:
time: 628 us; the launch traced here: 624 us
  Pallas kernels  556 us (89%)
  local copies, waits for them, and re-layouts  27.3 us (4%)
  other arithmetic  21.7 us (3%)
  matrix products  17.1 us (3%)
    pallas_call x1, Pallas kernels, feed_forward(): pl.pallas_call(kernel, name='feed_forward', out_shape=out_shape, in_specs...  252 us
    pallas_call x1, Pallas kernels, attention_back(): pl.pallas_call(kernel, name='attention_back', out_shape=out_shape, in_spe...  177 us
    pallas_call x2, Pallas kernels, communicate(): pl.pallas_call(kernel, name=name, out_shape=[s for op in ops for s in op....  88.4 us
    pallas_call x1, Pallas kernels, finish_small(): pl.pallas_call(kernel, name='finish_small', out_shape=[moved, spread], in...  27.5 us

profile of v5, /device:TPU:0, one launch (start us, length us, event | category | flops | bytes accessed | tf_op | source)
XLA Modules:
  0.0 624.3 jit_solution(10443504445337140509)
XLA Ops:
  0.7 1.4 fusion.15
  2.1 0.5 fusion.27
  2.6 2.2 convert_multiply_fusion
  4.9 0.4 fusion.1.refs_17_
  5.4 0.3 fusion.33
  5.7 0.3 multiply_cosine_fusion
  6.1 0.3 copy-done.5
  6.4 0.7 copy-done.26
  7.1 0.4 fusion.2.refs_18_
  7.5 1.0 copy-done.4
  8.5 0.3 convolution_convert_fusion.3
  8.8 0.7 pad_maximum_fusion.2.refs_1_
  9.5 0.6 scatter.4.refs_2_
  10.1 41.5 %gather_attention.1 = (bf16[4,128,2048]{2,1,0:T(8,128)(2,1)}, bf16[32,128,512]{2,1,0:T(8,128)(2,1)}, f32[32,16,128]{2,1,0:T(8,128)}) custom-call(bf16[128,2048]{1,0:T(8,128)(2,1)} %copy-done.6, bf16[128,512]{1,0:T(8,128)(2,1)} %pad_maximum_fusion.2.refs_1_, f32[16,128]{1,0:T(8,128)} %scatter.4.refs_2_), custom_call_target="tpu_custom_call" | custom-call | tf_op jit(solution)/shard_map/gather_attention/pallas_call | solution.py:627
  51.7 0.9 slice_reduce_fusion
  52.7 1.9 compare_and_fusion
  54.6 2.3 add_convert_fusion.1.refs_16_
  57.0 2.6 copy.109
  59.6 3.7 fusion.5
  63.5 0.8 fusion
  64.3 1.0 exponential_reduce_fusion
  65.3 0.6 copy-done.47
  65.8 2.3 fusion.14
  68.1 2.1 copy.89
  70.2 1.1 copy.110
  71.4 1.8 add_convert_fusion.refs_15_
  73.2 2.6 convolution_convert_fusion
  75.8 46.9 %sum_attention.1 = (f32[128,2048]{1,0:T(8,128)}, bf16[16,128,2048]{2,1,0:T(8,128)(2,1)}) custom-call(bf16[4,128,2048]{2,1,0:T(8,128)(2,1)} %bitcast.138, bf16[128,2048]{1,0:T(8,128)(2,1)} %bitcast.133), custom_call_target="tpu_custom_call" | custom-call | tf_op jit(solution)/shard_map/sum_attention/pallas_call | solution.py:627
  122.8 1.5 multiply_reduce_fusion.2
  124.3 1.0 copy-done.2
  125.4 1.1 pad_maximum_fusion.refs_1_
  126.6 251.7 %feed_forward.1 = (bf16[16,256,2048]{2,1,0:T(8,128)(2,1)}, bf16[4,288,1024]{2,1,0:T(8,128)(2,1)}, bf16[4,288,1024]{2,1,0:T(8,128)(2,1)}, bf16[4,288,1024]{2,1,0:...) custom-call(bf16[128,2048]{1,0:T(8,128)(2,1)} %copy-done.23, ...), custom_call_target="tpu_custom_call" | custom-call | flops 154618822656 | bytes 134217728 | tf_op jit(solution)/shard_map/feed_forward/pallas_call | solution.py:1065
  378.3 2.2 multiply_reduce_fusion
  380.6 3.3 fusion.28
  383.9 1.1 add.111.refs_5_
  385.1 0.5 copy.90
  385.6 0.9 copy.111
  386.5 0.7 fusion.53
  387.2 0.7 copy.92.refs_6_
  388.0 1.3 constant_dynamic-slice_fusion
  389.3 0.7 copy.93.refs_10_
  390.0 177.0 %attention_back.1 = (bf16[128,2048]{1,0:T(8,128)(2,1)}, f32[288,512]{1,0:T(8,128)}, f32[288,512]{1,0:T(8,128)}, f32[96,512]{1,0:T(8,128)}, bf16[4,288,1024]{2,1,...) custom-call(bf16[128,2048]{1,0:T(8,128)(2,1)} %get-tuple-element.168.refs_0_, ...), custom_call_target="tpu_custom_call" | custom-call | tf_op jit(solution)/shard_map/attention_back/pallas_call | solution.py:1325
  567.0 11.8 %unfold.1 = (f32[256,4096]{1,0:T(8,128)}, f32[32,4096]{1,0:T(8,128)}, f32[256,4096]{1,0:T(8,128)}, f32[32,4096]{1,0:T(8,128)}, f32[4096,256]{1,0:T(8,128)}, /*in...) custom-call(s32[1]{0:T(128)} %bitcast.23.me, ...), custom_call_target="tpu_custom_call" | custom-call | tf_op jit(solution)/shard_map/unfold/pallas_call | solution.py:1372
  578.9 1.1 convert.47
  580.0 1.0 convert.48
  581.3 0.8 pad_maximum_fusion.1
  582.1 0.8 copy.98
  582.8 0.3 convolution_convert_fusion.1
  583.1 1.1 maximum_bitcast_fusion
  584.2 0.7 copy.99
  584.9 0.7 slice.158
  585.7 1.1 fusion.17.x_ref
  586.9 27.5 %finish_small.1 = (f32[208,256]{1,0:T(8,128)S(1)}, f32[8,16,256]{2,1,0:T(8,128)S(1)}) custom-call(bf16[4,336,256]{2,1,0:T(8,128)(2,1)S(1)} %fusion.17.x_ref), custom_call_target="tpu_custom_call" | custom-call | tf_op jit(solution)/shard_map/finish_small/pallas_call | solution.py:1410
  614.3 0.7 fusion.29
  615.0 0.7 fusion.32
  615.7 0.5 slice_bitcast_fusion.10
  616.2 1.4 copy.101
  617.6 1.0 copy.100
  618.7 0.8 fusion.20
  619.5 0.8 fusion.22
  620.3 1.5 slice.113
  621.8 0.6 slice_bitcast_fusion.9
  622.4 0.6 fusion.30
  623.0 0.8 copy.115
  (121 shorter events, 1.2 us)
Async XLA Ops:
  0.7 54.0 %copy-start = (bf16[256,512]{1,0:T(8,128)(2,1)S(1)}, bf16[256,512]{1,0:T(8,128)(2,1)}, u32[]{:S(2)}) copy-start(bf16[256,512]{1,0:T(8,128)(2,1)} %param.41) | copy-start | bytes 786436
  0.7 4.2 copy-start.25
  0.7 4.2 copy-start.16
  0.7 4.2 copy-start.37
  4.9 2.6 copy-start.6
  4.9 1.5 copy-start.14
  4.9 2.1 copy-start.26
  4.9 2.1 copy-start.35
  5.4 1.0 copy-start.5
  6.1 57.2 %copy-start.32 = (f32[128,128]{1,0:T(8,128)}, f32[128,128]{1,0:T(8,128)S(1)}, u32[]{:S(2)}) copy-start(f32[128,128]{1,0:T(8,128)S(1)} %get-tuple-element.190.refs_13_) | copy-start | bytes 196612
  6.1 57.2 %copy-start.33 = (f32[128,128]{1,0:T(8,128)}, f32[128,128]{1,0:T(8,128)S(1)}, u32[]{:S(2)}) copy-start(f32[128,128]{1,0:T(8,128)S(1)} %get-tuple-element.191.refs_14_) | copy-start | bytes 196612
  7.1 2.4 copy-start.52
  7.5 1.0 copy-start.4
  8.5 46.1 %copy-start.12 = (bf16[2048,256]{1,0:T(8,128)(2,1)S(1)}, bf16[2048,256]{1,0:T(8,128)(2,1)}, u32[]{:S(2)}) copy-start(bf16[2048,256]{1,0:T(8,128)(2,1)} %refs_19_.1) | copy-start | bytes 3145732
  52.6 2.0 copy-start.43
  56.9 2.6 copy-start.1
  59.6 3.9 copy-start.11
  59.6 3.9 copy-start.20
  63.4 0.8 copy-start.27
  63.4 0.8 copy-start.29
  65.2 0.6 copy-start.47
  65.8 5.5 copy-start.22
  68.1 3.3 copy-start.13
  71.3 1.9 copy-start.24
  73.2 2.6 copy-start.7
  75.8 46.9 %copy-start.10 = (bf16[1,1,128,2048]{3,2,1,0:T(8,128)(2,1)S(1)}, bf16[1,1,128,2048]{3,2,1,0:T(8,128)(2,1)}, u32[]{:S(2)}) copy-start(bf16[1,1,128,2048]{3,2,1,0:T(8,128)(2,1)} %param.28) | copy-start | bytes 1572868
  75.8 49.4 %copy-start.45 = (f32[2048]{0:T(1024)S(1)}, f32[2048]{0:T(1024)}, u32[]{:S(2)}) copy-start(f32[2048]{0:T(1024)} %param.32) | copy-start | bytes 24580
  122.7 2.7 copy-start.8
  124.3 1.0 copy-start.2
  124.3 1.0 copy-start.49
  125.4 1.1 copy-start.23
  126.6 251.7 %copy-start.3 = (f32[128,2048]{1,0:T(8,128)S(1)}, f32[128,2048]{1,0:T(8,128)}, u32[]{:S(2)}) copy-start(f32[128,2048]{1,0:T(8,128)} %copy-done.2) | copy-start | bytes 3145732
  126.6 251.7 %copy-start.46 = (f32[2048]{0:T(1024)S(1)}, f32[2048]{0:T(1024)}, u32[]{:S(2)}) copy-start(f32[2048]{0:T(1024)} %param.32) | copy-start | bytes 24580
  126.6 251.7 %copy-start.50 = (f32[128]{0:T(128)S(1)}, f32[128]{0:T(128)}, u32[]{:S(2)}) copy-start(f32[128]{0:T(128)} %copy-done.49) | copy-start | bytes 1540
  378.3 2.3 copy-start.9
  380.5 3.3 copy-start.48
  380.5 4.5 copy-start.28
  380.5 4.5 copy-start.30
  383.9 4.1 copy-start.15
  383.9 4.1 copy-start.17
  385.1 4.2 copy-start.51
  567.0 13.9 %copy-start.34 = (f32[288,512]{1,0:T(8,128)S(1)}, f32[288,512]{1,0:T(8,128)}, u32[]{:S(2)}) copy-start(f32[288,512]{1,0:T(8,128)} %get-tuple-element.79) | copy-start | bytes 1769476
  578.9 3.2 copy-start.40
  578.9 4.0 copy-start.18
  578.9 3.9 copy-start.31
  581.0 4.0 copy-start.21
  583.1 33.1 %copy-start.19 = (f32[4096,32]{1,0:T(8,128)S(1)}, f32[4096,32]{1,0:T(8,128)}, u32[]{:S(2)}) copy-start(f32[4096,32]{1,0:T(8,128)} %get-tuple-element.164) | copy-start | bytes 1572868
  616.2 2.4 copy-start.44
  616.2 2.5 copy-start.36
  616.2 3.3 copy-start.38
  617.6 5.4 copy-start.39
  618.6 5.2 copy-start.41
  618.7 5.2 copy-start.42

commit v6 on v5

--- a/solution.py
+++ b/solution.py
@@ -752,7 +752,7 @@
     far = row_parts(2 * rows, ("hxlbc", "hlbxc", "hbxlc"), (1, 1, 1))
     gather_n = Gather(topo, "half", normed, near, need=need, keep=False)
     gather_far = Gather(topo, "all", both, far, beyond="h", need=need)
-    thirds = row_parts(2 * rows, ("cxlb", "cbxl", "clbx"), (1, 1, 1))
+    thirds = row_parts(2 * rows, ("cxbl", "cblx", "clxb"), (1, 1, 1))
     sum_both = SlimScatter(topo, "half", (half, 2 * rows, width), BF16, thirds)
     comm = [gather_n, gather_far, sum_both]
 
@@ -1083,8 +1083,8 @@
 EARLY = 8
 NEAR_US = 45.0
 FAR_AT = 5.0
-FAR_US = 1.4
-SUM_US = 2.4
+FAR_US = 1.5
+SUM_US = 2.0
 
 
 def attention_back(

time: 628 us -> 621 us (0.989)
  Pallas kernels: 556 us -> 549 us
    pallas_call x1, Pallas kernels: 252 us -> 245 us  [feed_forward(): pl.pallas_call(kernel, name='feed_forward', out_shape=out_shape, in_specs...]
where the time goes in v6:
time: 621 us; the launch traced here: 617 us
  Pallas kernels  549 us (88%)
  local copies, waits for them, and re-layouts  27.3 us (4%)
  other arithmetic  21.7 us (3%)
  matrix products  17.1 us (3%)
    pallas_call x1, Pallas kernels, feed_forward(): pl.pallas_call(kernel, name='feed_forward', out_shape=out_shape, in_specs...  245 us
    pallas_call x1, Pallas kernels, attention_back(): pl.pallas_call(kernel, name='attention_back', out_shape=out_shape, in_spe...  178 us
    pallas_call x2, Pallas kernels, communicate(): pl.pallas_call(kernel, name=name, out_shape=[s for op in ops for s in op....  88.4 us
    pallas_call x1, Pallas kernels, finish_small(): pl.pallas_call(kernel, name='finish_small', out_shape=[moved, spread], in...  26.5 us

profile of v6, /device:TPU:0, one launch (start us, length us, event | category | flops | bytes accessed | tf_op | source)
XLA Modules:
  0.0 617.3 jit_solution(2399276953678150302)
XLA Ops:
  0.7 1.4 fusion.15
  2.1 0.5 fusion.27
  2.6 2.2 convert_multiply_fusion
  4.9 0.4 fusion.1.refs_17_
  5.4 0.3 fusion.33
  5.7 0.3 multiply_cosine_fusion
  6.1 0.3 copy-done.5
  6.4 0.7 copy-done.26
  7.1 0.4 fusion.2.refs_18_
  7.5 1.0 copy-done.4
  8.5 0.3 convolution_convert_fusion.3
  8.8 0.7 pad_maximum_fusion.2.refs_1_
  9.5 0.6 scatter.4.refs_2_
  10.1 41.5 %gather_attention.1 = (bf16[4,128,2048]{2,1,0:T(8,128)(2,1)}, bf16[32,128,512]{2,1,0:T(8,128)(2,1)}, f32[32,16,128]{2,1,0:T(8,128)}) custom-call(bf16[128,2048]{1,0:T(8,128)(2,1)} %copy-done.6, bf16[128,512]{1,0:T(8,128)(2,1)} %pad_maximum_fusion.2.refs_1_, f32[16,128]{1,0:T(8,128)} %scatter.4.refs_2_), custom_call_target="tpu_custom_call" | custom-call | tf_op jit(solution)/shard_map/gather_attention/pallas_call | solution.py:627
  51.7 0.9 slice_reduce_fusion
  52.7 1.9 compare_and_fusion
  54.6 2.3 add_convert_fusion.1.refs_16_
  57.0 2.6 copy.109
  59.6 3.7 fusion.5
  63.5 0.8 fusion
  64.3 1.0 exponential_reduce_fusion
  65.3 0.6 copy-done.47
  65.8 2.3 fusion.14
  68.1 2.1 copy.89
  70.2 1.1 copy.110
  71.4 1.8 add_convert_fusion.refs_15_
  73.2 2.6 convolution_convert_fusion
  75.8 46.9 %sum_attention.1 = (f32[128,2048]{1,0:T(8,128)}, bf16[16,128,2048]{2,1,0:T(8,128)(2,1)}) custom-call(bf16[4,128,2048]{2,1,0:T(8,128)(2,1)} %bitcast.138, bf16[128,2048]{1,0:T(8,128)(2,1)} %bitcast.133), custom_call_target="tpu_custom_call" | custom-call | tf_op jit(solution)/shard_map/sum_attention/pallas_call | solution.py:627
  122.8 1.5 multiply_reduce_fusion.2
  124.3 1.0 copy-done.2
  125.4 1.1 pad_maximum_fusion.refs_1_
  126.6 244.8 %feed_forward.1 = (bf16[16,256,2048]{2,1,0:T(8,128)(2,1)}, bf16[4,288,1024]{2,1,0:T(8,128)(2,1)}, bf16[4,288,1024]{2,1,0:T(8,128)(2,1)}, bf16[4,288,1024]{2,1,0:...) custom-call(bf16[128,2048]{1,0:T(8,128)(2,1)} %copy-done.23, ...), custom_call_target="tpu_custom_call" | custom-call | flops 154618822656 | bytes 134217728 | tf_op jit(solution)/shard_map/feed_forward/pallas_call | solution.py:1065
  371.4 2.2 multiply_reduce_fusion
  373.6 3.3 fusion.28
  376.9 1.1 add.111.refs_5_
  378.2 0.5 copy.90
  378.7 0.9 copy.111
  379.6 0.7 fusion.53
  380.3 0.7 copy.92.refs_6_
  381.0 1.3 constant_dynamic-slice_fusion
  382.4 0.7 copy.93.refs_10_
  383.1 177.9 %attention_back.1 = (bf16[128,2048]{1,0:T(8,128)(2,1)}, f32[288,512]{1,0:T(8,128)}, f32[288,512]{1,0:T(8,128)}, f32[96,512]{1,0:T(8,128)}, bf16[4,288,1024]{2,1,...) custom-call(bf16[128,2048]{1,0:T(8,128)(2,1)} %get-tuple-element.168.refs_0_, ...), custom_call_target="tpu_custom_call" | custom-call | tf_op jit(solution)/shard_map/attention_back/pallas_call | solution.py:1325
  561.0 11.8 %unfold.1 = (f32[256,4096]{1,0:T(8,128)}, f32[32,4096]{1,0:T(8,128)}, f32[256,4096]{1,0:T(8,128)}, f32[32,4096]{1,0:T(8,128)}, f32[4096,256]{1,0:T(8,128)}, /*in...) custom-call(s32[1]{0:T(128)} %bitcast.23.me, ...), custom_call_target="tpu_custom_call" | custom-call | tf_op jit(solution)/shard_map/unfold/pallas_call | solution.py:1372
  572.9 1.1 convert.47
  573.9 1.0 convert.48
  575.2 0.8 pad_maximum_fusion.1
  576.0 0.8 copy.98
  576.8 0.3 convolution_convert_fusion.1
  577.1 1.1 maximum_bitcast_fusion
  578.2 0.7 copy.99
  578.9 0.7 slice.158
  579.7 1.1 fusion.17.x_ref
  580.8 26.5 %finish_small.1 = (f32[208,256]{1,0:T(8,128)S(1)}, f32[8,16,256]{2,1,0:T(8,128)S(1)}) custom-call(bf16[4,336,256]{2,1,0:T(8,128)(2,1)S(1)} %fusion.17.x_ref), custom_call_target="tpu_custom_call" | custom-call | tf_op jit(solution)/shard_map/finish_small/pallas_call | solution.py:1410
  607.3 0.7 fusion.29
  608.0 0.7 fusion.32
  608.7 0.5 slice_bitcast_fusion.10
  609.2 1.4 copy.101
  610.6 1.0 copy.100
  611.7 0.8 fusion.20
  612.5 0.8 fusion.22
  613.3 1.5 slice.113
  614.8 0.6 slice_bitcast_fusion.9
  615.4 0.6 fusion.30
  616.0 0.8 copy.115
  (121 shorter events, 1.2 us)
Async XLA Ops:
  0.7 54.0 %copy-start = (bf16[256,512]{1,0:T(8,128)(2,1)S(1)}, bf16[256,512]{1,0:T(8,128)(2,1)}, u32[]{:S(2)}) copy-start(bf16[256,512]{1,0:T(8,128)(2,1)} %param.41) | copy-start | bytes 786436
  0.7 4.2 copy-start.25
  0.7 4.2 copy-start.16
  0.7 4.2 copy-start.37
  4.9 2.6 copy-start.6
  4.9 1.5 copy-start.14
  4.9 2.1 copy-start.26
  4.9 2.1 copy-start.35
  5.4 1.0 copy-start.5
  6.1 57.2 %copy-start.32 = (f32[128,128]{1,0:T(8,128)}, f32[128,128]{1,0:T(8,128)S(1)}, u32[]{:S(2)}) copy-start(f32[128,128]{1,0:T(8,128)S(1)} %get-tuple-element.190.refs_13_) | copy-start | bytes 196612
  6.1 57.2 %copy-start.33 = (f32[128,128]{1,0:T(8,128)}, f32[128,128]{1,0:T(8,128)S(1)}, u32[]{:S(2)}) copy-start(f32[128,128]{1,0:T(8,128)S(1)} %get-tuple-element.191.refs_14_) | copy-start | bytes 196612
  7.1 2.4 copy-start.52
  7.5 1.0 copy-start.4
  8.5 46.1 %copy-start.12 = (bf16[2048,256]{1,0:T(8,128)(2,1)S(1)}, bf16[2048,256]{1,0:T(8,128)(2,1)}, u32[]{:S(2)}) copy-start(bf16[2048,256]{1,0:T(8,128)(2,1)} %refs_19_.1) | copy-start | bytes 3145732
  52.6 2.0 copy-start.43
  56.9 2.6 copy-start.1
  59.6 3.9 copy-start.11
  59.6 3.9 copy-start.20
  63.4 0.8 copy-start.27
  63.4 0.8 copy-start.29
  65.2 0.6 copy-start.47
  65.8 5.5 copy-start.22
  68.1 3.3 copy-start.13
  71.3 1.9 copy-start.24
  73.2 2.6 copy-start.7
  75.8 46.9 %copy-start.10 = (bf16[1,1,128,2048]{3,2,1,0:T(8,128)(2,1)S(1)}, bf16[1,1,128,2048]{3,2,1,0:T(8,128)(2,1)}, u32[]{:S(2)}) copy-start(bf16[1,1,128,2048]{3,2,1,0:T(8,128)(2,1)} %param.28) | copy-start | bytes 1572868
  75.8 49.4 %copy-start.45 = (f32[2048]{0:T(1024)S(1)}, f32[2048]{0:T(1024)}, u32[]{:S(2)}) copy-start(f32[2048]{0:T(1024)} %param.32) | copy-start | bytes 24580
  122.7 2.7 copy-start.8
  124.3 1.0 copy-start.2
  124.3 1.0 copy-start.49
  125.4 1.1 copy-start.23
  126.6 244.8 %copy-start.3 = (f32[128,2048]{1,0:T(8,128)S(1)}, f32[128,2048]{1,0:T(8,128)}, u32[]{:S(2)}) copy-start(f32[128,2048]{1,0:T(8,128)} %copy-done.2) | copy-start | bytes 3145732
  126.6 244.8 %copy-start.46 = (f32[2048]{0:T(1024)S(1)}, f32[2048]{0:T(1024)}, u32[]{:S(2)}) copy-start(f32[2048]{0:T(1024)} %param.32) | copy-start | bytes 24580
  126.6 244.8 %copy-start.50 = (f32[128]{0:T(128)S(1)}, f32[128]{0:T(128)}, u32[]{:S(2)}) copy-start(f32[128]{0:T(128)} %copy-done.49) | copy-start | bytes 1540
  371.3 2.3 copy-start.9
  373.6 3.3 copy-start.48
  373.6 4.5 copy-start.28
  373.6 4.5 copy-start.30
  376.9 4.1 copy-start.15
  376.9 4.1 copy-start.17
  378.2 4.2 copy-start.51
  561.0 13.9 %copy-start.34 = (f32[288,512]{1,0:T(8,128)S(1)}, f32[288,512]{1,0:T(8,128)}, u32[]{:S(2)}) copy-start(f32[288,512]{1,0:T(8,128)} %get-tuple-element.79) | copy-start | bytes 1769476
  572.8 3.2 copy-start.40
  572.8 4.0 copy-start.18
  572.9 4.0 copy-start.31
  574.9 4.0 copy-start.21
  577.1 32.1 %copy-start.19 = (f32[4096,32]{1,0:T(8,128)S(1)}, f32[4096,32]{1,0:T(8,128)}, u32[]{:S(2)}) copy-start(f32[4096,32]{1,0:T(8,128)} %get-tuple-element.164) | copy-start | bytes 1572868
  609.2 2.4 copy-start.44
  609.2 2.5 copy-start.36
  609.2 3.3 copy-start.38
  610.6 5.4 copy-start.39
  611.6 5.2 copy-start.41
  611.6 5.2 copy-start.42
